TPU v7x, 128 devices: a whole 4x4x4 slice. The times are simulated.
128 devices in a mesh: depth: 32 (over x, z, core), stripe: 4 (over y).
Axes of the slice: x: 4, y: 4, z: 4, core: 2. Of those that a mesh axis runs over, the one named last changes fastest.
Arguments:
- object_slices: float32 [32, 2, 1024, 384], P('depth', None, 'stripe'), may hold values from -1 to 1, as said below
- probe_wave: bfloat16 [2, 256, 256], replicated, may hold values from -5 to 5
- amplitudes: bfloat16 [16, 256, 256], P('stripe'), may hold values from 0 to 2
- positions: int32 [16, 2], replicated, may hold values from 0 to 255, as said below
- counts: int32 [4], replicated, may hold values from 1 to 4, as said below
Outputs:
- grad_object: float32 [32, 2, 1024, 384], P('depth', None, 'stripe')
Inputs may be any that keep to these rules, and one draw needn't show every extreme that they name: `object_slices`: every cell has magnitude at most 1. `positions`: row offsets lie in 0 to 255 and column offsets in 0 to 128. The counts sum to 8 and the largest equals 4; a stripe's live slots are its first ones.
All inputs are finite; a program needn't handle non-finite values.
Results may differ from a plain program's by a relative error of at most 0.0003.
Values may be sent and summed in bfloat16 or wider, within the bound.
No kernel may reach another device: no remote copies, remote signals or barrier semaphores. Data moves between devices by JAX's collectives and lax.ppermute only.
A program may use at most 64 MiB of HBM per device.

v0:
```python
import math

import jax
import jax.numpy as jnp
from jax import lax
from jax.sharding import PartitionSpec as P

smoothing = 0.25
highest = lax.Precision.HIGHEST


def passed_along(block, axis, distance):
    devices = range(lax.axis_size(axis))
    route = [(i - distance, i) for i in devices if i - distance in devices]
    return lax.ppermute(block, axis, route)


def shifted(value, axis, steps):
    count = lax.axis_size(axis)
    pairs = [(source, (source + steps) % count) for source in range(count)]
    return lax.ppermute(value, axis, pairs)


def make_tables(length):
    index_row = jnp.arange(length, dtype=jnp.int32)
    product = index_row[:, None] * index_row[None, :] % length
    angle = 2.0 * math.pi * product.astype(jnp.float32) / length
    scale = 1.0 / math.sqrt(length)
    cos_part = jnp.cos(angle) * scale
    sin_part = -jnp.sin(angle) * scale
    neg_part = jnp.sin(angle) * scale
    right_fwd = jnp.concatenate([cos_part, sin_part], axis=1)
    left_fwd = jnp.concatenate([cos_part, sin_part], axis=0)
    right_inv = jnp.concatenate([cos_part, neg_part], axis=1)
    left_inv = jnp.concatenate([cos_part, neg_part], axis=0)
    freq = ((index_row + length // 2) % length - length // 2).astype(jnp.float32)
    phase = (
        -math.pi * (freq[:, None] * freq[:, None] + freq[None, :] * freq[None, :]) / (2.0 * length)
    )
    return (right_fwd, left_fwd, right_inv, left_inv, jnp.cos(phase), jnp.sin(phase))


def transform(real_in, imag_in, right_tab, left_tab):
    length = real_in.shape[0]
    stacked = jnp.concatenate([real_in, imag_in], axis=0)
    first_pass = jnp.dot(stacked, right_tab, precision=highest, preferred_element_type=jnp.float32)
    mid_real = first_pass[:length, :length] - first_pass[length:, length:]
    mid_imag = first_pass[:length, length:] + first_pass[length:, :length]
    second = jnp.dot(
        left_tab,
        jnp.concatenate([mid_real, mid_imag], axis=1),
        precision=highest,
        preferred_element_type=jnp.float32,
    )
    out_real = second[:length, :length] - second[length:, length:]
    out_imag = second[:length, length:] + second[length:, :length]
    return (out_real, out_imag)


def transmit(wave_in, window):
    real_t = wave_in[0] * window[0] - wave_in[1] * window[1]
    imag_t = wave_in[0] * window[1] + wave_in[1] * window[0]
    return (real_t, imag_t)


def advance(wave_in, window, tables):
    right_fwd, left_fwd, right_inv, left_inv, prop_cos, prop_sin = tables
    real_t, imag_t = transmit(wave_in, window)
    spec_real, spec_imag = transform(real_t, imag_t, right_fwd, left_fwd)
    prop_real = spec_real * prop_cos - spec_imag * prop_sin
    prop_imag = spec_real * prop_sin + spec_imag * prop_cos
    out_real, out_imag = transform(prop_real, prop_imag, right_inv, left_inv)
    return jnp.stack([out_real, out_imag])


def exit_adjoint(wave_in, window, amplitude, tables):
    right_fwd, left_fwd = (tables[0], tables[1])
    real_t, imag_t = transmit(wave_in, window)
    far_real, far_imag = transform(real_t, imag_t, right_fwd, left_fwd)
    smooth = jnp.sqrt(far_real * far_real + far_imag * far_imag + smoothing)
    factor = 1.0 - amplitude.astype(jnp.float32) / smooth
    return jnp.stack([factor * far_real, factor * far_imag])


def unfold(adjoint, tables):
    out_real, out_imag = transform(adjoint[0], adjoint[1], tables[2], tables[3])
    return jnp.stack([out_real, out_imag])


def retreat(adjoint, tables):
    right_fwd, left_fwd, right_inv, left_inv, prop_cos, prop_sin = tables
    spec_real, spec_imag = transform(adjoint[0], adjoint[1], right_fwd, left_fwd)
    back_real = spec_real * prop_cos + spec_imag * prop_sin
    back_imag = spec_imag * prop_cos - spec_real * prop_sin
    out_real, out_imag = transform(back_real, back_imag, right_inv, left_inv)
    return jnp.stack([out_real, out_imag])


def slice_grad(wave_in, middle):
    return jnp.stack(
        [
            wave_in[0] * middle[0] + wave_in[1] * middle[1],
            wave_in[0] * middle[1] - wave_in[1] * middle[0],
        ]
    )


def back_wave(window, middle):
    return jnp.stack(
        [
            window[0] * middle[0] + window[1] * middle[1],
            window[0] * middle[1] - window[1] * middle[0],
        ]
    )


def depth_chain(
    object_slab, probe_float, patterns, pattern_index, row_start, col_start, live_mask, tables
):
    depth_count = lax.axis_size("depth")
    depth_index = lax.axis_index("depth")
    slot_count = row_start.shape[0]
    layers = object_slab.shape[0]
    window_size = probe_float.shape[1]
    is_last = depth_index == depth_count - 1
    is_first = depth_index == 0
    step_count = slot_count + depth_count - 1
    empty_wave = jnp.zeros((2, window_size, window_size), jnp.float32)
    stored_start = jnp.zeros((slot_count, layers, 2, window_size, window_size), jnp.float32)
    starts_start = jnp.zeros((slot_count, 2, window_size, window_size), jnp.float32)
    zero_index = jnp.zeros((), jnp.int32)

    def corner_of(layer_id, slot_id):
        return (jnp.int32(layer_id), zero_index, row_start[slot_id], col_start[slot_id])

    def window_at(layer_id, slot_id):
        return lax.dynamic_slice(
            object_slab, corner_of(layer_id, slot_id), (1, 2, window_size, window_size)
        )[0]

    def forward_step(carry, step_id):
        outgoing, stored, starts = carry
        received = passed_along(outgoing, "depth", 1)
        slot_raw = step_id - depth_index
        inside = (slot_raw >= 0) & (slot_raw < slot_count)
        slot_id = jnp.clip(slot_raw, 0, slot_count - 1)
        active = inside & live_mask[slot_id]

        def forward_compute_step(buffers):
            stored, starts = buffers
            wave_in = jnp.where(is_first, probe_float, received)
            stored = lax.dynamic_update_slice(
                stored,
                wave_in[None, None],
                (slot_id, jnp.int32(0), zero_index, zero_index, zero_index),
            )
            window = window_at(0, slot_id)
            pattern = lax.dynamic_index_in_dim(patterns, pattern_index[slot_id], 0, keepdims=False)
            wave_in = lax.cond(
                is_last,
                lambda: exit_adjoint(wave_in, window, pattern, tables),
                lambda: advance(wave_in, window, tables),
            )
            starts = lax.dynamic_update_slice(
                starts, wave_in[None], (slot_id, zero_index, zero_index, zero_index)
            )
            return (wave_in, stored, starts)

        def forward_skip_step(buffers):
            return (empty_wave, buffers[0], buffers[1])

        outgoing, stored, starts = lax.cond(
            active, forward_compute_step, forward_skip_step, (stored, starts)
        )
        return ((outgoing, stored, starts), None)

    (_, stored, starts), _ = lax.scan(
        forward_step,
        (empty_wave, stored_start, starts_start),
        jnp.arange(step_count, dtype=jnp.int32),
    )

    def backward_step(carry, step_id):
        outgoing, gradient = carry
        received = passed_along(outgoing, "depth", -1)
        slot_raw = step_id - (depth_count - 1 - depth_index)
        inside = (slot_raw >= 0) & (slot_raw < slot_count)
        slot_id = jnp.clip(slot_raw, 0, slot_count - 1)
        active = inside & live_mask[slot_id]

        def backward_compute_step(gradient):
            adjoint = jnp.where(is_last, starts[slot_id], received)
            for layer_id in reversed(range(layers)):
                window = window_at(layer_id, slot_id)
                wave_in = stored[slot_id, layer_id]
                middle = lax.cond(
                    is_last, lambda: unfold(adjoint, tables), lambda: retreat(adjoint, tables)
                )
                corner = corner_of(layer_id, slot_id)
                region = lax.dynamic_slice(gradient, corner, (1, 2, window_size, window_size))
                gradient = lax.dynamic_update_slice(
                    gradient, region + slice_grad(wave_in, middle)[None], corner
                )
                adjoint = back_wave(window, middle)
            return (adjoint, gradient)

        def backward_skip_step(gradient):
            return (empty_wave, gradient)

        outgoing, gradient = lax.cond(active, backward_compute_step, backward_skip_step, gradient)
        return ((outgoing, gradient), None)

    grad_start = jnp.zeros(object_slab.shape, jnp.float32)
    (_, gradient), _ = lax.scan(
        backward_step, (empty_wave, grad_start), jnp.arange(step_count, dtype=jnp.int32)
    )
    return gradient


def body(object_slices, probe_wave, amplitudes, positions, counts):
    stripe_index = lax.axis_index("stripe")
    stripe_rows = object_slices.shape[2]
    window_size = probe_wave.shape[1]
    capacity = amplitudes.shape[0]
    tables = make_tables(window_size)
    probe_float = probe_wave.astype(jnp.float32)
    next_rows = shifted(object_slices, "stripe", -1)
    object_slab = jnp.concatenate([object_slices, next_rows], axis=2)
    local_rows = lax.dynamic_slice_in_dim(positions, stripe_index * capacity, capacity, 0)
    row_start = local_rows[:, 0]
    col_start = local_rows[:, 1]
    slot_range = jnp.arange(capacity, dtype=jnp.int32)
    live_mask = slot_range < counts[stripe_index]
    gradient = depth_chain(
        object_slab, probe_float, amplitudes, slot_range, row_start, col_start, live_mask, tables
    )
    carried_back = shifted(gradient[:, :, stripe_rows:], "stripe", 1)
    head_rows = gradient[:, :, :window_size] + carried_back
    return jnp.concatenate([head_rows, gradient[:, :, window_size:stripe_rows]], axis=2)


def solution(mesh):
    return jax.shard_map(
        body,
        mesh=mesh,
        in_specs=(P("depth", None, "stripe", None), P(), P("stripe", None, None), P(), P()),
        out_specs=P("depth", None, "stripe", None),
        check_vma=False,
    )
```

profile of v0, /device:TPU:16, one launch (start us, length us, event | category | flops | bytes accessed | tf_op | source)
XLA Modules:
  0.0 2135.1 jit_solution(14163987279730319424)
XLA Ops:
  9.1 11.8 collective-permute-done.2
  30.4 653.7 %while.37 = (s32[]{:T(128)}, f32[2,256,256]{1,2,0:T(8,128)}, f32[4,1,2,256,256]{4,3,2,1,0:T(8,128)}, f32[4,2,256,256]{2,3,1,0:T(8,128)}, s32[35]{0:T(128)S(1)}, ...) while((s32[]{:T(128)}, f32[2,256,256]{1,2,0:T(8,128)}, ...), condition=%wide.region_5.6_spmd.clone.clone.clone, body=%wide.region_0.5_spmd.clone.clone.clone.sunk | while | flops 3223584768 | bytes 32247176 | solution.py:177
  36.3 17.8 conditional.14
  59.9 17.8 conditional.14
  83.7 17.8 conditional.14
  109.9 17.8 conditional.14
  141.4 24.2 %collective-permute-start = (f32[2,256,256]{2,1,0:T(8,128)S(1)}, f32[2,256,256]{2,1,0:T(8,128)S(1)}, u32[]{:S(2)}, u32[]{:S(2)}) collective-permute-start(f32[2,256,256]{2,1,0:T(8,128)S(1)} %copy.18), channel_id=1, source_target_pairs={{0,4},{4,8},{8,12},{12,16},{16,20},{20,24},{24,28},{28,32},{32,36}... | collective-permute-start | bytes 1572872 | tf_op jit(solution)/shard_map/while/body/eval_jaxpr/ppermute | solution.py:15
  183.6 24.1 %collective-permute-start = (f32[2,256,256]{2,1,0:T(8,128)S(1)}, f32[2,256,256]{2,1,0:T(8,128)S(1)}, u32[]{:S(2)}, u32[]{:S(2)}) collective-permute-start(f32[2,256,256]{2,1,0:T(8,128)S(1)} %copy.18), channel_id=1, source_target_pairs={{0,4},{4,8},{8,12},{12,16},{16,20},{20,24},{24,28},{28,32},{32,36}... | collective-permute-start | bytes 1572872 | tf_op jit(solution)/shard_map/while/body/eval_jaxpr/ppermute | solution.py:15
  225.7 12.2 collective-permute-start
  255.9 21.7 %collective-permute-start = (f32[2,256,256]{2,1,0:T(8,128)S(1)}, f32[2,256,256]{2,1,0:T(8,128)S(1)}, u32[]{:S(2)}, u32[]{:S(2)}) collective-permute-start(f32[2,256,256]{2,1,0:T(8,128)S(1)} %copy.18), channel_id=1, source_target_pairs={{0,4},{4,8},{8,12},{12,16},{16,20},{20,24},{24,28},{28,32},{32,36}... | collective-permute-start | bytes 1572872 | tf_op jit(solution)/shard_map/while/body/eval_jaxpr/ppermute | solution.py:15
  295.6 12.2 collective-permute-start
  325.8 21.7 %collective-permute-start = (f32[2,256,256]{2,1,0:T(8,128)S(1)}, f32[2,256,256]{2,1,0:T(8,128)S(1)}, u32[]{:S(2)}, u32[]{:S(2)}) collective-permute-start(f32[2,256,256]{2,1,0:T(8,128)S(1)} %copy.18), channel_id=1, source_target_pairs={{0,4},{4,8},{8,12},{12,16},{16,20},{20,24},{24,28},{28,32},{32,36}... | collective-permute-start | bytes 1572872 | tf_op jit(solution)/shard_map/while/body/eval_jaxpr/ppermute | solution.py:15
  365.5 13.7 collective-permute-start
  384.6 9.2 collective-permute-start
  399.3 26.3 %collective-permute-start = (f32[2,256,256]{2,1,0:T(8,128)S(1)}, f32[2,256,256]{2,1,0:T(8,128)S(1)}, u32[]{:S(2)}, u32[]{:S(2)}) collective-permute-start(f32[2,256,256]{2,1,0:T(8,128)S(1)} %copy.18), channel_id=1, source_target_pairs={{0,4},{4,8},{8,12},{12,16},{16,20},{20,24},{24,28},{28,32},{32,36}... | collective-permute-start | bytes 1572872 | tf_op jit(solution)/shard_map/while/body/eval_jaxpr/ppermute | solution.py:15
  430.9 9.3 collective-permute-start
  445.6 10.1 collective-permute-start
  461.1 9.3 collective-permute-start
  475.8 19.6 collective-permute-start
  500.8 9.3 collective-permute-start
  515.5 10.1 collective-permute-start
  530.9 9.3 collective-permute-start
  545.6 19.6 collective-permute-start
  570.6 9.3 collective-permute-start
  585.3 10.1 collective-permute-start
  600.8 9.3 collective-permute-start
  615.5 19.6 collective-permute-start
  640.4 9.3 collective-permute-start
  655.1 10.1 collective-permute-start
  670.6 9.3 collective-permute-start
  692.1 1428.1 %while.38 = (s32[]{:T(128)}, f32[2,256,256]{1,2,0:T(8,128)}, f32[1,2,512,384]{2,3,1,0:T(8,128)}, s32[35]{0:T(128)S(1)}, s32[]{:T(128)}, /*index=5*/pred[4]{0:T(5...) while((s32[]{:T(128)}, f32[2,256,256]{1,2,0:T(8,128)}, ...), condition=%wide.region_11.12_spmd.clone.clone.clone, body=%wide.region_6.11_spmd.clone.clone.clone.sunk | while | flops 3224109056 | bytes 29624028 | solution.py:214
  697.3 19.3 collective-permute-done.1
  722.6 9.5 collective-permute-done.1
  751.6 9.5 collective-permute-done.1
  767.0 17.1 collective-permute-done.1
  790.0 9.5 collective-permute-done.1
  819.0 9.5 collective-permute-done.1
  834.5 17.1 collective-permute-done.1
  857.5 9.5 collective-permute-done.1
  872.9 8.7 collective-permute-done.1
  887.6 8.7 collective-permute-done.1
  902.3 16.7 collective-permute-done.1
  925.0 9.5 collective-permute-done.1
  955.1 8.7 collective-permute-done.1
  969.7 19.0 collective-permute-done.1
  994.7 9.5 collective-permute-done.1
  1024.8 8.7 collective-permute-done.1
  1039.5 16.7 collective-permute-done.1
  1062.2 9.5 collective-permute-done.1
  1077.6 8.7 collective-permute-done.1
  1107.0 16.7 collective-permute-done.1
  1129.6 8.7 collective-permute-done.1
  1144.3 8.7 collective-permute-done.1
  1159.0 8.7 collective-permute-done.1
  1173.7 17.4 collective-permute-done.1
  1197.1 8.7 collective-permute-done.1
  1211.8 8.8 collective-permute-done.1
  1226.5 747.1 %collective-permute-done.1 = f32[2,256,256]{2,1,0:T(8,128)S(1)} collective-permute-done((f32[2,256,256]{2,1,0:T(8,128)S(1)}, f32[2,256,256]{2,1,0:T(8,128)S(1)}, u32[]{:S(2)}, u32[]{:S(2)}) %collective-permute-start.1) | collective-permute-done | bytes 524320 | tf_op jit(solution)/shard_map/while/body/eval_jaxpr/ppermute | solution.py:15
  1973.7 25.0 %conditional.15 = (f32[2,256,256]{1,2,0:T(8,128)}, f32[1,2,512,384]{2,3,1,0:T(8,128)}) conditional(s32[]{:T(128)} %convert_element_type.96, f32[1,2,512,384]{2,3,1,0:T(8,128)} %get-tuple-element.1459, (s32[]{:T(128)}, s32[4]{0:T(128)S(1)}, s32[4]{0:T(128)S(1)}, f32[1,2,512,384]{2,3,1,0:T(8,128)}, pred[]{:T(512)}, ...), branch_computations={%region_7.7_spmd, %region_8.10_spmd.clone} | conditional | flops 3223977984 | bytes 26214700 | solution.py:210
  2012.2 24.9 %conditional.15 = (f32[2,256,256]{1,2,0:T(8,128)}, f32[1,2,512,384]{2,3,1,0:T(8,128)}) conditional(s32[]{:T(128)} %convert_element_type.96, f32[1,2,512,384]{2,3,1,0:T(8,128)} %get-tuple-element.1459, (s32[]{:T(128)}, s32[4]{0:T(128)S(1)}, s32[4]{0:T(128)S(1)}, f32[1,2,512,384]{2,3,1,0:T(8,128)}, pred[]{:T(512)}, ...), branch_computations={%region_7.7_spmd, %region_8.10_spmd.clone} | conditional | flops 3223977984 | bytes 26214700 | solution.py:210
  2048.6 24.6 %conditional.15 = (f32[2,256,256]{1,2,0:T(8,128)}, f32[1,2,512,384]{2,3,1,0:T(8,128)}) conditional(s32[]{:T(128)} %convert_element_type.96, f32[1,2,512,384]{2,3,1,0:T(8,128)} %get-tuple-element.1459, (s32[]{:T(128)}, s32[4]{0:T(128)S(1)}, s32[4]{0:T(128)S(1)}, f32[1,2,512,384]{2,3,1,0:T(8,128)}, pred[]{:T(512)}, ...), branch_computations={%region_7.7_spmd, %region_8.10_spmd.clone} | conditional | flops 3223977984 | bytes 26214700 | solution.py:210
  2078.3 16.6 collective-permute-done.1
  2095.0 25.2 %conditional.15 = (f32[2,256,256]{1,2,0:T(8,128)}, f32[1,2,512,384]{2,3,1,0:T(8,128)}) conditional(s32[]{:T(128)} %convert_element_type.96, f32[1,2,512,384]{2,3,1,0:T(8,128)} %get-tuple-element.1459, (s32[]{:T(128)}, s32[4]{0:T(128)S(1)}, s32[4]{0:T(128)S(1)}, f32[1,2,512,384]{2,3,1,0:T(8,128)}, pred[]{:T(512)}, ...), branch_computations={%region_7.7_spmd, %region_8.10_spmd.clone} | conditional | flops 3223977984 | bytes 26214700 | solution.py:210
  2122.2 12.0 collective-permute-done.3
  (735 shorter events, 671.2 us)
Async XLA Ops:
  1.5 19.5 collective-permute-start.2
  141.4 27.5 %collective-permute-start = (f32[2,256,256]{2,1,0:T(8,128)S(1)}, f32[2,256,256]{2,1,0:T(8,128)S(1)}, u32[]{:S(2)}, u32[]{:S(2)}) collective-permute-start(f32[2,256,256]{2,1,0:T(8,128)S(1)} %copy.18), channel_id=1, source_target_pairs={{0,4},{4,8},{8,12},{12,16},{16,20},{20,24},{24,28},{28,32},{32,36}... | collective-permute-start | bytes 1572872 | tf_op jit(solution)/shard_map/while/body/eval_jaxpr/ppermute | solution.py:15
  183.6 27.5 %collective-permute-start = (f32[2,256,256]{2,1,0:T(8,128)S(1)}, f32[2,256,256]{2,1,0:T(8,128)S(1)}, u32[]{:S(2)}, u32[]{:S(2)}) collective-permute-start(f32[2,256,256]{2,1,0:T(8,128)S(1)} %copy.18), channel_id=1, source_target_pairs={{0,4},{4,8},{8,12},{12,16},{16,20},{20,24},{24,28},{28,32},{32,36}... | collective-permute-start | bytes 1572872 | tf_op jit(solution)/shard_map/while/body/eval_jaxpr/ppermute | solution.py:15
  213.1 10.5 collective-permute-start
  225.7 15.5 collective-permute-start
  243.3 10.5 collective-permute-start
  255.9 25.1 %collective-permute-start = (f32[2,256,256]{2,1,0:T(8,128)S(1)}, f32[2,256,256]{2,1,0:T(8,128)S(1)}, u32[]{:S(2)}, u32[]{:S(2)}) collective-permute-start(f32[2,256,256]{2,1,0:T(8,128)S(1)} %copy.18), channel_id=1, source_target_pairs={{0,4},{4,8},{8,12},{12,16},{16,20},{20,24},{24,28},{28,32},{32,36}... | collective-permute-start | bytes 1572872 | tf_op jit(solution)/shard_map/while/body/eval_jaxpr/ppermute | solution.py:15
  283.0 10.5 collective-permute-start
  295.6 15.5 collective-permute-start
  325.8 25.1 %collective-permute-start = (f32[2,256,256]{2,1,0:T(8,128)S(1)}, f32[2,256,256]{2,1,0:T(8,128)S(1)}, u32[]{:S(2)}, u32[]{:S(2)}) collective-permute-start(f32[2,256,256]{2,1,0:T(8,128)S(1)} %copy.18), channel_id=1, source_target_pairs={{0,4},{4,8},{8,12},{12,16},{16,20},{20,24},{24,28},{28,32},{32,36}... | collective-permute-start | bytes 1572872 | tf_op jit(solution)/shard_map/while/body/eval_jaxpr/ppermute | solution.py:15
  352.9 10.5 collective-permute-start
  365.5 17.1 collective-permute-start
  384.6 12.6 collective-permute-start
  399.3 29.6 %collective-permute-start = (f32[2,256,256]{2,1,0:T(8,128)S(1)}, f32[2,256,256]{2,1,0:T(8,128)S(1)}, u32[]{:S(2)}, u32[]{:S(2)}) collective-permute-start(f32[2,256,256]{2,1,0:T(8,128)S(1)} %copy.18), channel_id=1, source_target_pairs={{0,4},{4,8},{8,12},{12,16},{16,20},{20,24},{24,28},{28,32},{32,36}... | collective-permute-start | bytes 1572872 | tf_op jit(solution)/shard_map/while/body/eval_jaxpr/ppermute | solution.py:15
  430.9 12.6 collective-permute-start
  445.6 13.4 collective-permute-start
  461.1 12.6 collective-permute-start
  475.8 22.9 %collective-permute-start = (f32[2,256,256]{2,1,0:T(8,128)S(1)}, f32[2,256,256]{2,1,0:T(8,128)S(1)}, u32[]{:S(2)}, u32[]{:S(2)}) collective-permute-start(f32[2,256,256]{2,1,0:T(8,128)S(1)} %copy.18), channel_id=1, source_target_pairs={{0,4},{4,8},{8,12},{12,16},{16,20},{20,24},{24,28},{28,32},{32,36}... | collective-permute-start | bytes 1572872 | tf_op jit(solution)/shard_map/while/body/eval_jaxpr/ppermute | solution.py:15
  500.8 12.6 collective-permute-start
  515.5 13.4 collective-permute-start
  530.9 12.6 collective-permute-start
  545.6 22.9 %collective-permute-start = (f32[2,256,256]{2,1,0:T(8,128)S(1)}, f32[2,256,256]{2,1,0:T(8,128)S(1)}, u32[]{:S(2)}, u32[]{:S(2)}) collective-permute-start(f32[2,256,256]{2,1,0:T(8,128)S(1)} %copy.18), channel_id=1, source_target_pairs={{0,4},{4,8},{8,12},{12,16},{16,20},{20,24},{24,28},{28,32},{32,36}... | collective-permute-start | bytes 1572872 | tf_op jit(solution)/shard_map/while/body/eval_jaxpr/ppermute | solution.py:15
  570.6 12.6 collective-permute-start
  585.3 13.4 collective-permute-start
  600.8 12.6 collective-permute-start
  615.5 22.9 %collective-permute-start = (f32[2,256,256]{2,1,0:T(8,128)S(1)}, f32[2,256,256]{2,1,0:T(8,128)S(1)}, u32[]{:S(2)}, u32[]{:S(2)}) collective-permute-start(f32[2,256,256]{2,1,0:T(8,128)S(1)} %copy.18), channel_id=1, source_target_pairs={{0,4},{4,8},{8,12},{12,16},{16,20},{20,24},{24,28},{28,32},{32,36}... | collective-permute-start | bytes 1572872 | tf_op jit(solution)/shard_map/while/body/eval_jaxpr/ppermute | solution.py:15
  640.4 12.6 collective-permute-start
  655.1 13.4 collective-permute-start
  670.6 12.6 collective-permute-start
  693.4 23.2 %collective-permute-start.1 = (f32[2,256,256]{2,1,0:T(8,128)S(1)}, f32[2,256,256]{2,1,0:T(8,128)S(1)}, u32[]{:S(2)}, u32[]{:S(2)}) collective-permute-start(f32[2,256,256]{2,1,0:T(8,128)S(1)} %copy.19), channel_id=1, source_target_pairs={{4,0},{8,4},{12,8},{16,12},{20,16},{24,20},{28,24},{32,28},{36,32}... | collective-permute-start | bytes 1572872 | tf_op jit(solution)/shard_map/while/body/eval_jaxpr/ppermute | solution.py:15
  718.7 13.4 collective-permute-start.1
  734.1 11.5 collective-permute-start.1
  747.7 13.4 collective-permute-start.1
  763.1 21.0 collective-permute-start.1
  786.1 13.4 collective-permute-start.1
  801.6 11.5 collective-permute-start.1
  815.1 13.4 collective-permute-start.1
  830.6 21.0 collective-permute-start.1
  853.6 13.4 collective-permute-start.1
  869.0 12.6 collective-permute-start.1
  883.7 12.6 collective-permute-start.1
  898.4 20.6 collective-permute-start.1
  921.1 13.4 collective-permute-start.1
  936.5 12.6 collective-permute-start.1
  951.2 12.6 collective-permute-start.1
  965.8 22.9 %collective-permute-start.1 = (f32[2,256,256]{2,1,0:T(8,128)S(1)}, f32[2,256,256]{2,1,0:T(8,128)S(1)}, u32[]{:S(2)}, u32[]{:S(2)}) collective-permute-start(f32[2,256,256]{2,1,0:T(8,128)S(1)} %copy.19), channel_id=1, source_target_pairs={{4,0},{8,4},{12,8},{16,12},{20,16},{24,20},{28,24},{32,28},{36,32}... | collective-permute-start | bytes 1572872 | tf_op jit(solution)/shard_map/while/body/eval_jaxpr/ppermute | solution.py:15
  990.8 13.4 collective-permute-start.1
  1006.2 12.6 collective-permute-start.1
  1020.9 12.6 collective-permute-start.1
  1035.6 20.6 collective-permute-start.1
  1058.3 13.4 collective-permute-start.1
  1073.7 12.6 collective-permute-start.1
  1088.4 12.6 collective-permute-start.1
  1103.1 20.6 collective-permute-start.1
  1125.7 12.6 collective-permute-start.1
  1140.4 12.6 collective-permute-start.1
  1155.1 12.6 collective-permute-start.1
  1169.8 21.3 collective-permute-start.1
  1193.2 12.6 collective-permute-start.1
  1207.9 12.7 collective-permute-start.1
  1222.6 751.0 %collective-permute-start.1 = (f32[2,256,256]{2,1,0:T(8,128)S(1)}, f32[2,256,256]{2,1,0:T(8,128)S(1)}, u32[]{:S(2)}, u32[]{:S(2)}) collective-permute-start(f32[2,256,256]{2,1,0:T(8,128)S(1)} %copy.19), channel_id=1, source_target_pairs={{4,0},{8,4},{12,8},{16,12},{20,16},{24,20},{28,24},{32,28},{36,32}... | collective-permute-start | bytes 1572872 | tf_op jit(solution)/shard_map/while/body/eval_jaxpr/ppermute | solution.py:15
  1999.9 12.2 collective-permute-start.1
  2074.4 20.5 collective-permute-start.1
  2122.1 12.1 collective-permute-start.3
  (22 other events, 116.5 us)
where the time goes:
time: 2140 us
  waiting for transfers between devices  1150 us (54%)
  starting transfers between devices  442 us (21%)
  local copies, waits for them, and re-layouts  302 us (14%)
  loops' own time  127 us (6%)
  other arithmetic  82.4 us (4%)
  matrix products  34.1 us (2%)
    ppermute x70, waiting for transfers between devices, passed_along(): return lax.ppermute(block, axis, route)  1120 us
    ppermute x70, starting transfers between devices, passed_along(): return lax.ppermute(block, axis, route)  442 us
    while x70, local copies, waits for them, and re-layouts  86.5 us
    broadcast_in_dim x64, local copies, waits for them, and re-layouts, depth_chain(): empty_wave = jnp.zeros((2, window_size, window_size), jnp.float32)  53 us
    another operation x1, loops' own time, depth_chain(): lax.scan(backward_step, (empty_wave, grad_start), jnp.arange(step_count,...  46.9 us
    another operation x1, loops' own time, depth_chain(): lax.scan(forward_step, (empty_wave, stored_start, starts_start), jnp.aran...  46.6 us
  transfers between devices with their start and end apart: 72, of which 37 were waited for; matrix products, arithmetic and copies ran while one was open for 6% of the time, Pallas kernels for 0%

commit v1 on v0

v1 whole, which is shorter than its diff:
```python
import numpy as np

import jax
import jax.numpy as jnp
from jax import lax
from jax.experimental import pallas as pl
from jax.experimental.pallas import tpu as pltpu
from jax.sharding import PartitionSpec as P

WIN = 256
HALF = 128
ROWS = 256
COLS = 384
CAP = 4
GROUP = 8
STAGES = 4
CHUNK = 64
smoothing = 0.25
f32 = jnp.float32
bf16 = jnp.bfloat16


def split_np(table):
    high = table.astype(bf16)
    low = (table - high.astype(np.float64)).astype(bf16)
    return high, low


def make_tables():
    n = np.arange(HALF)[:, None]
    k = np.arange(HALF)[None, :]
    tables = []
    for parity in (0, 1):
        angle = -2.0 * np.pi * ((n * (2 * k + parity)) % WIN) / WIN
        c, s = np.cos(angle) / 16.0, np.sin(angle) / 16.0
        full = np.block([[c, s], [-s, c]])
        for table in (full, full.T):
            tables.extend(split_np(table))
    dft = np.stack(tables)
    order = np.concatenate([np.arange(0, WIN, 2), np.arange(1, WIN, 2)])
    freq = (((order + HALF) % WIN) - HALF).astype(np.float64)
    phase = -np.pi * (freq[:, None] ** 2 + freq[None, :] ** 2) / (2.0 * WIN)
    fresnel = np.stack([np.cos(phase), np.sin(phase)]).astype(np.float32)
    pick = np.zeros((WIN, WIN))
    pick[np.arange(WIN), order] = 1.0
    return dft, fresnel, np.stack([pick, pick.T]).astype(bf16)


EVEN, EVEN_T, ODD, ODD_T = 0, 2, 4, 6


def halves(value):
    high = value.astype(bf16)
    low = (value - high.astype(f32)).astype(bf16)
    return high, low


def mm(a, b):
    return jnp.dot(a, b, preferred_element_type=f32)


def right_mul(data, dft, which):
    high, low = halves(data)
    return mm(high, dft[which]) + mm(low, dft[which]) + mm(high, dft[which + 1])


def left_mul(dft, which, data):
    high, low = halves(data)
    return mm(dft[which], high) + mm(dft[which], low) + mm(dft[which + 1], high)


def lanes(a, b):
    return jnp.concatenate([a, b], axis=1)


def rows(a, b):
    return jnp.concatenate([a, b], axis=0)


def propagate(source, sink, dft, mid, pointwise):
    for start in range(0, WIN, CHUNK):
        part = slice(start, start + CHUNK)
        re, im = source(part)
        even = lanes(re[:, :HALF] + re[:, HALF:], im[:, :HALF] + im[:, HALF:])
        odd = lanes(re[:, :HALF] - re[:, HALF:], im[:, :HALF] - im[:, HALF:])
        even = right_mul(even, dft, EVEN)
        odd = right_mul(odd, dft, ODD)
        mid[0, part, :] = lanes(even[:, :HALF], odd[:, :HALF])
        mid[1, part, :] = lanes(even[:, HALF:], odd[:, HALF:])
    re_top, re_low = mid[0, :HALF, :], mid[0, HALF:, :]
    im_top, im_low = mid[1, :HALF, :], mid[1, HALF:, :]
    even = left_mul(dft, EVEN_T, rows(re_top + re_low, im_top + im_low))
    odd = left_mul(dft, ODD_T, rows(re_top - re_low, im_top - im_low))
    even = pointwise(slice(0, HALF), even[:HALF], even[HALF:])
    odd = pointwise(slice(HALF, WIN), odd[:HALF], odd[HALF:])
    even = left_mul(dft, EVEN, rows(*even))
    odd = left_mul(dft, ODD, rows(*odd))
    mid[0, :HALF, :] = even[:HALF] + odd[:HALF]
    mid[0, HALF:, :] = even[:HALF] - odd[:HALF]
    mid[1, :HALF, :] = even[HALF:] + odd[HALF:]
    mid[1, HALF:, :] = even[HALF:] - odd[HALF:]
    for start in range(0, WIN, CHUNK):
        part = slice(start, start + CHUNK)
        re, im = mid[0, part, :], mid[1, part, :]
        even = right_mul(lanes(re[:, :HALF], im[:, :HALF]), dft, EVEN_T)
        odd = right_mul(lanes(re[:, HALF:], im[:, HALF:]), dft, ODD_T)
        total, diff = even + odd, even - odd
        sink(part, lanes(total[:, :HALF], diff[:, :HALF]), lanes(total[:, HALF:], diff[:, HALF:]))


def fresnel_times(fresnel, sign):
    def pointwise(part, re, im):
        c, s = fresnel[0, part, :], fresnel[1, part, :]
        if sign > 0:
            return re * c - im * s, re * s + im * c
        return re * c + im * s, im * c - re * s

    return pointwise


def forward_kernel(last, flag, wave_in, win_re, win_im, dft, fresnel, *rest):
    if last:
        pattern, pick, wave_out, stored, wave, mid, far_amp = rest
    else:
        wave_out, stored, wave, mid = rest
    step = pl.program_id(0)

    @pl.when(flag[0] == 1)
    def _():
        @pl.when(step == 0)
        def _():
            wave[...] = wave_in[...].astype(f32)
            if last:
                picked = mm(pick[0], pattern[...]).astype(bf16)
                far_amp[...] = mm(picked, pick[1])

        stored[0] = wave[...]

        def source(part):
            wr, wi = wave[0, part, :], wave[1, part, :]
            tr, ti = win_re[0, part, :], win_im[0, part, :]
            return wr * tr - wi * ti, wr * ti + wi * tr

        def sink(part, re, im):
            wave[0, part, :] = re
            wave[1, part, :] = im

        def sink_out(part, re, im):
            wave_out[0, part, :] = re
            wave_out[1, part, :] = im

        def exit_point(part, re, im):
            smooth = jnp.sqrt(re * re + im * im + smoothing)
            factor = 1.0 - far_amp[part, :] / smooth
            return factor * re, factor * im

        if last:
            @pl.when(step < GROUP - 1)
            def _():
                propagate(source, sink, dft, mid, fresnel_times(fresnel, 1))

            @pl.when(step == GROUP - 1)
            def _():
                propagate(source, sink_out, dft, mid, exit_point)
        else:
            propagate(source, sink, dft, mid, fresnel_times(fresnel, 1))

            @pl.when(step == GROUP - 1)
            def _():
                wave_out[...] = wave[...]


def forward_stage(last, flag, wave, win_re, win_im, dft, fresnel, pattern=None, pick=None):
    whole = lambda *shape: pl.BlockSpec(shape, lambda i, flag: (0,) * len(shape))
    one = pl.BlockSpec((1, WIN, WIN), lambda i, flag: (i * flag[0], 0, 0))
    args = [wave, win_re, win_im, dft, fresnel]
    specs = [whole(2, WIN, WIN), one, one, whole(8, WIN, WIN), whole(2, WIN, WIN)]
    scratch = [pltpu.VMEM((2, WIN, WIN), f32), pltpu.VMEM((2, WIN, WIN), f32)]
    if last:
        args += [pattern, pick]
        specs += [whole(WIN, WIN), whole(2, WIN, WIN)]
        scratch += [pltpu.VMEM((WIN, WIN), f32)]
    return pl.pallas_call(
        lambda *refs: forward_kernel(last, *refs),
        grid_spec=pltpu.PrefetchScalarGridSpec(
            num_scalar_prefetch=1,
            grid=(GROUP,),
            in_specs=specs,
            out_specs=[
                whole(2, WIN, WIN),
                pl.BlockSpec((1, 2, WIN, WIN), lambda i, flag: (i * flag[0], 0, 0, 0)),
            ],
            scratch_shapes=scratch,
        ),
        out_shape=[
            jax.ShapeDtypeStruct((2, WIN, WIN), f32),
            jax.ShapeDtypeStruct((GROUP, 2, WIN, WIN), f32),
        ],
        compiler_params=pltpu.CompilerParams(vmem_limit_bytes=40 * 2**20),
        name="forward_last" if last else "forward_stage",
    )(flag, *args)


def backward_kernel(last, flag, adj_in, win_re, win_im, stored, dft, fresnel, grad_in,
                    adj_out, grad, adj, mid, grad_buf, sem):
    del grad_in
    step = pl.program_id(0)
    slot = lax.rem(step, 2)

    def grad_copy(slot_id, slice_id):
        return pltpu.make_async_copy(grad_buf.at[slot_id], grad.at[:, slice_id], sem.at[slot_id])

    @pl.when(flag[0] == 1)
    def _():
        @pl.when(step >= 2)
        def _():
            grad_copy(slot, GROUP - 1 - (step - 2)).wait()

        def finish(part, mr, mi):
            wr, wi = stored[0, 0, part, :], stored[0, 1, part, :]
            grad_buf[slot, 0, part, :] = wr * mr + wi * mi
            grad_buf[slot, 1, part, :] = wr * mi - wi * mr
            tr, ti = win_re[0, part, :], win_im[0, part, :]
            adj[0, part, :] = tr * mr + ti * mi
            adj[1, part, :] = tr * mi - ti * mr

        def source(part):
            return adj[0, part, :], adj[1, part, :]

        if last:
            @pl.when(step == 0)
            def _():
                for start in range(0, WIN, CHUNK):
                    part = slice(start, start + CHUNK)
                    finish(part, adj_in[0, part, :], adj_in[1, part, :])

            @pl.when(step > 0)
            def _():
                propagate(source, finish, dft, mid, fresnel_times(fresnel, -1))
        else:
            @pl.when(step == 0)
            def _():
                adj[...] = adj_in[...]

            propagate(source, finish, dft, mid, fresnel_times(fresnel, -1))

        grad_copy(slot, GROUP - 1 - step).start()

        @pl.when(step == GROUP - 1)
        def _():
            adj_out[...] = adj[...]
            grad_copy(1 - slot, 1).wait()
            grad_copy(slot, 0).wait()


def backward_stage(last, flag, adj, win_re, win_im, stored, dft, fresnel, grad):
    whole = lambda *shape: pl.BlockSpec(shape, lambda i, flag: (0,) * len(shape))
    one = pl.BlockSpec((1, WIN, WIN), lambda i, flag: ((GROUP - 1 - i) * flag[0], 0, 0))
    return pl.pallas_call(
        lambda *refs: backward_kernel(last, *refs),
        grid_spec=pltpu.PrefetchScalarGridSpec(
            num_scalar_prefetch=1,
            grid=(GROUP,),
            in_specs=[
                whole(2, WIN, WIN),
                one,
                one,
                pl.BlockSpec((1, 2, WIN, WIN), lambda i, flag: ((GROUP - 1 - i) * flag[0], 0, 0, 0)),
                whole(8, WIN, WIN),
                whole(2, WIN, WIN),
                pl.BlockSpec(memory_space=pl.ANY),
            ],
            out_specs=[whole(2, WIN, WIN), pl.BlockSpec(memory_space=pl.ANY)],
            scratch_shapes=[
                pltpu.VMEM((2, WIN, WIN), f32),
                pltpu.VMEM((2, WIN, WIN), f32),
                pltpu.VMEM((2, 2, WIN, WIN), f32),
                pltpu.SemaphoreType.DMA((2,)),
            ],
        ),
        out_shape=[
            jax.ShapeDtypeStruct((2, WIN, WIN), f32),
            jax.ShapeDtypeStruct((2, GROUP, WIN, WIN), f32),
        ],
        input_output_aliases={7: 1},
        compiler_params=pltpu.CompilerParams(vmem_limit_bytes=40 * 2**20),
        name="backward_last" if last else "backward_stage",
    )(flag, adj, win_re, win_im, stored, dft, fresnel, grad)


def corner(place, slot):
    row, col = place[slot, 0], place[slot, 1]
    base = pl.multiple_of((row >> 3) << 3, 8)
    return base, row - base, col


def cut_kernel(place, own, after, out, slab):
    slab[:, :ROWS, :] = own[0]
    slab[:, ROWS:, :] = after[0]
    for slot in range(CAP):
        base, shift, col = corner(place, slot)
        for comp in range(2):
            picked = slab[comp, pl.ds(base, WIN + 8), :]
            picked = pltpu.roll(picked, lax.rem(COLS - col, COLS), 1)[:, :WIN]
            out[2 * slot + comp] = pltpu.roll(picked, lax.rem(WIN + 8 - shift, WIN + 8), 0)[:WIN]


def cut_windows(place, own, after):
    vmem = pl.BlockSpec(memory_space=pltpu.VMEM)
    return pl.pallas_call(
        cut_kernel,
        in_specs=[pl.BlockSpec(memory_space=pltpu.SMEM), vmem, vmem],
        out_specs=vmem,
        out_shape=jax.ShapeDtypeStruct((2 * CAP, WIN, WIN), f32),
        scratch_shapes=[pltpu.VMEM((2, 2 * ROWS, COLS), f32)],
        compiler_params=pltpu.CompilerParams(vmem_limit_bytes=40 * 2**20),
        name="cut_windows",
    )(place, own, after)


def add_kernel(place, live, grads, top, low, slab):
    slab[...] = jnp.zeros_like(slab)
    for slot in range(CAP):
        base, shift, col = corner(place, slot)

        @pl.when(slot < live[0])
        def _():
            for comp in range(2):
                tall = rows(grads[2 * slot + comp], jnp.zeros((8, WIN), f32))
                tall = pltpu.roll(tall, shift, 0)
                wide = lanes(tall, jnp.zeros((WIN + 8, COLS - WIN), f32))
                slab[comp, pl.ds(base, WIN + 8), :] += pltpu.roll(wide, col, 1)
    top[0] = slab[:, :ROWS, :]
    low[0] = slab[:, ROWS:, :]


def add_windows(place, live, grads):
    vmem = pl.BlockSpec(memory_space=pltpu.VMEM)
    smem = pl.BlockSpec(memory_space=pltpu.SMEM)
    shape = jax.ShapeDtypeStruct((1, 2, ROWS, COLS), f32)
    return pl.pallas_call(
        add_kernel,
        in_specs=[smem, smem, vmem],
        out_specs=[vmem, vmem],
        out_shape=[shape, shape],
        scratch_shapes=[pltpu.VMEM((2, 2 * ROWS, COLS), f32)],
        compiler_params=pltpu.CompilerParams(vmem_limit_bytes=40 * 2**20),
        name="add_windows",
    )(place, live, grads)


def device(x, z, core):
    return x * GROUP + z * 2 + core


ring = range(4)
rings = [[x * GROUP + i for i in range(GROUP)] for x in ring]


def body(object_slices, probe_wave, amplitudes, positions, counts):
    depth = lax.axis_index("depth")
    stripe = lax.axis_index("stripe")
    stage = depth // GROUP
    slot = (depth % GROUP) // 2
    core = depth % 2
    dft, fresnel, pick = (jnp.asarray(t) for t in make_tables())
    place = lax.dynamic_slice_in_dim(positions, stripe * CAP, CAP, 0)
    live = lax.dynamic_slice_in_dim(counts, stripe, 1, 0)
    works = (core == 0) & (slot < live[0])

    def flag_of(t):
        return (works & (stage == t)).astype(jnp.int32)[None]

    after = lax.ppermute(object_slices, "stripe", [(i, (i - 1) % 4) for i in ring])
    windows = cut_windows(place, object_slices, after)
    mine = lax.all_to_all(windows, "depth", 0, 0, axis_index_groups=rings, tiled=True)
    win_im = lax.ppermute(mine, "depth", [(device(x, z, 1), device(x, z, 0)) for x in ring for z in ring])
    win_re = mine

    pattern = lax.dynamic_index_in_dim(amplitudes, slot, 0, keepdims=False)
    wave = probe_wave
    stored = []
    for t in range(STAGES):
        last = t == STAGES - 1
        extra = (pattern, pick) if last else ()
        wave, kept = forward_stage(last, flag_of(t), wave, win_re, win_im, dft, fresnel, *extra)
        stored.append(kept)
        if not last:
            wave = lax.ppermute(wave, "depth", [(device(t, z, 0), device(t + 1, z, 0)) for z in ring])
    grad = jnp.zeros((2, GROUP, WIN, WIN), f32)
    for t in reversed(range(STAGES)):
        last = t == STAGES - 1
        wave, grad = backward_stage(
            last, flag_of(t), wave, win_re, win_im, stored[t], dft, fresnel, grad
        )
        if t > 0:
            wave = lax.ppermute(wave, "depth", [(device(t, z, 0), device(t - 1, z, 0)) for z in ring])
    grad_im = lax.ppermute(
        grad[1], "depth", [(device(x, z, 0), device(x, z, 1)) for x in ring for z in ring]
    )
    outgoing = jnp.where(core == 0, grad[0], grad_im)
    back = lax.all_to_all(outgoing, "depth", 0, 0, axis_index_groups=rings, tiled=True)
    top, low = add_windows(place, live, back)
    return top + lax.ppermute(low, "stripe", [(i, (i + 1) % 4) for i in ring])


def solution(mesh):
    return jax.shard_map(
        body,
        mesh=mesh,
        in_specs=(P("depth", None, "stripe", None), P(), P("stripe", None, None), P(), P()),
        out_specs=P("depth", None, "stripe", None),
        check_vma=False,
    )
```

time: 2140 us -> 341 us (0.16)
  waiting for transfers between devices: 1150 us -> 193 us
  starting transfers between devices: 442 us -> 12.7 us
  local copies, waits for them, and re-layouts: 302 us -> 16 us
  loops' own time: 127 us -> 0 us
  other arithmetic: 82.4 us -> 1.23 us
  blocking collectives: 0 us -> 62.6 us
  Pallas kernels: 0 us -> 51.7 us
  matrix products: 34.1 us -> 0 us
    ppermute x72 -> x10, waiting for transfers between devices: 1150 us -> 193 us  [the longest x3 144 us: body(): lax.ppermute(wave, 'depth', [(device(t, z, 0), device(t - 1, z, 0)) for z...]
    ppermute x72 -> x10, starting transfers between devices: 442 us -> 12.7 us  [the longest x3 5.09 us: body(): lax.ppermute(wave, 'depth', [(device(t, z, 0), device(t + 1, z, 0)) for z...]
    another operation x80 -> x0, loops' own time: 127 us -> none  [the longest x1 46.9 us: depth_chain(): lax.scan(backward_step, (empty_wave, grad_start), jnp.arange(step_count,...]
    dynamic_slice x158 -> x2, local copies, waits for them, and re-layouts: 94.6 us -> 1.4 us  [the longest x1 0.75 us: body(): place = lax.dynamic_slice_in_dim(positions, stripe * CAP, CAP, 0)]
    while x71 -> x0, local copies, waits for them, and re-layouts: 88.4 us -> none
    all_to_all x0 -> x2, blocking collectives: none -> 62.6 us  [the longest x1 32.6 us: body(): lax.all_to_all(windows, 'depth', 0, 0, axis_index_groups=rings, tiled=True)]
    broadcast_in_dim x67 -> x1, local copies, waits for them, and re-layouts: 57.4 us -> 0.4 us  [body(): grad = jnp.zeros((2, GROUP, WIN, WIN), f32)]
    pallas_call x0 -> x10, Pallas kernels: none -> 51.7 us  [the longest x4 23.8 us: forward_stage(): pl.pallas_call(lambda *refs: forward_kernel(last, *refs), grid_spec=pltpu...]
  transfers between devices with their start and end apart: 72 -> 10, of which waited for: 37 -> 6; matrix products, arithmetic and copies ran while one was open for 6% -> 0% of each run, Pallas kernels for 0% -> 0%
where the time goes in v1:
time: 341 us; the launch traced here: 338 us
  waiting for transfers between devices  193 us (57%)
  blocking collectives  62.6 us (18%)
  Pallas kernels  51.7 us (15%)
  local copies, waits for them, and re-layouts  16 us (5%)
  starting transfers between devices  12.7 us (4%)
    ppermute x3, waiting for transfers between devices, body(): lax.ppermute(wave, 'depth', [(device(t, z, 0), device(t - 1, z, 0)) for z...  144 us
    all_to_all x1, blocking collectives, body(): lax.all_to_all(windows, 'depth', 0, 0, axis_index_groups=rings, tiled=True)  32.6 us
    all_to_all x1, blocking collectives, body(): lax.all_to_all(outgoing, 'depth', 0, 0, axis_index_groups=rings, tiled=True)  30 us
    pallas_call x4, Pallas kernels, forward_stage(): pl.pallas_call(lambda *refs: forward_kernel(last, *refs), grid_spec=pltpu...  23.8 us
    pallas_call x4, Pallas kernels, backward_stage(): pl.pallas_call(lambda *refs: backward_kernel(last, *refs), grid_spec=pltp...  23.2 us
    ppermute x1, waiting for transfers between devices, body(): lax.ppermute(object_slices, 'stripe', [(i, (i - 1) % 4) for i in ring])  18.2 us
    ppermute x1, waiting for transfers between devices, body(): return top + lax.ppermute(low, 'stripe', [(i, (i + 1) % 4) for i in ring])  17.4 us
    unnamed x31, local copies, waits for them, and re-layouts  14.1 us
  transfers between devices with their start and end apart: 10, of which 6 were waited for; matrix products, arithmetic and copies ran while one was open for 0% of the time, Pallas kernels for 0%

profile of v1, /device:TPU:16, one launch (start us, length us, event | category | flops | bytes accessed | tf_op | source)
XLA Modules:
  0.0 338.5 jit_solution(3094688116417910841)
XLA Ops:
  0.0 0.0 copy-start
  0.0 0.0 copy-start.6
  0.0 0.4 collective-permute-start
  0.5 0.7 constant_dynamic-slice_fusion
  1.2 0.1 copy.14.place
  1.3 18.2 %collective-permute-done.after = f32[1,2,256,384]{3,2,1,0:T(8,128)S(1)} collective-permute-done((f32[1,2,256,384]{3,2,1,0:T(8,128)}, f32[1,2,256,384]{3,2,1,0:T(8,128)S(1)}, u32[]{:S(2)}, u32[]{:S(2)}) %collective-permute-start) | collective-permute-done | bytes 786464 | tf_op jit(solution)/shard_map/ppermute | solution.py:374
  19.5 0.0 copy-start.11
  19.5 1.1 copy-done.11
  20.6 0.0 copy-start.14
  20.6 0.0 copy-start.12
  20.6 1.9 cut_windows.1
  22.5 32.6 %all_to_all.10.refs_2_ = f32[8,256,256]{2,1,0:T(8,128)S(1)} all-to-all(f32[8,256,256]{2,1,0:T(8,128)S(1)} %cut_windows.1), channel_id=1, replica_groups={{0,4,8,12,16,20,24,28},{32,36,40,44,48,52,56,60},{64,68,72,76,80,84,88,..., dimensions={0} | all-to-all | bytes 4194304 | tf_op jit(solution)/shard_map/all_to_all | solution.py:376
  55.1 1.3 collective-permute-start.1
  56.5 0.0 copy-done.14
  56.5 0.7 dynamic_slice.11.live
  57.8 3.5 %collective-permute-done.1.refs_3_ = f32[8,256,256]{2,1,0:T(8,128)} collective-permute-done((f32[8,256,256]{2,1,0:T(8,128)S(1)}, f32[8,256,256]{2,1,0:T(8,128)}, u32[]{:S(2)}, u32[]{:S(2)}) %collective-permute-start.1) | collective-permute-done | bytes 2097184 | tf_op jit(solution)/shard_map/ppermute | solution.py:377
  61.3 0.0 copy-done.6
  61.3 0.0 copy-done.12
  61.3 0.0 copy-start.1
  61.3 1.2 copy-done.1
  62.6 18.8 %forward_stage.3 = (f32[2,256,256]{2,1,0:T(8,128)}, f32[8,2,256,256]{3,2,1,0:T(8,128)S(1)}) custom-call(s32[1]{0:T(128)} %bitcast.1.refs_0_, bf16[2,256,256]{2,1,0:T(8,128)(2,1)S(1)} %copy-done.12, f32[8,256,256]{2,1,0:T(8,128)S(1)} %all_to_all.10.refs_2_, f32[8,256,256]{2,1,0:T(8,128)} %collective-permute-done.1.refs_3_, ...), custom_call_target="tpu_custom_call" | custom-call | tf_op jit(solution)/shard_map/forward_stage/pallas_call | solution.py:183
  81.4 0.0 copy-start.7
  81.4 2.0 copy-done.7
  83.3 2.1 collective-permute-start.2
  85.4 6.2 %collective-permute-done.2.refs_1_ = f32[2,256,256]{2,1,0:T(8,128)} collective-permute-done((f32[2,256,256]{2,1,0:T(8,128)}, f32[2,256,256]{2,1,0:T(8,128)}, u32[]{:S(2)}, u32[]{:S(2)}) %collective-permute-start.2) | collective-permute-done | bytes 524320 | tf_op jit(solution)/shard_map/ppermute | solution.py:389
  91.6 0.0 copy-start.2
  91.6 1.2 copy-done.2
  92.8 2.0 forward_stage.4
  94.8 2.0 copy-done.8
  96.8 1.5 collective-permute-start.3
  98.3 0.0 collective-permute-done.3.refs_1_
  98.3 1.2 copy-done.3
  99.6 1.9 forward_stage.5
  101.5 2.0 copy-done.9
  103.5 1.5 collective-permute-start.4
  105.0 0.0 copy-done
  105.0 0.0 collective-permute-done.4.refs_1_
  105.0 0.0 copy-done.13
  105.0 0.0 copy-start.4
  105.0 1.2 copy-done.4
  106.2 1.1 forward_last.1
  107.4 1.9 copy-done.10
  109.3 0.4 broadcast_in_dim.35.refs_7_
  109.7 1.2 backward_last.1
  110.9 0.9 collective-permute-start.5
  111.8 0.0 collective-permute-done.5.refs_1_
  111.8 1.2 backward_stage.3
  112.9 0.7 collective-permute-start.6
  113.6 0.0 collective-permute-done.6.refs_1_
  113.6 0.0 copy-start.5
  113.7 1.2 backward_stage.4
  114.9 1.3 collective-permute-start.7
  116.2 144.5 %collective-permute-done.7.refs_1_ = f32[2,256,256]{2,1,0:T(8,128)S(1)} collective-permute-done((f32[2,256,256]{2,1,0:T(8,128)S(1)}, f32[2,256,256]{2,1,0:T(8,128)S(1)}, u32[]{:S(2)}, u32[]{:S(2)}) %collective-permute-start.7) | collective-permute-done | bytes 524320 | tf_op jit(solution)/shard_map/ppermute | solution.py:397
  260.7 0.0 copy-done.5
  260.7 19.7 %backward_stage.5 = (f32[2,256,256]{2,1,0:T(8,128)}, f32[2,8,256,256]{3,2,1,0:T(8,128)S(1)}) custom-call(s32[1]{0:T(128)} %bitcast.1.refs_0_, f32[2,256,256]{2,1,0:T(8,128)S(1)} %collective-permute-done.7.refs_1_, f32[8,256,256]{2,1,0:T(8,128)S(1)} %all_to_all.10.refs_2_, ...), custom_call_target="tpu_custom_call", output_to_operand_aliasing={{1}: (7, {})} | custom-call | tf_op jit(solution)/shard_map/backward_stage/pallas_call | solution.py:259
  280.4 0.1 slice_bitcast_fusion
  280.5 1.4 collective-permute-start.8
  281.9 3.6 %collective-permute-done.8 = f32[8,256,256]{2,1,0:T(8,128)S(1)} collective-permute-done((f32[8,256,256]{2,1,0:T(8,128)S(1)}, f32[8,256,256]{2,1,0:T(8,128)S(1)}, u32[]{:S(2)}, u32[]{:S(2)}) %collective-permute-start.8) | collective-permute-done | bytes 2097184 | tf_op jit(solution)/shard_map/ppermute | solution.py:398
  285.6 0.3 bitcast_select_fusion
  285.8 30.0 %all_to_all.11.grads = f32[8,256,256]{2,1,0:T(8,128)S(1)} all-to-all(f32[8,256,256]{2,1,0:T(8,128)S(1)} %bitcast_select_fusion), channel_id=1, replica_groups={{0,4,8,12,16,20,24,28},{32,36,40,44,48,52,56,60},{64,68,72,76,80,84,88,..., dimensions={0} | all-to-all | bytes 4194304 | tf_op jit(solution)/shard_map/all_to_all | solution.py:402
  315.8 2.7 add_windows.1
  318.5 1.6 collective-permute-start.9
  320.2 17.4 %collective-permute-done.9 = f32[1,2,256,384]{3,2,1,0:T(8,128)S(1)} collective-permute-done((f32[1,2,256,384]{3,2,1,0:T(8,128)S(1)}, f32[1,2,256,384]{3,2,1,0:T(8,128)S(1)}, u32[]{:S(2)}, u32[]{:S(2)}) %collective-permute-start.9) | collective-permute-done | bytes 786464 | tf_op jit(solution)/shard_map/ppermute | solution.py:404
  337.5 1.0 add.27
  (6 shorter events, 0.0 us)
Async XLA Ops:
  0.0 105.0 %copy-start = (bf16[4,256,256]{2,1,0:T(8,128)(2,1)S(1)}, bf16[4,256,256]{2,1,0:T(8,128)(2,1)}, u32[]{:S(2)}) copy-start(bf16[4,256,256]{2,1,0:T(8,128)(2,1)} %param.10) | copy-start | bytes 1572868
  0.0 61.3 %copy-start.6 = (f32[2,256,256]{2,1,0:T(8,128)S(1)}, f32[2,256,256]{2,1,0:T(8,128)}, u32[]{:S(2)}) copy-start(f32[2,256,256]{2,1,0:T(8,128)} %constant.72.clone.refs_5_.refs_6_) | copy-start | bytes 1572868
  0.0 19.5 %collective-permute-start = (f32[1,2,256,384]{3,2,1,0:T(8,128)}, f32[1,2,256,384]{3,2,1,0:T(8,128)S(1)}, u32[]{:S(2)}, u32[]{:S(2)}) collective-permute-start(f32[1,2,256,384]{3,2,1,0:T(8,128)} %own.1), channel_id=1, source_target_pairs={{0,3},{1,0},{2,1},{3,2},{4,7},{5,4},{6,5},{7,6},{8,11},{9,8},{10,9... | collective-permute-start | bytes 2359304 | tf_op jit(solution)/shard_map/ppermute | solution.py:374
  19.5 1.1 copy-start.11
  20.6 35.9 %copy-start.14 = (s32[4]{0:T(128)S(1)}, s32[4]{0:T(128)}, u32[]{:S(2)}) copy-start(s32[4]{0:T(128)} %param.12) | copy-start | bytes 52
  20.6 40.7 %copy-start.12 = (bf16[2,256,256]{2,1,0:T(8,128)(2,1)S(1)}, bf16[2,256,256]{2,1,0:T(8,128)(2,1)}, u32[]{:S(2)}) copy-start(bf16[2,256,256]{2,1,0:T(8,128)(2,1)} %refs_1_.1) | copy-start | bytes 786436
  55.1 6.2 %collective-permute-start.1 = (f32[8,256,256]{2,1,0:T(8,128)S(1)}, f32[8,256,256]{2,1,0:T(8,128)}, u32[]{:S(2)}, u32[]{:S(2)}) collective-permute-start(f32[8,256,256]{2,1,0:T(8,128)S(1)} %all_to_all.10.refs_2_), channel_id=1, source_target_pairs={{4,0},{12,8},{20,16},{28,24},{36,32},{44,40},{52,48},{60,56},{68,6... | collective-permute-start | bytes 6291464 | tf_op jit(solution)/shard_map/ppermute | solution.py:377
  61.3 1.2 copy-start.1
  81.4 2.0 copy-start.7
  83.3 8.3 %collective-permute-start.2 = (f32[2,256,256]{2,1,0:T(8,128)}, f32[2,256,256]{2,1,0:T(8,128)}, u32[]{:S(2)}, u32[]{:S(2)}) collective-permute-start(f32[2,256,256]{2,1,0:T(8,128)} %get-tuple-element.22), channel_id=1, source_target_pairs={{0,32},{8,40},{16,48},{24,56},{1,33},{9,41},{17,49},{25,57},{2,34}... | collective-permute-start | bytes 1572872 | tf_op jit(solution)/shard_map/ppermute | solution.py:389
  91.6 1.2 copy-start.2
  92.8 12.2 %copy-start.13 = (bf16[2,256,256]{2,1,0:T(8,128)(2,1)S(1)}, bf16[2,256,256]{2,1,0:T(8,128)(2,1)}, u32[]{:S(2)}) copy-start(bf16[2,256,256]{2,1,0:T(8,128)(2,1)} %constant.73.clone.refs_7_) | copy-start | bytes 786436
  94.8 2.0 copy-start.8
  96.8 1.5 collective-permute-start.3
  98.3 1.2 copy-start.3
  101.5 2.0 copy-start.9
  103.5 1.5 collective-permute-start.4
  105.0 1.2 copy-start.4
  107.4 1.9 copy-start.10
  110.9 0.9 collective-permute-start.5
  112.9 0.7 collective-permute-start.6
  113.6 147.0 %copy-start.5 = (bf16[8,256,256]{2,1,0:T(8,128)(2,1)S(1)}, bf16[8,256,256]{2,1,0:T(8,128)(2,1)}, u32[]{:S(2)}) copy-start(bf16[8,256,256]{2,1,0:T(8,128)(2,1)} %constant.71.clone.refs_4_.refs_5_) | copy-start | bytes 3145732
  114.9 145.8 %collective-permute-start.7 = (f32[2,256,256]{2,1,0:T(8,128)S(1)}, f32[2,256,256]{2,1,0:T(8,128)S(1)}, u32[]{:S(2)}, u32[]{:S(2)}) collective-permute-start(f32[2,256,256]{2,1,0:T(8,128)S(1)} %get-tuple-element.33), channel_id=1, source_target_pairs={{32,0},{40,8},{48,16},{56,24},{33,1},{41,9},{49,17},{57,25},{34,2}... | collective-permute-start | bytes 1572872 | tf_op jit(solution)/shard_map/ppermute | solution.py:397
  280.5 5.1 %collective-permute-start.8 = (f32[8,256,256]{2,1,0:T(8,128)S(1)}, f32[8,256,256]{2,1,0:T(8,128)S(1)}, u32[]{:S(2)}, u32[]{:S(2)}) collective-permute-start(f32[8,256,256]{2,1,0:T(8,128)S(1)} %slice_bitcast_fusion), channel_id=1, source_target_pairs={{0,4},{8,12},{16,20},{24,28},{32,36},{40,44},{48,52},{56,60},{64,6... | collective-permute-start | bytes 6291464 | tf_op jit(solution)/shard_map/ppermute | solution.py:398
  318.5 19.0 %collective-permute-start.9 = (f32[1,2,256,384]{3,2,1,0:T(8,128)S(1)}, f32[1,2,256,384]{3,2,1,0:T(8,128)S(1)}, u32[]{:S(2)}, u32[]{:S(2)}) collective-permute-start(f32[1,2,256,384]{3,2,1,0:T(8,128)S(1)} %get-tuple-element.38), channel_id=1, source_target_pairs={{0,1},{1,2},{2,3},{3,0},{4,5},{5,6},{6,7},{7,4},{8,9},{9,10},{10,1... | collective-permute-start | bytes 2359304 | tf_op jit(solution)/shard_map/ppermute | solution.py:404

commit v2 on v1

v2 whole, which is shorter than its diff:
```python
import numpy as np

import jax
import jax.numpy as jnp
from jax import lax
from jax.experimental import pallas as pl
from jax.experimental.pallas import tpu as pltpu
from jax.sharding import PartitionSpec as P

WIN = 256
HALF = 128
ROWS = 256
COLS = 384
CAP = 4
GROUP = 8
STAGES = 4
CHUNK = 128
smoothing = 0.25
f32 = jnp.float32
bf16 = jnp.bfloat16


def split_np(table):
    high = table.astype(bf16)
    low = (table - high.astype(np.float64)).astype(bf16)
    return high, low


def make_tables():
    n = np.arange(HALF)[:, None]
    k = np.arange(HALF)[None, :]
    tables = []
    for parity in (0, 1):
        angle = -2.0 * np.pi * ((n * (2 * k + parity)) % WIN) / WIN
        c, s = np.cos(angle) / 16.0, np.sin(angle) / 16.0
        full = np.block([[c, s], [-s, c]])
        for table in (full, full.T):
            tables.extend(split_np(table))
    dft = np.stack(tables)
    freq = (((np.arange(WIN) + HALF) % WIN) - HALF).astype(np.float64)
    response = np.fft.ifft(np.exp(-1j * np.pi * freq**2 / (2.0 * WIN)))
    near = response[(n - k) % WIN]
    far = response[(n - k - HALF) % WIN]
    tables = []
    for block in ((near + far) / 2.0, (near - far) / 2.0):
        tables.extend(split_np(np.block([[block.real, block.imag], [-block.imag, block.real]])))
    chirp = np.stack(tables)
    order = np.concatenate([np.arange(0, WIN, 2), np.arange(1, WIN, 2)])
    pick = np.zeros((WIN, WIN))
    pick[np.arange(WIN), order] = 1.0
    return dft, chirp, np.stack([pick, pick.T]).astype(bf16)


SUM, DIFF = 0, 2
EVEN, EVEN_T, ODD, ODD_T = 0, 2, 4, 6


def halves(value):
    high = value.astype(bf16)
    low = (value - high.astype(f32)).astype(bf16)
    return high, low


def mm(a, b):
    return jnp.dot(a, b, preferred_element_type=f32)


def right_mul(data, dft, which):
    high, low = halves(data)
    return mm(high, dft[which]) + mm(low, dft[which]) + mm(high, dft[which + 1])


def left_mul(dft, which, data):
    high, low = halves(data)
    return mm(dft[which], high) + mm(dft[which], low) + mm(dft[which + 1], high)


def lanes(a, b):
    return jnp.concatenate([a, b], axis=1)


def rows(a, b):
    return jnp.concatenate([a, b], axis=0)


def propagate(source, sink, chirp):
    top, low = slice(0, HALF), slice(HALF, WIN)
    re_top, im_top = source(top)
    re_low, im_low = source(low)

    sr, si, dr, di = re_top + re_low, im_top + im_low, re_top - re_low, im_top - im_low
    re, im = rows(sr, dr), rows(si, di)
    scol = right_mul(lanes(re[:, :HALF] + re[:, HALF:], im[:, :HALF] + im[:, HALF:]), chirp, SUM)
    dcol = right_mul(lanes(re[:, :HALF] - re[:, HALF:], im[:, :HALF] - im[:, HALF:]), chirp, DIFF)
    im, re = lanes(scol[:, HALF:], dcol[:, HALF:]), lanes(scol[:, :HALF], dcol[:, :HALF])
    total = left_mul(chirp, SUM, rows(im[:HALF], re[:HALF]))
    diff = left_mul(chirp, DIFF, rows(im[HALF:], re[HALF:]))
    for part, both in ((top, total + diff), (low, total - diff)):
        im, re = both[:HALF], both[HALF:]
        sink(
            part,
            lanes(re[:, :HALF] + re[:, HALF:], re[:, :HALF] - re[:, HALF:]),
            lanes(im[:, :HALF] + im[:, HALF:], im[:, :HALF] - im[:, HALF:]),
        )


def exit_wave(source, sink, dft, mid, pointwise):
    for start in range(0, WIN, CHUNK):
        part = slice(start, start + CHUNK)
        re, im = source(part)
        even = lanes(re[:, :HALF] + re[:, HALF:], im[:, :HALF] + im[:, HALF:])
        odd = lanes(re[:, :HALF] - re[:, HALF:], im[:, :HALF] - im[:, HALF:])
        even = right_mul(even, dft, EVEN)
        odd = right_mul(odd, dft, ODD)
        mid[0, part, :] = lanes(even[:, :HALF], odd[:, :HALF])
        mid[1, part, :] = lanes(even[:, HALF:], odd[:, HALF:])
    re_top, re_low = mid[0, :HALF, :], mid[0, HALF:, :]
    im_top, im_low = mid[1, :HALF, :], mid[1, HALF:, :]
    even = left_mul(dft, EVEN_T, rows(re_top + re_low, im_top + im_low))
    odd = left_mul(dft, ODD_T, rows(re_top - re_low, im_top - im_low))
    even = pointwise(slice(0, HALF), even[:HALF], even[HALF:])
    odd = pointwise(slice(HALF, WIN), odd[:HALF], odd[HALF:])
    even = left_mul(dft, EVEN, rows(*even))
    odd = left_mul(dft, ODD, rows(*odd))
    mid[0, :HALF, :] = even[:HALF] + odd[:HALF]
    mid[0, HALF:, :] = even[:HALF] - odd[:HALF]
    mid[1, :HALF, :] = even[HALF:] + odd[HALF:]
    mid[1, HALF:, :] = even[HALF:] - odd[HALF:]
    for start in range(0, WIN, CHUNK):
        part = slice(start, start + CHUNK)
        re, im = mid[0, part, :], mid[1, part, :]
        even = right_mul(lanes(re[:, :HALF], im[:, :HALF]), dft, EVEN_T)
        odd = right_mul(lanes(re[:, HALF:], im[:, HALF:]), dft, ODD_T)
        total, diff = even + odd, even - odd
        sink(part, lanes(total[:, :HALF], diff[:, :HALF]), lanes(total[:, HALF:], diff[:, HALF:]))


CODED = WIN + 16
i16 = jnp.int16


def exponent(most):
    return jnp.ceil(jnp.log2(jnp.maximum(most, 1e-30)))


def encode(dst, part, value):
    exp = exponent(jnp.max(jnp.abs(value), axis=0, keepdims=True))
    scaled = jnp.clip(jnp.round(value * jnp.exp2(15.0 - exp)), -32767.0, 32767.0)
    dst[part, :] = scaled.astype(jnp.int32).astype(i16)
    return jnp.broadcast_to(exp, (8, value.shape[1])).astype(jnp.int32)


def encode_tail(dst, top, low):
    dst[WIN:, :] = jnp.concatenate([top, low], axis=0).astype(i16)


def decode(src, part):
    tail = src[WIN:, :].astype(jnp.int32)[8 * (part.start // HALF):][:1].astype(f32)
    return src[part, :].astype(jnp.int32).astype(f32) * jnp.exp2(tail - 15.0)


TOP, LOW = slice(0, HALF), slice(HALF, WIN)


def encode_plane(dst, top, low):
    encode_tail(dst, encode(dst, TOP, top), encode(dst, LOW, low))


def decode_wave(dst, src):
    for comp in range(2):
        for part in (TOP, LOW):
            dst[comp, part, :] = decode(src.at[comp], part)


def encode_wave(dst, src):
    for comp in range(2):
        encode_plane(dst.at[comp], src[comp, TOP, :], src[comp, LOW, :])


def times(re, im, win, slot, part):
    tr, ti = win[slot, 0, part, :], win[slot, 1, part, :]
    return re * tr - im * ti, re * ti + im * tr


class Windows:
    def __init__(self, piles, buf, sem):
        self.piles, self.buf, self.sem = piles, buf, sem

    def copies(self, i, odd):
        return [
            pltpu.make_async_copy(self.piles[2 * odd + comp].at[i >> 1], self.buf.at[odd, comp], self.sem.at[odd, comp])
            for comp in range(2)
        ]

    def start(self, i):
        for odd in range(2):
            @pl.when((i & 1) == odd)
            def _():
                for copy in self.copies(i, odd):
                    copy.start()

    def wait(self, i):
        for comp in range(2):
            pltpu.make_async_copy(
                self.piles[comp].at[i >> 1], self.buf.at[i & 1, comp], self.sem.at[i & 1, comp]
            ).wait()


def forward_slice(src, dst, windows, i, chirp):
    def source(part):
        return times(src[0, part, :], src[1, part, :], windows.buf, i & 1, part)

    def sink(part, re, im):
        dst[0, part, :] = re
        dst[1, part, :] = im

    propagate(source, sink, chirp)


def retreat(i, part, re, im, adj, wave, windows, grad, tails):
    wr, wi = wave[0, part, :], wave[1, part, :]
    half = part.start // HALF
    for comp, value in enumerate((wr * re - wi * im, -(wr * im + wi * re))):
        tails[comp, 8 * half:8 * half + 8, :] = encode(grad.at[comp], part, value)
    adj[0, part, :], adj[1, part, :] = times(re, im, windows.buf, i & 1, part)


def finish_grad(grad, tails):
    for comp in range(2):
        grad[comp, WIN:, :] = tails[comp].astype(i16)


def backward_slice(i, adj, wave, windows, chirp, grad, tails):
    def source(part):
        return adj[0, part, :], adj[1, part, :]

    def sink(part, re, im):
        retreat(i, part, re, im, adj, wave, windows, grad, tails)

    propagate(source, sink, chirp)
    finish_grad(grad, tails)


def copy_wave(dst, src):
    for comp in range(2):
        dst[comp] = src[comp].astype(f32)


def forward_kernel(first, flag, wave_in, er, ei, orr, oi, chirp, *rest):
    wave_out, waves, win_buf, win_sem, buf, sem = rest[-6:]
    windows = Windows((er, ei, orr, oi), win_buf, win_sem)

    def store(i):
        slot = lax.rem(i, 3)
        return pltpu.make_async_copy(buf.at[slot], waves.at[i], sem.at[slot])

    @pl.when(flag[0] == 1)
    def _():
        windows.start(jnp.int32(0))
        if first:
            copy_wave(buf.at[0], wave_in)
        else:
            decode_wave(buf.at[0], wave_in)

        @pl.loop(0, GROUP)
        def _(i):
            @pl.when(i + 1 < GROUP)
            def _():
                windows.start(i + 1)

            store(i).start()

            @pl.when(i >= 2)
            def _():
                store(i - 2).wait()

            windows.wait(i)
            forward_slice(buf.at[lax.rem(i, 3)], buf.at[lax.rem(i + 1, 3)], windows, i, chirp)

        encode_wave(wave_out, buf.at[GROUP % 3])
        store(jnp.int32(GROUP - 2)).wait()
        store(jnp.int32(GROUP - 1)).wait()


class Gradients:
    def __init__(self, grads, buf, sem):
        self.grads, self.buf, self.sem = grads, buf, sem

    def copies(self, i):
        slot = i & 1
        return [
            pltpu.make_async_copy(self.buf.at[slot, comp], self.grads.at[comp, slot, i >> 1], self.sem.at[slot, comp])
            for comp in range(2)
        ]

    def start(self, i):
        for copy in self.copies(i):
            copy.start()

    def wait(self, i):
        for copy in self.copies(i):
            copy.wait()


def turn_kernel(flag, wave_in, er, ei, orr, oi, chirp, dft, pattern, pick, adj_out, grads,
                win_buf, win_sem, grad_buf, grad_sem, adj, tails, waves, mid, far_amp):
    windows = Windows((er, ei, orr, oi), win_buf, win_sem)
    out = Gradients(grads, grad_buf, grad_sem)
    end = GROUP - 1

    @pl.when(flag[0] == 1)
    def _():
        windows.start(jnp.int32(0))
        picked = mm(pick[0], pattern[...]).astype(bf16)
        far_amp[...] = mm(picked, pick[1])
        decode_wave(waves.at[0], wave_in)

        @pl.loop(0, end)
        def _(i):
            windows.start(i + 1)
            windows.wait(i)
            forward_slice(waves.at[i], waves.at[i + 1], windows, i, chirp)

        windows.wait(jnp.int32(end))
        windows.start(jnp.int32(end - 1))

        def source(part):
            return times(waves[end, 0, part, :], waves[end, 1, part, :], win_buf, end & 1, part)

        def exit_point(part, re, im):
            smooth = jnp.sqrt(re * re + im * im + smoothing)
            factor = 1.0 - far_amp[part, :] / smooth
            return factor * re, factor * im

        def sink(part, re, im):
            retreat(end, part, re, -im, adj, waves.at[end], windows, grad_buf.at[end & 1], tails)

        exit_wave(source, sink, dft, mid, exit_point)
        finish_grad(grad_buf.at[end & 1], tails)
        out.start(jnp.int32(end))

        @pl.loop(0, end)
        def _(step):
            i = end - 1 - step
            windows.wait(i)

            @pl.when(i > 0)
            def _():
                windows.start(i - 1)

            @pl.when(step > 0)
            def _():
                out.wait(i + 2)

            backward_slice(i, adj, waves.at[i], windows, chirp, grad_buf.at[i & 1], tails)
            out.start(i)

        encode_wave(adj_out, adj)
        out.wait(jnp.int32(1))
        out.wait(jnp.int32(0))


def backward_kernel(flag, adj_in, er, ei, orr, oi, chirp, waves, grads_in, adj_out, grads,
                    win_buf, win_sem, grad_buf, grad_sem, adj, tails, wave_buf, wave_sem):
    del grads_in
    windows = Windows((er, ei, orr, oi), win_buf, win_sem)
    out = Gradients(grads, grad_buf, grad_sem)

    def load(i):
        return pltpu.make_async_copy(waves.at[i], wave_buf.at[i & 1], wave_sem.at[i & 1])

    @pl.when(flag[0] == 1)
    def _():
        windows.start(jnp.int32(GROUP - 1))
        load(jnp.int32(GROUP - 1)).start()
        decode_wave(adj, adj_in)

        @pl.loop(0, GROUP)
        def _(step):
            i = GROUP - 1 - step
            windows.wait(i)
            load(i).wait()

            @pl.when(i > 0)
            def _():
                windows.start(i - 1)
                load(i - 1).start()

            @pl.when(step >= 2)
            def _():
                out.wait(i + 2)

            backward_slice(i, adj, wave_buf.at[i & 1], windows, chirp, grad_buf.at[i & 1], tails)
            out.start(i)

        encode_wave(adj_out, adj)
        out.wait(jnp.int32(1))
        out.wait(jnp.int32(0))


vmem = pl.BlockSpec(memory_space=pltpu.VMEM)
smem = pl.BlockSpec(memory_space=pltpu.SMEM)
hbm = pl.BlockSpec(memory_space=pltpu.HBM)
params = pltpu.CompilerParams(vmem_limit_bytes=20 * 2**20)
wave_shape = jax.ShapeDtypeStruct((2, CODED, WIN), i16)
waves_shape = pltpu.HBM((GROUP, 2, WIN, WIN), f32)
grads_shape = pltpu.HBM((2, 2, GROUP // 2, CODED, WIN), i16)
pair = lambda: [pltpu.VMEM((2, 2, WIN, WIN), f32), pltpu.SemaphoreType.DMA((2, 2))]
grad_scratch = lambda: [
    pltpu.VMEM((2, 2, CODED, WIN), i16),
    pltpu.SemaphoreType.DMA((2, 2)),
    pltpu.VMEM((2, WIN, WIN), f32),
    pltpu.VMEM((2, 16, WIN), jnp.int32),
]


def forward_stage(flag, wave, wins, chirp, waves):
    first = waves is None
    args = [flag, wave, *wins, chirp] + ([] if first else [waves])
    return pl.pallas_call(
        lambda *refs: forward_kernel(first, *refs),
        in_specs=[smem, vmem] + [hbm] * 4 + [vmem] + ([] if first else [hbm]),
        out_specs=[vmem, hbm],
        out_shape=[wave_shape, waves_shape],
        input_output_aliases={} if first else {7: 1},
        scratch_shapes=pair() + [pltpu.VMEM((3, 2, WIN, WIN), f32), pltpu.SemaphoreType.DMA((3,))],
        compiler_params=params,
        name="forward_stage",
    )(*args)


def turn_stage(flag, wave, wins, chirp, dft, pattern, pick):
    return pl.pallas_call(
        turn_kernel,
        in_specs=[smem, vmem] + [hbm] * 4 + [vmem] * 4,
        out_specs=[vmem, hbm],
        out_shape=[wave_shape, grads_shape],
        scratch_shapes=pair() + grad_scratch() + [
            pltpu.VMEM((GROUP, 2, WIN, WIN), f32),
            pltpu.VMEM((2, WIN, WIN), f32),
            pltpu.VMEM((WIN, WIN), f32),
        ],
        compiler_params=params,
        name="turn_stage",
    )(flag, wave, *wins, chirp, dft, pattern, pick)


def backward_stage(flag, adj, wins, chirp, waves, grads):
    return pl.pallas_call(
        backward_kernel,
        in_specs=[smem, vmem] + [hbm] * 4 + [vmem, hbm, hbm],
        out_specs=[vmem, hbm],
        out_shape=[wave_shape, grads_shape],
        input_output_aliases={8: 1},
        scratch_shapes=pair() + grad_scratch() + [pltpu.VMEM((2, 2, WIN, WIN), f32), pltpu.SemaphoreType.DMA((2,))],
        compiler_params=params,
        name="backward_stage",
    )(flag, adj, *wins, chirp, waves, grads)


def corner(place, slot):
    row, col = place[slot, 0], place[slot, 1]
    base = pl.multiple_of((row >> 3) << 3, 8)
    return base, row - base, col


def cut_kernel(place, own, after, out, slab):
    slab[:ROWS, :] = own[...]
    slab[ROWS:, :] = after[...]
    for slot in range(CAP):
        base, shift, col = corner(place, slot)
        picked = slab[pl.ds(base, WIN + 8), :]
        picked = pltpu.roll(picked, lax.rem(COLS - col, COLS), 1)[:, :WIN]
        out[slot] = pltpu.roll(picked, lax.rem(WIN + 8 - shift, WIN + 8), 0)[:WIN]


def cut_windows(place, own, after):
    return pl.pallas_call(
        cut_kernel,
        in_specs=[smem, vmem, vmem],
        out_specs=vmem,
        out_shape=jax.ShapeDtypeStruct((CAP, WIN, WIN), f32),
        scratch_shapes=[pltpu.VMEM((2 * ROWS, COLS), f32)],
        compiler_params=params,
        name="cut_windows",
    )(place, own, after)


def add_kernel(place, live, grads, top, low, slab):
    slab[...] = jnp.zeros_like(slab)
    for slot in range(CAP):
        base, shift, col = corner(place, slot)

        @pl.when(slot < live[0])
        def _():
            own = grads.at[slot]
            tall = jnp.concatenate([decode(own, TOP), decode(own, LOW), jnp.zeros((8, WIN), f32)], axis=0)
            tall = pltpu.roll(tall, shift, 0)
            wide = lanes(tall, jnp.zeros((WIN + 8, COLS - WIN), f32))
            slab[pl.ds(base, WIN + 8), :] += pltpu.roll(wide, col, 1)
    top[...] = slab[:ROWS, :]
    encode_plane(low, slab[ROWS:ROWS + HALF, :], slab[ROWS + HALF:, :])


def add_windows(place, live, grads):
    return pl.pallas_call(
        add_kernel,
        in_specs=[smem, smem, vmem],
        out_specs=[vmem, vmem],
        out_shape=[jax.ShapeDtypeStruct((ROWS, COLS), f32), jax.ShapeDtypeStruct((CODED, COLS), i16)],
        scratch_shapes=[pltpu.VMEM((2 * ROWS, COLS), f32)],
        compiler_params=params,
        name="add_windows",
    )(place, live, grads)


def join_kernel(top_re, low_re, top_im, low_im, out):
    for comp, (top, low) in enumerate(((top_re, low_re), (top_im, low_im))):
        for part in (TOP, LOW):
            out[0, comp, part, :] = top[part, :] + decode(low, part)


def join(parts):
    return pl.pallas_call(
        join_kernel,
        in_specs=[vmem] * 4,
        out_specs=vmem,
        out_shape=jax.ShapeDtypeStruct((1, 2, ROWS, COLS), f32),
        compiler_params=params,
        name="join",
    )(*parts)


def device(x, z, core):
    return x * GROUP + z * 2 + core


ring = range(4)
rings = [[device(x, z, core) for z in ring] for x in ring for core in range(2)]


def after_that(value, *earlier):
    return lax.optimization_barrier((value, *earlier))[0]


def exchange(value):
    return lax.all_to_all(value, "depth", 0, 0, axis_index_groups=rings, tiled=True)


def to_other_core(value, source):
    pairs = [(device(x, z, source), device(x, z, 1 - source)) for x in ring for z in ring]
    return lax.ppermute(value, "depth", pairs)


def hop(value, source, target):
    return lax.ppermute(value, "depth", [(device(source, z, 0), device(target, z, 0)) for z in ring])


def body(object_slices, probe_wave, amplitudes, positions, counts):
    depth = lax.axis_index("depth")
    stripe = lax.axis_index("stripe")
    stage = depth // GROUP
    slot = (depth % GROUP) // 2
    core = depth % 2
    dft, chirp, pick = (jnp.asarray(t) for t in make_tables())
    place = lax.dynamic_slice_in_dim(positions, stripe * CAP, CAP, 0)
    live = lax.dynamic_slice_in_dim(counts, stripe, 1, 0)
    works = (core == 0) & (slot < live[0])

    def flag_of(t):
        return (works & (stage == t)).astype(jnp.int32)[None]

    own_re, own_im = object_slices[0, 0], object_slices[0, 1]
    back = [(i, (i - 1) % 4) for i in ring]
    after_re = lax.ppermute(own_re, "stripe", back)
    after_im = lax.ppermute(own_im, "stripe", back)
    even_re = exchange(cut_windows(place, own_re, after_re))
    even_im = exchange(cut_windows(place, own_im, after_im))
    odd_re, odd_im = to_other_core(even_re, 1), to_other_core(even_im, 1)
    wins = (even_re, even_im, odd_re, odd_im)

    pattern = lax.dynamic_index_in_dim(amplitudes, slot, 0, keepdims=False)
    wave, waves = probe_wave, None
    for t in range(STAGES - 1):
        wave, waves = forward_stage(flag_of(t), wave, wins, chirp, waves)
        wave = hop(wave, t, t + 1)
    wave, grads = turn_stage(flag_of(STAGES - 1), wave, wins, chirp, dft, pattern, pick)
    for t in reversed(range(STAGES - 1)):
        wave = hop(wave, t + 1, t)
        wave, grads = backward_stage(flag_of(t), wave, wins, chirp, waves, grads)

    forth = [(i, (i + 1) % 4) for i in ring]
    parts = []
    for even, odd in grads:
        odd = to_other_core(odd, 0)
        top, low = add_windows(place, live, exchange(jnp.where(core == 0, even, odd)))
        parts += [top, lax.ppermute(low, "stripe", forth)]
    return join(parts)


def solution(mesh):
    return jax.shard_map(
        body,
        mesh=mesh,
        in_specs=(P("depth", None, "stripe", None), P(), P("stripe", None, None), P(), P()),
        out_specs=P("depth", None, "stripe", None),
        check_vma=False,
    )
```

time: 341 us -> 222 us (0.65)
  waiting for transfers between devices: 193 us -> 136 us
  blocking collectives: 62.6 us -> 13 us
  Pallas kernels: 51.7 us -> 31.5 us
  starting transfers between devices: 12.7 us -> 27.5 us
  local copies, waits for them, and re-layouts: 16 us -> 9.53 us
    ppermute x10 -> x14, waiting for transfers between devices: 193 us -> 117 us  [the longest x6 89.5 us: hop(): lax.ppermute(value, 'depth', [(device(source, z, 0), device(target, z, 0)...]
    all_to_all x2 -> x1, blocking collectives: 62.6 us -> 13 us  [exchange(): lax.all_to_all(value, 'depth', 0, 0, axis_index_groups=rings, tiled=True)]
    pallas_call x9 -> x10, Pallas kernels: 48.9 us -> 26.7 us  [the longest x3 11.3 us: backward_stage(): pl.pallas_call(backward_kernel, in_specs=[smem, vmem] + [hbm] * 4 + [vmem...]
    all_to_all x0 -> x3, waiting for transfers between devices: none -> 18.8 us  [exchange(): lax.all_to_all(value, 'depth', 0, 0, axis_index_groups=rings, tiled=True)]
    all_to_all x0 -> x3, starting transfers between devices: none -> 12.3 us  [exchange(): lax.all_to_all(value, 'depth', 0, 0, axis_index_groups=rings, tiled=True)]
    unnamed x31 -> x19, local copies, waits for them, and re-layouts: 14.1 us -> 5.48 us
    ppermute x10 -> x14, starting transfers between devices: 12.7 us -> 15.2 us  [the longest x6 5.44 us: hop(): lax.ppermute(value, 'depth', [(device(source, z, 0), device(target, z, 0)...]
  transfers between devices with their start and end apart: 10 -> 17, of which waited for: 6 -> 11; matrix products, arithmetic and copies ran while one was open for 0% -> 1% of each run, Pallas kernels for 0% -> 3%
where the time goes in v2:
time: 222 us; the launch traced here: 219 us
  waiting for transfers between devices  136 us (61%)
  Pallas kernels  31.5 us (14%)
  starting transfers between devices  27.5 us (12%)
  blocking collectives  13 us (6%)
  local copies, waits for them, and re-layouts  9.53 us (4%)
    ppermute x6, waiting for transfers between devices, hop(): lax.ppermute(value, 'depth', [(device(source, z, 0), device(target, z, 0)...  89.5 us
    all_to_all x3, waiting for transfers between devices, exchange(): lax.all_to_all(value, 'depth', 0, 0, axis_index_groups=rings, tiled=True)  18.8 us
    all_to_all x1, blocking collectives, exchange(): lax.all_to_all(value, 'depth', 0, 0, axis_index_groups=rings, tiled=True)  13 us
    all_to_all x3, starting transfers between devices, exchange(): lax.all_to_all(value, 'depth', 0, 0, axis_index_groups=rings, tiled=True)  12.3 us
    pallas_call x3, Pallas kernels, backward_stage(): pl.pallas_call(backward_kernel, in_specs=[smem, vmem] + [hbm] * 4 + [vmem...  11.3 us
    pallas_call x3, Pallas kernels, forward_stage(): pl.pallas_call(lambda *refs: forward_kernel(first, *refs), in_specs=[smem...  10.8 us
    ppermute x1, waiting for transfers between devices, body(): after_im = lax.ppermute(own_im, 'stripe', back)  10 us
    ppermute x1, waiting for transfers between devices, body(): after_re = lax.ppermute(own_re, 'stripe', back)  9.56 us
  transfers between devices with their start and end apart: 17, of which 11 were waited for; matrix products, arithmetic and copies ran while one was open for 1% of the time, Pallas kernels for 3%

profile of v2, /device:TPU:16, one launch (start us, length us, event | category | flops | bytes accessed | tf_op | source)
XLA Modules:
  0.0 219.2 jit_solution(3238916518738703172)
XLA Ops:
  0.0 0.0 copy-start
  0.0 1.2 slice_bitcast_fusion.2
  1.2 0.5 collective-permute-start
  1.7 0.7 constant_dynamic-slice_fusion
  2.5 0.1 copy.15.place
  2.6 9.6 %collective-permute-done.after = f32[256,384]{1,0:T(8,128)S(1)} collective-permute-done((f32[256,384]{1,0:T(8,128)S(1)}, f32[256,384]{1,0:T(8,128)S(1)}, u32[]{:S(2)}, u32[]{:S(2)}) %collective-permute-start) | collective-permute-done | bytes 393248 | tf_op jit(solution)/shard_map/ppermute | solution.py:575
  12.2 2.3 %cut_windows.2 = f32[4,256,256]{2,1,0:T(8,128)} custom-call(s32[4,2]{1,0:T(4,128)S(1)} %copy.15.place, f32[256,384]{1,0:T(8,128)S(1)} %get-tuple-element.44.own, f32[256,384]{1,0:T(8,128)S(1)} %collective-permute-done.after), custom_call_target="tpu_custom_call" | custom-call | tf_op jit(solution)/shard_map/cut_windows/pallas_call | solution.py:478
  14.4 5.3 %all-to-all-start = ((f32[4,256,256]{2,1,0:T(8,128)}), f32[4,256,256]{2,1,0:T(8,128)S(1)}, u32[]{:S(2)}, u32[]{:S(2)}) async-start(f32[4,256,256]{2,1,0:T(8,128)} %cut_windows.2), calls=%async_computation | async-start | bytes 2097152 | tf_op jit(solution)/shard_map/all_to_all | solution.py:547
  19.7 0.4 collective-permute-start.1
  20.2 10.0 %collective-permute-done.1.after = f32[256,384]{1,0:T(8,128)S(1)} collective-permute-done((f32[256,384]{1,0:T(8,128)S(1)}, f32[256,384]{1,0:T(8,128)S(1)}, u32[]{:S(2)}, u32[]{:S(2)}) %collective-permute-start.1) | collective-permute-done | bytes 393248 | tf_op jit(solution)/shard_map/ppermute | solution.py:576
  30.2 1.3 cut_windows.3
  31.5 0.0 copy-start.3
  31.5 1.0 copy-done.3
  32.4 1.5 all-to-all-done.refs_2_.er
  33.9 3.5 %all-to-all-start.1 = ((f32[4,256,256]{2,1,0:T(8,128)}), f32[4,256,256]{2,1,0:T(8,128)S(1)}, u32[]{:S(2)}, u32[]{:S(2)}) async-start(f32[4,256,256]{2,1,0:T(8,128)} %copy-done.3), calls=%async_computation.1 | async-start | bytes 2097152 | tf_op jit(solution)/shard_map/all_to_all | solution.py:547
  37.5 1.3 collective-permute-start.2
  38.8 12.0 %all-to-all-done.1.refs_3_.ei = f32[4,256,256]{2,1,0:T(8,128)S(1)} async-done(((f32[4,256,256]{2,1,0:T(8,128)}), f32[4,256,256]{2,1,0:T(8,128)S(1)}, u32[]{:S(2)}, u32[]{:S(2)}) %all-to-all-start.1) | async-done | bytes 1048608 | tf_op jit(solution)/shard_map/all_to_all | solution.py:547
  50.7 1.3 collective-permute-start.3
  52.1 0.0 copy-done.8
  52.1 0.6 dynamic_slice.11.live
  53.3 0.0 collective-permute-done.2.refs_4_.orr
  53.3 2.1 collective-permute-done.3.refs_5_.oi
  55.4 0.0 copy-done.2
  55.4 0.9 copy-done.5
  56.4 9.2 %forward_stage.3 = (s16[2,272,256]{2,1,0:T(8,128)(2,1)}, f32[8,2,256,256]{3,2,1,0:T(8,128)}) custom-call(s32[1]{0:T(128)} %bitcast.1.refs_0_.flag, bf16[2,256,256]{2,1,0:T(8,128)(2,1)S(1)} %copy-done.5, f32[4,256,256]{2,1,0:T(8,128)S(1)} %all-to-all-done.refs_2_.er, f32[4,256,256]{2,1,0:T(8,128)S(1)} %all-to-all-done.1.refs_3_.ei, ...), custom_call_target="tpu_custom_call" | custom-call | tf_op jit(solution)/shard_map/forward_stage/pallas_call | solution.py:420
  65.6 1.3 collective-permute-start.4
  66.9 4.3 %collective-permute-done.4.refs_1_ = s16[2,272,256]{2,1,0:T(8,128)(2,1)S(1)} collective-permute-done((s16[2,272,256]{2,1,0:T(8,128)(2,1)}, s16[2,272,256]{2,1,0:T(8,128)(2,1)S(1)}, u32[]{:S(2)}, u32[]{:S(2)}) %collective-permute-start.4) | collective-permute-done | bytes 278560 | tf_op jit(solution)/shard_map/ppermute | solution.py:556
  71.3 0.8 forward_stage.4
  72.0 0.7 collective-permute-start.5
  72.7 0.0 collective-permute-done.5.refs_1_
  72.7 0.8 forward_stage.5
  73.5 0.7 collective-permute-start.6
  74.2 0.0 copy-done
  74.3 0.0 collective-permute-done.6.wave_in
  74.3 0.0 copy-start.4
  74.3 1.2 copy-done.4
  75.5 0.9 copy-done.6
  76.5 0.1 turn_stage.1
  76.5 0.8 collective-permute-start.7
  77.4 0.0 collective-permute-done.7.adj_in
  77.4 1.3 copy-done.1
  78.6 0.1 backward_stage.3
  78.7 0.7 collective-permute-start.8
  79.4 0.0 collective-permute-done.8.adj_in
  79.4 0.1 backward_stage.4
  79.5 1.3 collective-permute-start.9
  80.8 85.2 %collective-permute-done.9.adj_in = s16[2,272,256]{2,1,0:T(8,128)(2,1)S(1)} collective-permute-done((s16[2,272,256]{2,1,0:T(8,128)(2,1)S(1)}, s16[2,272,256]{2,1,0:T(8,128)(2,1)S(1)}, u32[]{:S(2)}, u32[]{:S(2)}) %collective-permute-start.9) | collective-permute-done | bytes 278560 | tf_op jit(solution)/shard_map/ppermute | solution.py:556
  166.0 11.1 %backward_stage.5 = (s16[2,272,256]{2,1,0:T(8,128)(2,1)}, s16[2,2,4,272,256]{4,3,2,1,0:T(8,128)(2,1)}) custom-call(s32[1]{0:T(128)} %bitcast.1.refs_0_.flag, s16[2,272,256]{2,1,0:T(8,128)(2,1)S(1)} %collective-permute-done.9.adj_in, f32[4,256,256]{2,1,0:T(8,128)S(1)} %all-to-all-done.refs_2_.er, ...), custom_call_target="tpu_custom_call", output_to_operand_aliasing={{1}: (8, {})} | custom-call | tf_op jit(solution)/shard_map/backward_stage/pallas_call | solution.py:449
  177.2 1.4 slice_bitcast_fusion
  178.6 1.3 collective-permute-start.12
  180.0 1.3 collective-permute-start.10
  181.3 0.2 collective-permute-done.12
  181.5 1.3 collective-permute-done.10
  182.8 1.1 bitcast_select_fusion
  183.9 13.0 %all_to_all.20.grads = s16[4,272,256]{2,1,0:T(8,128)(2,1)S(1)} all-to-all(s16[4,272,256]{2,1,0:T(8,128)(2,1)S(1)} %get-tuple-element.39), channel_id=1, replica_groups={{0,8,16,24},{4,12,20,28},{32,40,48,56},{36,44,52,60},{64,72,80,88},{68,..., dimensions={0} | all-to-all | bytes 1114112 | tf_op jit(solution)/shard_map/all_to_all | solution.py:547
  197.0 3.5 %all-to-all-start.2 = ((s16[4,272,256]{2,1,0:T(8,128)(2,1)}), s16[4,272,256]{2,1,0:T(8,128)(2,1)S(1)}, u32[]{:S(2)}, u32[]{:S(2)}) async-start(s16[4,272,256]{2,1,0:T(8,128)(2,1)} %get-tuple-element.40), calls=%async_computation.2 | async-start | bytes 1114112 | tf_op jit(solution)/shard_map/all_to_all | solution.py:547
  200.4 2.4 %add_windows.3 = (f32[256,384]{1,0:T(8,128)S(1)}, s16[272,384]{1,0:T(8,128)(2,1)S(1)}) custom-call(s32[4,2]{1,0:T(4,128)S(1)} %copy.15.place, s32[1]{0:T(128)} %dynamic_slice.11.live, s16[4,272,256]{2,1,0:T(8,128)(2,1)S(1)} %all_to_all.20.grads), custom_call_target="tpu_custom_call" | custom-call | tf_op jit(solution)/shard_map/add_windows/pallas_call | solution.py:506
  202.8 1.8 collective-permute-start.13
  204.6 5.3 %all-to-all-done.2.grads = s16[4,272,256]{2,1,0:T(8,128)(2,1)S(1)} async-done(((s16[4,272,256]{2,1,0:T(8,128)(2,1)}), s16[4,272,256]{2,1,0:T(8,128)(2,1)S(1)}, u32[]{:S(2)}, u32[]{:S(2)}) %all-to-all-start.2) | async-done | bytes 557088 | tf_op jit(solution)/shard_map/all_to_all | solution.py:547
  209.9 2.4 %add_windows.2 = (f32[256,384]{1,0:T(8,128)S(1)}, s16[272,384]{1,0:T(8,128)(2,1)S(1)}) custom-call(s32[4,2]{1,0:T(4,128)S(1)} %copy.15.place, s32[1]{0:T(128)} %dynamic_slice.11.live, s16[4,272,256]{2,1,0:T(8,128)(2,1)S(1)} %all-to-all-done.2.grads), custom_call_target="tpu_custom_call" | custom-call | tf_op jit(solution)/shard_map/add_windows/pallas_call | solution.py:506
  212.3 1.8 collective-permute-start.11
  214.1 0.0 collective-permute-done.13.low_im
  214.1 4.1 %collective-permute-done.11.low_re = s16[272,384]{1,0:T(8,128)(2,1)S(1)} collective-permute-done((s16[272,384]{1,0:T(8,128)(2,1)S(1)}, s16[272,384]{1,0:T(8,128)(2,1)S(1)}, u32[]{:S(2)}, u32[]{:S(2)}) %collective-permute-start.11) | collective-permute-done | bytes 208928 | tf_op jit(solution)/shard_map/ppermute | solution.py:597
  218.2 1.0 join.1
  (8 shorter events, 0.0 us)
Async XLA Ops:
  0.0 74.2 %copy-start = (bf16[4,256,256]{2,1,0:T(8,128)(2,1)S(1)}, bf16[4,256,256]{2,1,0:T(8,128)(2,1)}, u32[]{:S(2)}) copy-start(bf16[4,256,256]{2,1,0:T(8,128)(2,1)} %param.10) | copy-start | bytes 1572868
  1.2 10.9 %collective-permute-start = (f32[256,384]{1,0:T(8,128)S(1)}, f32[256,384]{1,0:T(8,128)S(1)}, u32[]{:S(2)}, u32[]{:S(2)}) collective-permute-start(f32[256,384]{1,0:T(8,128)S(1)} %get-tuple-element.44.own), channel_id=1, source_target_pairs={{0,3},{1,0},{2,1},{3,2},{4,7},{5,4},{6,5},{7,6},{8,11},{9,8},{10,9... | collective-permute-start | bytes 1179656 | tf_op jit(solution)/shard_map/ppermute | solution.py:575
  14.4 19.5 %all-to-all-start = ((f32[4,256,256]{2,1,0:T(8,128)}), f32[4,256,256]{2,1,0:T(8,128)S(1)}, u32[]{:S(2)}, u32[]{:S(2)}) async-start(f32[4,256,256]{2,1,0:T(8,128)} %cut_windows.2), calls=%async_computation | async-start | bytes 2097152 | tf_op jit(solution)/shard_map/all_to_all | solution.py:547
  19.7 32.4 %copy-start.8 = (s32[4]{0:T(128)S(1)}, s32[4]{0:T(128)}, u32[]{:S(2)}) copy-start(s32[4]{0:T(128)} %param.12) | copy-start | bytes 52
  19.7 35.7 %copy-start.2 = (bf16[4,256,256]{2,1,0:T(8,128)(2,1)S(1)}, bf16[4,256,256]{2,1,0:T(8,128)(2,1)}, u32[]{:S(2)}) copy-start(bf16[4,256,256]{2,1,0:T(8,128)(2,1)} %constant.70.clone.refs_6_.chirp) | copy-start | bytes 1572868
  19.7 10.4 %collective-permute-start.1 = (f32[256,384]{1,0:T(8,128)S(1)}, f32[256,384]{1,0:T(8,128)S(1)}, u32[]{:S(2)}, u32[]{:S(2)}) collective-permute-start(f32[256,384]{1,0:T(8,128)S(1)} %get-tuple-element.43.own), channel_id=1, source_target_pairs={{0,3},{1,0},{2,1},{3,2},{4,7},{5,4},{6,5},{7,6},{8,11},{9,8},{10,9... | collective-permute-start | bytes 1179656 | tf_op jit(solution)/shard_map/ppermute | solution.py:576
  31.5 1.0 copy-start.3
  33.9 16.8 %all-to-all-start.1 = ((f32[4,256,256]{2,1,0:T(8,128)}), f32[4,256,256]{2,1,0:T(8,128)S(1)}, u32[]{:S(2)}, u32[]{:S(2)}) async-start(f32[4,256,256]{2,1,0:T(8,128)} %copy-done.3), calls=%async_computation.1 | async-start | bytes 2097152 | tf_op jit(solution)/shard_map/all_to_all | solution.py:547
  37.5 15.9 %collective-permute-start.2 = (f32[4,256,256]{2,1,0:T(8,128)S(1)}, f32[4,256,256]{2,1,0:T(8,128)}, u32[]{:S(2)}, u32[]{:S(2)}) collective-permute-start(f32[4,256,256]{2,1,0:T(8,128)S(1)} %all-to-all-done.refs_2_.er), channel_id=1, source_target_pairs={{4,0},{12,8},{20,16},{28,24},{36,32},{44,40},{52,48},{60,56},{68,6... | collective-permute-start | bytes 3145736 | tf_op jit(solution)/shard_map/ppermute | solution.py:552
  50.7 4.7 %collective-permute-start.3 = (f32[4,256,256]{2,1,0:T(8,128)S(1)}, f32[4,256,256]{2,1,0:T(8,128)}, u32[]{:S(2)}, u32[]{:S(2)}) collective-permute-start(f32[4,256,256]{2,1,0:T(8,128)S(1)} %all-to-all-done.1.refs_3_.ei), channel_id=1, source_target_pairs={{4,0},{12,8},{20,16},{28,24},{36,32},{44,40},{52,48},{60,56},{68,6... | collective-permute-start | bytes 3145736 | tf_op jit(solution)/shard_map/ppermute | solution.py:552
  55.4 1.0 copy-start.5
  65.6 5.7 %collective-permute-start.4 = (s16[2,272,256]{2,1,0:T(8,128)(2,1)}, s16[2,272,256]{2,1,0:T(8,128)(2,1)S(1)}, u32[]{:S(2)}, u32[]{:S(2)}) collective-permute-start(s16[2,272,256]{2,1,0:T(8,128)(2,1)} %get-tuple-element.22), channel_id=1, source_target_pairs={{0,32},{8,40},{16,48},{24,56},{1,33},{9,41},{17,49},{25,57},{2,34}... | collective-permute-start | bytes 835592 | tf_op jit(solution)/shard_map/ppermute | solution.py:556
  72.0 0.7 collective-permute-start.5
  73.5 0.7 collective-permute-start.6
  74.3 1.2 copy-start.4
  75.5 0.9 copy-start.6
  76.5 2.2 copy-start.1
  76.5 0.8 collective-permute-start.7
  78.7 0.7 collective-permute-start.8
  79.5 86.5 %collective-permute-start.9 = (s16[2,272,256]{2,1,0:T(8,128)(2,1)S(1)}, s16[2,272,256]{2,1,0:T(8,128)(2,1)S(1)}, u32[]{:S(2)}, u32[]{:S(2)}) collective-permute-start(s16[2,272,256]{2,1,0:T(8,128)(2,1)S(1)} %get-tuple-element.32), channel_id=1, source_target_pairs={{32,0},{40,8},{48,16},{56,24},{33,1},{41,9},{49,17},{57,25},{34,2}... | collective-permute-start | bytes 835592 | tf_op jit(solution)/shard_map/ppermute | solution.py:556
  177.2 5.7 %copy-start.7 = (s16[2,2,4,272,256]{4,3,2,1,0:T(8,128)(2,1)S(1)}, s16[2,2,4,272,256]{4,3,2,1,0:T(8,128)(2,1)}, u32[]{:S(2)}) copy-start(s16[2,2,4,272,256]{4,3,2,1,0:T(8,128)(2,1)} %get-tuple-element.34) | copy-start | bytes 6684676
  178.6 2.9 %collective-permute-start.12 = (s16[4,272,256]{2,1,0:T(8,128)(2,1)S(1)}, s16[4,272,256]{2,1,0:T(8,128)(2,1)S(1)}, u32[]{:S(2)}, u32[]{:S(2)}) collective-permute-start(s16[4,272,256]{2,1,0:T(8,128)(2,1)S(1)} %get-tuple-element.41), channel_id=1, source_target_pairs={{0,4},{8,12},{16,20},{24,28},{32,36},{40,44},{48,52},{56,60},{64,6... | collective-permute-start | bytes 1671176 | tf_op jit(solution)/shard_map/ppermute | solution.py:552
  180.0 2.9 %collective-permute-start.10 = (s16[4,272,256]{2,1,0:T(8,128)(2,1)S(1)}, s16[4,272,256]{2,1,0:T(8,128)(2,1)S(1)}, u32[]{:S(2)}, u32[]{:S(2)}) collective-permute-start(s16[4,272,256]{2,1,0:T(8,128)(2,1)S(1)} %get-tuple-element.42), channel_id=1, source_target_pairs={{0,4},{8,12},{16,20},{24,28},{32,36},{40,44},{48,52},{56,60},{64,6... | collective-permute-start | bytes 1671176 | tf_op jit(solution)/shard_map/ppermute | solution.py:552
  197.0 13.0 %all-to-all-start.2 = ((s16[4,272,256]{2,1,0:T(8,128)(2,1)}), s16[4,272,256]{2,1,0:T(8,128)(2,1)S(1)}, u32[]{:S(2)}, u32[]{:S(2)}) async-start(s16[4,272,256]{2,1,0:T(8,128)(2,1)} %get-tuple-element.40), calls=%async_computation.2 | async-start | bytes 1114112 | tf_op jit(solution)/shard_map/all_to_all | solution.py:547
  202.8 11.3 %collective-permute-start.13 = (s16[272,384]{1,0:T(8,128)(2,1)S(1)}, s16[272,384]{1,0:T(8,128)(2,1)S(1)}, u32[]{:S(2)}, u32[]{:S(2)}) collective-permute-start(s16[272,384]{1,0:T(8,128)(2,1)S(1)} %get-tuple-element.38), channel_id=1, source_target_pairs={{0,1},{1,2},{2,3},{3,0},{4,5},{5,6},{6,7},{7,4},{8,9},{9,10},{10,1... | collective-permute-start | bytes 626696 | tf_op jit(solution)/shard_map/ppermute | solution.py:597
  212.3 5.9 %collective-permute-start.11 = (s16[272,384]{1,0:T(8,128)(2,1)S(1)}, s16[272,384]{1,0:T(8,128)(2,1)S(1)}, u32[]{:S(2)}, u32[]{:S(2)}) collective-permute-start(s16[272,384]{1,0:T(8,128)(2,1)S(1)} %get-tuple-element.36), channel_id=1, source_target_pairs={{0,1},{1,2},{2,3},{3,0},{4,5},{5,6},{6,7},{7,4},{8,9},{9,10},{10,1... | collective-permute-start | bytes 626696 | tf_op jit(solution)/shard_map/ppermute | solution.py:597

commit v3 on v2

v3 whole, which is shorter than its diff:
```python
import numpy as np

import jax
import jax.numpy as jnp
from jax import lax
from jax.experimental import pallas as pl
from jax.experimental.pallas import tpu as pltpu
from jax.sharding import PartitionSpec as P

WIN = 256
HALF = 128
ROWS = 256
COLS = 384
CAP = 4
GROUP = 8
STAGES = 4
CHUNK = 128
smoothing = 0.25
f32 = jnp.float32
bf16 = jnp.bfloat16


def split_np(table):
    high = table.astype(bf16)
    low = (table - high.astype(np.float64)).astype(bf16)
    return high, low


def make_tables():
    n = np.arange(HALF)[:, None]
    k = np.arange(HALF)[None, :]
    tables = []
    for parity in (0, 1):
        angle = -2.0 * np.pi * ((n * (2 * k + parity)) % WIN) / WIN
        c, s = np.cos(angle) / 16.0, np.sin(angle) / 16.0
        full = np.block([[c, s], [-s, c]])
        for table in (full, full.T):
            tables.extend(split_np(table))
    dft = np.stack(tables)
    freq = (((np.arange(WIN) + HALF) % WIN) - HALF).astype(np.float64)
    response = np.fft.ifft(np.exp(-1j * np.pi * freq**2 / (2.0 * WIN)))
    near = response[(n - k) % WIN]
    far = response[(n - k - HALF) % WIN]
    tables = []
    for block in ((near + far) / 2.0, (near - far) / 2.0):
        tables.extend(split_np(np.block([[block.real, block.imag], [-block.imag, block.real]])))
    chirp = np.stack(tables)
    order = np.concatenate([np.arange(0, WIN, 2), np.arange(1, WIN, 2)])
    pick = np.zeros((WIN, WIN))
    pick[np.arange(WIN), order] = 1.0
    return dft, chirp, np.stack([pick, pick.T]).astype(bf16)


SUM, DIFF = 0, 2
EVEN, EVEN_T, ODD, ODD_T = 0, 2, 4, 6


def halves(value):
    high = value.astype(bf16)
    low = (value - high.astype(f32)).astype(bf16)
    return high, low


def mm(a, b):
    return jnp.dot(a, b, preferred_element_type=f32)


def right_mul(data, dft, which):
    high, low = halves(data)
    return mm(high, dft[which]) + mm(low, dft[which]) + mm(high, dft[which + 1])


def left_mul(dft, which, data):
    high, low = halves(data)
    return mm(dft[which], high) + mm(dft[which], low) + mm(dft[which + 1], high)


def lanes(a, b):
    return jnp.concatenate([a, b], axis=1)


def rows(a, b):
    return jnp.concatenate([a, b], axis=0)


def propagate(source, sink, chirp):
    top, low = slice(0, HALF), slice(HALF, WIN)
    re_top, im_top = source(top)
    re_low, im_low = source(low)

    sr, si, dr, di = re_top + re_low, im_top + im_low, re_top - re_low, im_top - im_low
    re, im = rows(sr, dr), rows(si, di)
    scol = right_mul(lanes(re[:, :HALF] + re[:, HALF:], im[:, :HALF] + im[:, HALF:]), chirp, SUM)
    dcol = right_mul(lanes(re[:, :HALF] - re[:, HALF:], im[:, :HALF] - im[:, HALF:]), chirp, DIFF)
    im, re = lanes(scol[:, HALF:], dcol[:, HALF:]), lanes(scol[:, :HALF], dcol[:, :HALF])
    total = left_mul(chirp, SUM, rows(im[:HALF], re[:HALF]))
    diff = left_mul(chirp, DIFF, rows(im[HALF:], re[HALF:]))
    for part, both in ((top, total + diff), (low, total - diff)):
        im, re = both[:HALF], both[HALF:]
        sink(
            part,
            lanes(re[:, :HALF] + re[:, HALF:], re[:, :HALF] - re[:, HALF:]),
            lanes(im[:, :HALF] + im[:, HALF:], im[:, :HALF] - im[:, HALF:]),
        )


def exit_wave(source, sink, dft, mid, pointwise):
    for start in range(0, WIN, CHUNK):
        part = slice(start, start + CHUNK)
        re, im = source(part)
        even = lanes(re[:, :HALF] + re[:, HALF:], im[:, :HALF] + im[:, HALF:])
        odd = lanes(re[:, :HALF] - re[:, HALF:], im[:, :HALF] - im[:, HALF:])
        even = right_mul(even, dft, EVEN)
        odd = right_mul(odd, dft, ODD)
        mid[0, part, :] = lanes(even[:, :HALF], odd[:, :HALF])
        mid[1, part, :] = lanes(even[:, HALF:], odd[:, HALF:])
    re_top, re_low = mid[0, :HALF, :], mid[0, HALF:, :]
    im_top, im_low = mid[1, :HALF, :], mid[1, HALF:, :]
    even = left_mul(dft, EVEN_T, rows(re_top + re_low, im_top + im_low))
    odd = left_mul(dft, ODD_T, rows(re_top - re_low, im_top - im_low))
    even = pointwise(slice(0, HALF), even[:HALF], even[HALF:])
    odd = pointwise(slice(HALF, WIN), odd[:HALF], odd[HALF:])
    even = left_mul(dft, EVEN, rows(*even))
    odd = left_mul(dft, ODD, rows(*odd))
    mid[0, :HALF, :] = even[:HALF] + odd[:HALF]
    mid[0, HALF:, :] = even[:HALF] - odd[:HALF]
    mid[1, :HALF, :] = even[HALF:] + odd[HALF:]
    mid[1, HALF:, :] = even[HALF:] - odd[HALF:]
    for start in range(0, WIN, CHUNK):
        part = slice(start, start + CHUNK)
        re, im = mid[0, part, :], mid[1, part, :]
        even = right_mul(lanes(re[:, :HALF], im[:, :HALF]), dft, EVEN_T)
        odd = right_mul(lanes(re[:, HALF:], im[:, HALF:]), dft, ODD_T)
        total, diff = even + odd, even - odd
        sink(part, lanes(total[:, :HALF], diff[:, :HALF]), lanes(total[:, HALF:], diff[:, HALF:]))


CODED = WIN + 16
i16 = jnp.int16


def exponent(most):
    return jnp.ceil(jnp.log2(jnp.maximum(most, 1e-30)))


def encode(dst, part, value):
    exp = exponent(jnp.max(jnp.abs(value), axis=0, keepdims=True))
    scaled = jnp.round(value * (jnp.exp2(-exp) * 32767.0))
    dst[part, :] = scaled.astype(jnp.int32).astype(i16)
    return jnp.broadcast_to(exp, (8, value.shape[1])).astype(jnp.int32)


def encode_tail(dst, top, low):
    dst[WIN:, :] = jnp.concatenate([top, low], axis=0).astype(i16)


def decode(src, part):
    tail = src[WIN:, :].astype(jnp.int32)[8 * (part.start // HALF):][:1].astype(f32)
    return src[part, :].astype(jnp.int32).astype(f32) * (jnp.exp2(tail) * (1.0 / 32767.0))


TOP, LOW = slice(0, HALF), slice(HALF, WIN)


def encode_plane(dst, top, low):
    encode_tail(dst, encode(dst, TOP, top), encode(dst, LOW, low))


def decode_wave(dst, src):
    for comp in range(2):
        for part in (TOP, LOW):
            dst[comp, part, :] = decode(src.at[comp], part)


def encode_wave(dst, src):
    for comp in range(2):
        encode_plane(dst.at[comp], src[comp, TOP, :], src[comp, LOW, :])


def times(re, im, win, part):
    tr, ti = win[0, part, :], win[1, part, :]
    return re * tr - im * ti, re * ti + im * tr


class Ahead:
    def __init__(self, arrays, buf, sem, depth):
        self.arrays, self.buf, self.sem, self.depth = arrays, buf, sem, depth

    def copy(self, i):
        slot = i & (self.depth - 1)
        return pltpu.make_async_copy(self.arrays.at[i], self.buf.at[slot], self.sem.at[slot])

    def start(self, i):
        self.copy(i).start()

    def wait(self, i):
        self.copy(i).wait()

    def at(self, i):
        return self.buf.at[i & (self.depth - 1)]


class Fetch:
    def __init__(self, pairs, sem):
        self.copies = [pltpu.make_async_copy(src, dst, sem.at[i]) for i, (src, dst) in enumerate(pairs)]

    def start(self):
        for copy in self.copies:
            copy.start()

    def wait(self):
        for copy in self.copies:
            copy.wait()


def forward_slice(src, dst, windows, i, chirp):
    def source(part):
        return times(src[0, part, :], src[1, part, :], windows.at(i), part)

    def sink(part, re, im):
        dst[0, part, :] = re
        dst[1, part, :] = im

    propagate(source, sink, chirp)


def retreat(i, part, re, im, adj, wave, windows, grad, tails):
    wr, wi = wave[0, part, :], wave[1, part, :]
    half = part.start // HALF
    for comp, value in enumerate((wr * re - wi * im, -(wr * im + wi * re))):
        tails[comp, 8 * half:8 * half + 8, :] = encode(grad.at[comp], part, value)
    adj[0, part, :], adj[1, part, :] = times(re, im, windows.at(i), part)


def finish_grad(grad, tails):
    for comp in range(2):
        grad[comp, WIN:, :] = tails[comp].astype(i16)


def backward_slice(i, adj, wave, windows, chirp, grad, tails):
    def source(part):
        return adj[0, part, :], adj[1, part, :]

    def sink(part, re, im):
        retreat(i, part, re, im, adj, wave, windows, grad, tails)

    propagate(source, sink, chirp)
    finish_grad(grad, tails)


def copy_wave(dst, src):
    for comp in range(2):
        dst[comp] = src[comp].astype(f32)


def forward_kernel(first, flag, coded, wins, chirp, *rest):
    wave_out, waves, win_buf, win_sem, buf, sem = rest[-6:]
    windows = Ahead(wins, win_buf, win_sem, win_buf.shape[0])

    def store(i):
        slot = lax.rem(i, 3)
        return pltpu.make_async_copy(buf.at[slot], waves.at[i], sem.at[slot])

    @pl.when(flag[0] >= 4)
    def _():
        for i in range(DEPTH - 1):
            windows.start(jnp.int32(i))
        if first:
            copy_wave(buf.at[0], coded)
        else:
            decode_wave(buf.at[0], coded)

        @pl.loop(0, GROUP)
        def _(i):
            @pl.when(i + DEPTH - 1 < GROUP)
            def _():
                windows.start(i + DEPTH - 1)

            store(i).start()

            @pl.when(i >= 2)
            def _():
                store(i - 2).wait()

            windows.wait(i)
            forward_slice(buf.at[lax.rem(i, 3)], buf.at[lax.rem(i + 1, 3)], windows, i, chirp)

        encode_wave(wave_out, buf.at[GROUP % 3])
        store(jnp.int32(GROUP - 2)).wait()
        store(jnp.int32(GROUP - 1)).wait()


class Gradients:
    def __init__(self, grads, buf, sem):
        self.grads, self.buf, self.sem = grads, buf, sem

    def copy(self, i, odd):
        return pltpu.make_async_copy(self.buf.at[odd], self.grads[odd].at[i >> 1], self.sem.at[odd])

    def start(self, i):
        for odd in range(2):
            @pl.when((i & 1) == odd)
            def _():
                self.copy(i, odd).start()

    def wait(self, i):
        for odd in range(2):
            @pl.when((i & 1) == odd)
            def _():
                self.copy(i, odd).wait()


def turn_kernel(flag, coded, wins, chirp, dft_in, patterns, pick_in, adj_out, *rest):
    *grads, win_buf, win_sem, grad_buf, grad_sem, adj, tails = rest[:8]
    waves, mid, far_amp, dft, pattern, pick, late_sem = rest[8:]
    windows = Ahead(wins, win_buf, win_sem, win_buf.shape[0])
    out = Gradients(grads, grad_buf, grad_sem)
    end = GROUP - 1

    @pl.when(flag[0] >= 4)
    def _():
        for i in range(GROUP):
            windows.start(jnp.int32(i))
        late = Fetch([(dft_in, dft), (patterns.at[flag[0] & 3], pattern), (pick_in, pick)], late_sem)
        late.start()
        decode_wave(waves.at[0], coded)

        @pl.loop(0, end)
        def _(i):
            windows.wait(i)
            forward_slice(waves.at[i], waves.at[i + 1], windows, i, chirp)

        windows.wait(jnp.int32(end))
        late.wait()
        picked = mm(pick[0], pattern[...]).astype(bf16)
        far_amp[...] = mm(picked, pick[1])

        def source(part):
            return times(waves[end, 0, part, :], waves[end, 1, part, :], win_buf.at[end], part)

        def exit_point(part, re, im):
            smooth = jnp.sqrt(re * re + im * im + smoothing)
            factor = 1.0 - far_amp[part, :] / smooth
            return factor * re, factor * im

        def sink(part, re, im):
            retreat(end, part, re, -im, adj, waves.at[end], windows, grad_buf.at[end & 1], tails)

        exit_wave(source, sink, dft, mid, exit_point)
        finish_grad(grad_buf.at[end & 1], tails)
        out.start(jnp.int32(end))

        @pl.loop(0, end)
        def _(step):
            i = end - 1 - step

            @pl.when(step > 0)
            def _():
                out.wait(i + 2)

            backward_slice(i, adj, waves.at[i], windows, chirp, grad_buf.at[i & 1], tails)
            out.start(i)

        encode_wave(adj_out, adj)
        out.wait(jnp.int32(1))
        out.wait(jnp.int32(0))


def backward_kernel(final, flag, coded, wins, chirp, waves, *rest):
    rest = rest[2:]
    if not final:
        adj_out, rest = rest[0], rest[1:]
    *grads, win_buf, win_sem, grad_buf, grad_sem, adj, tails = rest[:8]
    wave_buf, wave_sem = rest[8:]
    windows = Ahead(wins, win_buf, win_sem, win_buf.shape[0])
    out = Gradients(grads, grad_buf, grad_sem)

    kept = Ahead(waves, wave_buf, wave_sem, wave_buf.shape[0])

    @pl.when(flag[0] >= 4)
    def _():
        for i in range(DEPTH - 1):
            windows.start(jnp.int32(GROUP - 1 - i))
            kept.start(jnp.int32(GROUP - 1 - i))
        decode_wave(adj, coded)

        @pl.loop(0, GROUP)
        def _(step):
            i = GROUP - 1 - step
            windows.wait(i)
            kept.wait(i)

            @pl.when(i >= DEPTH - 1)
            def _():
                windows.start(i - DEPTH + 1)
                kept.start(i - DEPTH + 1)

            @pl.when(step >= 2)
            def _():
                out.wait(i + 2)

            backward_slice(i, adj, kept.at(i), windows, chirp, grad_buf.at[i & 1], tails)
            out.start(i)

        if not final:
            encode_wave(adj_out, adj)
        out.wait(jnp.int32(1))
        out.wait(jnp.int32(0))


vmem = pl.BlockSpec(memory_space=pltpu.VMEM)
smem = pl.BlockSpec(memory_space=pltpu.SMEM)
hbm = pl.BlockSpec(memory_space=pltpu.HBM)
params = pltpu.CompilerParams(vmem_limit_bytes=24 * 2**20)
wave_shape = jax.ShapeDtypeStruct((2, CODED, WIN), i16)
waves_shape = pltpu.HBM((GROUP, 2, WIN, WIN), f32)
grads_shape = [pltpu.HBM((GROUP // 2, 2, CODED, WIN), i16)] * 2
dma = pltpu.SemaphoreType.DMA
DEPTH = 4
win_scratch = lambda depth: [pltpu.VMEM((depth, 2, WIN, WIN), f32), dma((depth,))]
grad_scratch = lambda: [
    pltpu.VMEM((2, 2, CODED, WIN), i16),
    dma((2,)),
    pltpu.VMEM((2, WIN, WIN), f32),
    pltpu.VMEM((2, 16, WIN), jnp.int32),
]


def in_hbm(value):
    return pltpu.with_memory_space_constraint(value, pltpu.HBM)


def forward_stage(flag, wave, wins, chirp, waves):
    first = waves is None
    args = [flag, wave, in_hbm(wins), chirp]
    args += [] if first else [in_hbm(waves)]
    return pl.pallas_call(
        lambda *refs: forward_kernel(first, *refs),
        in_specs=[smem, vmem, hbm, vmem] + [hbm] * (len(args) - 4),
        out_specs=[vmem, hbm],
        out_shape=[wave_shape, waves_shape],
        input_output_aliases={} if first else {4: 1},
        scratch_shapes=win_scratch(DEPTH) + [
            pltpu.VMEM((3, 2, WIN, WIN), f32),
            dma((3,)),
        ],
        compiler_params=params,
        name="forward_stage",
    )(*args)


def turn_stage(flag, wave, wins, chirp, dft, patterns, pick):
    return pl.pallas_call(
        turn_kernel,
        in_specs=[smem, vmem, hbm, vmem] + [hbm] * 3,
        out_specs=[vmem] + [hbm] * 2,
        out_shape=[wave_shape, *grads_shape],
        scratch_shapes=win_scratch(GROUP) + grad_scratch() + [
            pltpu.VMEM((GROUP, 2, WIN, WIN), f32),
            pltpu.VMEM((2, WIN, WIN), f32),
            pltpu.VMEM((WIN, WIN), f32),
            pltpu.VMEM((8, WIN, WIN), bf16),
            pltpu.VMEM((WIN, WIN), bf16),
            pltpu.VMEM((2, WIN, WIN), bf16),
            dma((3,)),
        ],
        compiler_params=params,
        name="turn_stage",
    )(flag, wave, in_hbm(wins), chirp, in_hbm(dft), in_hbm(patterns), in_hbm(pick))


def backward_stage(final, flag, adj, wins, chirp, waves, grads):
    lead = 0 if final else 1
    return pl.pallas_call(
        lambda *refs: backward_kernel(final, *refs),
        in_specs=[smem, vmem, hbm, vmem] + [hbm] * 3,
        out_specs=[vmem] * lead + [hbm] * 2,
        out_shape=[wave_shape] * lead + grads_shape,
        input_output_aliases={5 + k: lead + k for k in range(2)},
        scratch_shapes=win_scratch(DEPTH) + grad_scratch() + [
            pltpu.VMEM((DEPTH, 2, WIN, WIN), f32),
            dma((DEPTH,)),
        ],
        compiler_params=params,
        name="backward_stage",
    )(flag, adj, in_hbm(wins), chirp, in_hbm(waves), *[in_hbm(grad) for grad in grads])


FINE = 2.0**23


def pack_kernel(own, out):
    for start in range(0, ROWS, 64):
        part = slice(start, start + 64)
        words = [
            jnp.minimum(jnp.round(own[0, comp, part, :] * FINE).astype(jnp.int32), 2**23 - 1) for comp in range(2)
        ]
        both = ((words[0] & 255) << 8) + (words[1] & 255) - 2**15
        for plane, value in enumerate((both, words[0] >> 8, words[1] >> 8)):
            out[plane, part, :] = value.astype(i16)


def pack(own):
    return pl.pallas_call(
        pack_kernel,
        in_specs=[vmem],
        out_specs=vmem,
        out_shape=jax.ShapeDtypeStruct((3, ROWS, COLS), i16),
        compiler_params=params,
        name="pack",
    )(own)


def unpack_kernel(even, odd, out, buf, sem):
    copies = []
    for i in range(GROUP):
        array = (even, odd)[i % 2]
        for start in range(0, WIN, 64):
            part = slice(start, start + 64)
            both = array[i // 2, 0, part, :].astype(jnp.int32) + 2**15
            for comp, byte in enumerate((both >> 8, both & 255)):
                word = (array[i // 2, 1 + comp, part, :].astype(jnp.int32) << 8) + byte
                buf[i, comp, part, :] = word.astype(f32) * (1.0 / FINE)
        copies.append(pltpu.make_async_copy(buf.at[i], out.at[i], sem.at[i]))
        copies[-1].start()
    for copy in copies:
        copy.wait()


def unpack(even, odd):
    return pl.pallas_call(
        unpack_kernel,
        in_specs=[vmem] * 2,
        out_specs=hbm,
        out_shape=pltpu.HBM((GROUP, 2, WIN, WIN), f32),
        scratch_shapes=[pltpu.VMEM((GROUP, 2, WIN, WIN), f32), dma((GROUP,))],
        compiler_params=params,
        name="unpack",
    )(even, odd)


def corner(place, slot):
    row, col = place[slot, 0], place[slot, 1]
    base = pl.multiple_of((row >> 3) << 3, 8)
    return base, row - base, col


def cut_kernel(place, own, after, out, slab):
    for plane in range(3):
        slab[:ROWS, :] = own[plane].astype(jnp.int32)
        slab[ROWS:, :] = after[plane].astype(jnp.int32)
        for slot in range(CAP):
            base, shift, col = corner(place, slot)
            picked = slab[pl.ds(base, WIN + 8), :]
            picked = pltpu.roll(picked, lax.rem(COLS - col, COLS), 1)[:, :WIN]
            picked = pltpu.roll(picked, lax.rem(WIN + 8 - shift, WIN + 8), 0)[:WIN]
            out[slot, plane] = picked.astype(i16)


def cut_windows(place, own, after):
    return pl.pallas_call(
        cut_kernel,
        in_specs=[smem, vmem, vmem],
        out_specs=vmem,
        out_shape=jax.ShapeDtypeStruct((CAP, 3, WIN, WIN), i16),
        scratch_shapes=[pltpu.VMEM((2 * ROWS, COLS), jnp.int32)],
        compiler_params=params,
        name="cut_windows",
    )(place, own, after)


def add_kernel(place, live, grads, top, low, slab):
    slab[...] = jnp.zeros_like(slab)
    for slot in range(CAP):
        base, shift, col = corner(place, slot)

        @pl.when(slot < live[0])
        def _():
            for comp in range(2):
                own = grads.at[slot, comp]
                tall = jnp.concatenate([decode(own, TOP), decode(own, LOW), jnp.zeros((8, WIN), f32)], axis=0)
                tall = pltpu.roll(tall, shift, 0)
                wide = lanes(tall, jnp.zeros((WIN + 8, COLS - WIN), f32))
                slab[comp, pl.ds(base, WIN + 8), :] += pltpu.roll(wide, col, 1)
    for comp in range(2):
        top[comp] = slab[comp, :ROWS, :]
        encode_plane(low.at[comp], slab[comp, ROWS:ROWS + HALF, :], slab[comp, ROWS + HALF:, :])


def add_windows(place, live, grads):
    return pl.pallas_call(
        add_kernel,
        in_specs=[smem, smem, vmem],
        out_specs=[vmem, vmem],
        out_shape=[
            jax.ShapeDtypeStruct((2, ROWS, COLS), f32),
            jax.ShapeDtypeStruct((2, CODED, COLS), i16),
        ],
        scratch_shapes=[pltpu.VMEM((2, 2 * ROWS, COLS), f32)],
        compiler_params=params,
        name="add_windows",
    )(place, live, grads)


def pick_kernel(core, odd, even, out, sem):
    del even

    @pl.when(core[0] == 1)
    def _():
        copies = [pltpu.make_async_copy(odd.at[i, comp], out.at[i, comp], sem.at[2 * i + comp]) for i in range(4) for comp in range(2)]
        for copy in copies:
            copy.start()
        for copy in copies:
            copy.wait()


def pick_pile(core, even, odd):
    return pl.pallas_call(
        pick_kernel,
        in_specs=[smem, hbm, hbm],
        out_specs=hbm,
        out_shape=grads_shape[0],
        input_output_aliases={2: 0},
        scratch_shapes=[dma((8,))],
        compiler_params=params,
        name="pick_pile",
    )(core, odd, even)


def join_kernel(top, low, out):
    for comp in range(2):
        for part in (TOP, LOW):
            out[0, comp, part, :] = top[comp, part, :] + decode(low.at[comp], part)


def join(top, low):
    return pl.pallas_call(
        join_kernel,
        in_specs=[vmem] * 2,
        out_specs=vmem,
        out_shape=jax.ShapeDtypeStruct((1, 2, ROWS, COLS), f32),
        compiler_params=params,
        name="join",
    )(top, low)


def device(x, z, core):
    return x * GROUP + z * 2 + core


ring = range(4)
def ring_step(value, steps, source, target):
    pairs = [(device(x, z, source), device(x, (z + steps) % 4, target)) for x in ring for z in ring]
    return lax.ppermute(value, "depth", pairs)


rings = [[device(x, z, core) for z in ring] for x in ring for core in range(2)]


def exchange(value):
    return lax.all_to_all(value, "depth", 0, 0, axis_index_groups=rings, tiled=True)


def hop(value, source, target):
    return lax.ppermute(value, "depth", [(device(source, z, 0), device(target, z, 0)) for z in ring])


def body(object_slices, probe_wave, amplitudes, positions, counts):
    depth = lax.axis_index("depth")
    stripe = lax.axis_index("stripe")
    stage = depth // GROUP
    slot = (depth % GROUP) // 2
    core = depth % 2
    dft, chirp, pick = (jnp.asarray(t) for t in make_tables())
    place = lax.dynamic_slice_in_dim(positions, stripe * CAP, CAP, 0)
    live = lax.dynamic_slice_in_dim(counts, stripe, 1, 0)
    works = (core == 0) & (slot < live[0])

    def flag_of(t):
        return (slot + 4 * (works & (stage == t))).astype(jnp.int32)[None]

    own = pack(object_slices)
    after = lax.ppermute(own, "stripe", [(i, (i - 1) % 4) for i in ring])
    even = exchange(cut_windows(place, own, after))
    wins = unpack(even, ring_step(even, 0, 1, 0))

    wave, waves = probe_wave, None
    for t in range(STAGES - 1):
        wave, waves = forward_stage(flag_of(t), wave, wins, chirp, waves)
        wave = hop(wave, t, t + 1)
    wave, *grads = turn_stage(flag_of(STAGES - 1), wave, wins, chirp, dft, amplitudes, pick)
    for t in reversed(range(STAGES - 1)):
        wave = hop(wave, t + 1, t)
        results = backward_stage(t == 0, flag_of(t), wave, wins, chirp, waves, grads)
        grads = results[-2:]
        wave = results[0]

    pile = pick_pile(core.astype(jnp.int32)[None], grads[0], ring_step(grads[1], 0, 0, 1))
    top, low = add_windows(place, live, exchange(pile))
    return join(top, lax.ppermute(low, "stripe", [(i, (i + 1) % 4) for i in ring]))


def solution(mesh):
    return jax.shard_map(
        body,
        mesh=mesh,
        in_specs=(P("depth", None, "stripe", None), P(), P("stripe", None, None), P(), P()),
        out_specs=P("depth", None, "stripe", None),
        check_vma=False,
    )
```

time: 222 us -> 207 us (0.932)
  blocking collectives: 13 us -> 45.2 us
  waiting for transfers between devices: 136 us -> 118 us
  starting transfers between devices: 27.5 us -> 9.92 us
  local copies, waits for them, and re-layouts: 9.53 us -> 1.92 us
  Pallas kernels: 31.5 us -> 28.8 us
    all_to_all x1 -> x2, blocking collectives: 13 us -> 45.2 us  [exchange(): lax.all_to_all(value, 'depth', 0, 0, axis_index_groups=rings, tiled=True)]
    all_to_all x3 -> x0, waiting for transfers between devices: 18.8 us -> none  [exchange(): lax.all_to_all(value, 'depth', 0, 0, axis_index_groups=rings, tiled=True)]
    all_to_all x3 -> x0, starting transfers between devices: 12.3 us -> none  [exchange(): lax.all_to_all(value, 'depth', 0, 0, axis_index_groups=rings, tiled=True)]
    ppermute x8 -> x4, starting transfers between devices: 9.77 us -> 4.61 us  [the longest x2 2.64 us: ring_step(): return lax.ppermute(value, 'depth', pairs)]
    unnamed x19 -> x11, local copies, waits for them, and re-layouts: 5.48 us -> 1.27 us
    ppermute x8 -> x4, waiting for transfers between devices: 27.2 us -> 30.2 us  [the longest x1 14.4 us: body(): after = lax.ppermute(own, 'stripe', [(i, (i - 1) % 4) for i in ring])]
    pallas_call x5 -> x8, Pallas kernels: 12.4 us -> 15.1 us  [the longest x3 10.1 us: backward_stage(): pl.pallas_call(lambda *refs: backward_kernel(final, *refs), in_specs=[sme...]
    pallas_call x3, Pallas kernels: 10.8 us -> 8.12 us  [forward_stage(): pl.pallas_call(lambda *refs: forward_kernel(first, *refs), in_specs=[smem...]
  transfers between devices with their start and end apart: 17 -> 10, of which waited for: 11 -> 6; matrix products, arithmetic and copies ran while one was open for 1% -> 0% of each run, Pallas kernels for 3% -> 0%
where the time goes in v3:
time: 207 us; the launch traced here: 204 us
  waiting for transfers between devices  118 us (57%)
  blocking collectives  45.2 us (22%)
  Pallas kernels  28.8 us (14%)
  starting transfers between devices  9.92 us (5%)
    ppermute x6, waiting for transfers between devices, hop(): lax.ppermute(value, 'depth', [(device(source, z, 0), device(target, z, 0)...  87.4 us
    all_to_all x2, blocking collectives, exchange(): lax.all_to_all(value, 'depth', 0, 0, axis_index_groups=rings, tiled=True)  45.2 us
    ppermute x1, waiting for transfers between devices, body(): after = lax.ppermute(own, 'stripe', [(i, (i - 1) % 4) for i in ring])  14.4 us
    ppermute x1, waiting for transfers between devices, body(): lax.ppermute(low, 'stripe', [(i, (i + 1) % 4) for i in ring])  10.4 us
    pallas_call x3, Pallas kernels, backward_stage(): pl.pallas_call(lambda *refs: backward_kernel(final, *refs), in_specs=[sme...  10.1 us
    pallas_call x3, Pallas kernels, forward_stage(): pl.pallas_call(lambda *refs: forward_kernel(first, *refs), in_specs=[smem...  8.12 us
    ppermute x6, starting transfers between devices, hop(): lax.ppermute(value, 'depth', [(device(source, z, 0), device(target, z, 0)...  5.31 us
    ppermute x2, waiting for transfers between devices, ring_step(): return lax.ppermute(value, 'depth', pairs)  5.3 us
  transfers between devices with their start and end apart: 10, of which 6 were waited for; matrix products, arithmetic and copies ran while one was open for 0% of the time, Pallas kernels for 0%

profile of v3, /device:TPU:16, one launch (start us, length us, event | category | flops | bytes accessed | tf_op | source)
XLA Modules:
  0.0 204.4 jit_solution(16422547824688428065)
XLA Ops:
  0.0 0.0 copy-start
  0.0 0.0 copy-start.2
  0.0 1.1 copy-done.2
  1.2 0.2 pack.1.own
  1.4 0.5 collective-permute-start
  1.9 0.0 copy-done
  1.9 0.1 constant_dynamic-slice_fusion
  2.0 0.1 copy.19.place
  2.1 14.4 %collective-permute-done.after = s16[3,256,384]{2,1,0:T(8,128)(2,1)S(1)} collective-permute-done((s16[3,256,384]{2,1,0:T(8,128)(2,1)S(1)}, s16[3,256,384]{2,1,0:T(8,128)(2,1)S(1)}, u32[]{:S(2)}, u32[]{:S(2)}) %collective-permute-start) | collective-permute-done | bytes 589856 | tf_op jit(solution)/shard_map/ppermute | solution.py:683
  16.5 2.6 %cut_windows.1 = s16[4,3,256,256]{3,2,1,0:T(8,128)(2,1)S(1)} custom-call(s32[4,2]{1,0:T(4,128)S(1)} %copy.19.place, s16[3,256,384]{2,1,0:T(8,128)(2,1)S(1)} %pack.1.own, s16[3,256,384]{2,1,0:T(8,128)(2,1)S(1)} %collective-permute-done.after), custom_call_target="tpu_custom_call" | custom-call | tf_op jit(solution)/shard_map/cut_windows/pallas_call | solution.py:561
  19.1 0.0 copy-start.4
  19.1 24.9 %all_to_all.10.even = s16[4,3,256,256]{3,2,1,0:T(8,128)(2,1)S(1)} all-to-all(s16[4,3,256,256]{3,2,1,0:T(8,128)(2,1)S(1)} %cut_windows.1), channel_id=1, replica_groups={{0,8,16,24},{4,12,20,28},{32,40,48,56},{36,44,52,60},{64,72,80,88},{68,..., dimensions={0} | all-to-all | bytes 3145728 | tf_op jit(solution)/shard_map/all_to_all | solution.py:661
  44.0 1.3 collective-permute-start.1
  45.4 0.0 copy-done.4
  45.4 0.6 dynamic_slice.7.live
  46.7 0.0 copy-start.1
  46.7 0.0 copy-start.3
  46.7 2.8 %collective-permute-done.1.odd = s16[4,3,256,256]{3,2,1,0:T(8,128)(2,1)} collective-permute-done((s16[4,3,256,256]{3,2,1,0:T(8,128)(2,1)S(1)}, s16[4,3,256,256]{3,2,1,0:T(8,128)(2,1)}, u32[]{:S(2)}, u32[]{:S(2)}) %collective-permute-start.1) | collective-permute-done | bytes 1572896 | tf_op jit(solution)/shard_map/ppermute | solution.py:654
  49.5 3.5 %unpack.1.refs_2_.wins = f32[8,2,256,256]{3,2,1,0:T(8,128)} custom-call(s16[4,3,256,256]{3,2,1,0:T(8,128)(2,1)S(1)} %all_to_all.10.even, s16[4,3,256,256]{3,2,1,0:T(8,128)(2,1)} %collective-permute-done.1.odd), custom_call_target="tpu_custom_call" | custom-call | tf_op jit(solution)/shard_map/unpack/pallas_call | solution.py:531
  53.0 0.0 copy-done.1
  53.0 0.0 copy-done.3
  53.0 8.0 %forward_stage.3 = (s16[2,272,256]{2,1,0:T(8,128)(2,1)S(1)}, f32[8,2,256,256]{3,2,1,0:T(8,128)}) custom-call(s32[1]{0:T(128)} %bitcast.2.refs_0_, bf16[2,256,256]{2,1,0:T(8,128)(2,1)S(1)} %copy-done.3, f32[8,2,256,256]{3,2,1,0:T(8,128)} %unpack.1.refs_2_.wins, bf16[4,256,256]{2,1,0:T(8,128)(2,1)S(1)} %copy-done.1), custom_call_target="tpu_custom_call" | custom-call | tf_op jit(solution)/shard_map/forward_stage/pallas_call | solution.py:437
  61.0 1.3 collective-permute-start.2
  62.4 4.0 %collective-permute-done.2.refs_1_ = s16[2,272,256]{2,1,0:T(8,128)(2,1)S(1)} collective-permute-done((s16[2,272,256]{2,1,0:T(8,128)(2,1)S(1)}, s16[2,272,256]{2,1,0:T(8,128)(2,1)S(1)}, u32[]{:S(2)}, u32[]{:S(2)}) %collective-permute-start.2) | collective-permute-done | bytes 278560 | tf_op jit(solution)/shard_map/ppermute | solution.py:665
  66.4 0.1 forward_stage.4
  66.4 0.7 collective-permute-start.3
  67.2 0.0 collective-permute-done.3.refs_1_
  67.2 0.1 forward_stage.5
  67.2 0.7 collective-permute-start.4
  67.9 0.0 collective-permute-done.4.coded
  68.0 0.1 turn_stage.1
  68.1 0.7 collective-permute-start.5
  68.8 0.0 collective-permute-done.5.refs_1_
  68.8 0.1 backward_stage.3
  68.9 0.7 collective-permute-start.6
  69.6 0.0 collective-permute-done.6.refs_1_
  69.6 0.1 backward_stage.4
  69.7 1.3 collective-permute-start.7
  71.0 83.3 %collective-permute-done.7.refs_1_ = s16[2,272,256]{2,1,0:T(8,128)(2,1)S(1)} collective-permute-done((s16[2,272,256]{2,1,0:T(8,128)(2,1)S(1)}, s16[2,272,256]{2,1,0:T(8,128)(2,1)S(1)}, u32[]{:S(2)}, u32[]{:S(2)}) %collective-permute-start.7) | collective-permute-done | bytes 278560 | tf_op jit(solution)/shard_map/ppermute | solution.py:665
  154.3 9.9 %backward_stage.5 = (s16[4,2,272,256]{3,2,1,0:T(8,128)(2,1)}, s16[4,2,272,256]{3,2,1,0:T(8,128)(2,1)}) custom-call(s32[1]{0:T(128)} %bitcast.2.refs_0_, s16[2,272,256]{2,1,0:T(8,128)(2,1)S(1)} %collective-permute-done.7.refs_1_, f32[8,2,256,256]{3,2,1,0:T(8,128)} %unpack.1.refs_2_.wins, ...), custom_call_target="tpu_custom_call", output_to_operand_aliasing={{0}: (5, {}), {1}: (6, {})} | custom-call | tf_op jit(solution)/shard_map/backward_stage/pallas_call | solution.py:474
  164.3 1.4 collective-permute-start.8
  165.6 2.5 %collective-permute-done.8.odd = s16[4,2,272,256]{3,2,1,0:T(8,128)(2,1)S(1)} collective-permute-done((s16[4,2,272,256]{3,2,1,0:T(8,128)(2,1)}, s16[4,2,272,256]{3,2,1,0:T(8,128)(2,1)S(1)}, u32[]{:S(2)}, u32[]{:S(2)}) %collective-permute-start.8) | collective-permute-done | bytes 1114144 | tf_op jit(solution)/shard_map/ppermute | solution.py:654
  168.2 0.1 pick_pile.1
  168.2 20.3 %all_to_all.11.grads = s16[4,2,272,256]{3,2,1,0:T(8,128)(2,1)S(1)} all-to-all(s16[4,2,272,256]{3,2,1,0:T(8,128)(2,1)} %pick_pile.1), channel_id=1, replica_groups={{0,8,16,24},{4,12,20,28},{32,40,48,56},{36,44,52,60},{64,72,80,88},{68,..., dimensions={0} | all-to-all | bytes 2228224 | tf_op jit(solution)/shard_map/all_to_all | solution.py:661
  188.5 3.0 %add_windows.1 = (f32[2,256,384]{2,1,0:T(8,128)S(1)}, s16[2,272,384]{2,1,0:T(8,128)(2,1)S(1)}) custom-call(s32[4,2]{1,0:T(4,128)S(1)} %copy.19.place, s32[1]{0:T(128)} %dynamic_slice.7.live, s16[4,2,272,256]{3,2,1,0:T(8,128)(2,1)S(1)} %all_to_all.11.grads), custom_call_target="tpu_custom_call" | custom-call | tf_op jit(solution)/shard_map/add_windows/pallas_call | solution.py:591
  191.5 1.4 collective-permute-start.9
  193.0 10.4 %collective-permute-done.9.low = s16[2,272,384]{2,1,0:T(8,128)(2,1)S(1)} collective-permute-done((s16[2,272,384]{2,1,0:T(8,128)(2,1)S(1)}, s16[2,272,384]{2,1,0:T(8,128)(2,1)S(1)}, u32[]{:S(2)}, u32[]{:S(2)}) %collective-permute-start.9) | collective-permute-done | bytes 417824 | tf_op jit(solution)/shard_map/ppermute | solution.py:700
  203.4 1.0 join.1
Async XLA Ops:
  0.0 1.9 copy-start
  0.0 1.1 copy-start.2
  1.4 15.1 %collective-permute-start = (s16[3,256,384]{2,1,0:T(8,128)(2,1)S(1)}, s16[3,256,384]{2,1,0:T(8,128)(2,1)S(1)}, u32[]{:S(2)}, u32[]{:S(2)}) collective-permute-start(s16[3,256,384]{2,1,0:T(8,128)(2,1)S(1)} %pack.1.own), channel_id=1, source_target_pairs={{0,3},{1,0},{2,1},{3,2},{4,7},{5,4},{6,5},{7,6},{8,11},{9,8},{10,9... | collective-permute-start | bytes 1769480 | tf_op jit(solution)/shard_map/ppermute | solution.py:683
  19.1 26.3 %copy-start.4 = (s32[4]{0:T(128)S(1)}, s32[4]{0:T(128)}, u32[]{:S(2)}) copy-start(s32[4]{0:T(128)} %param.12) | copy-start | bytes 52
  44.0 5.4 %collective-permute-start.1 = (s16[4,3,256,256]{3,2,1,0:T(8,128)(2,1)S(1)}, s16[4,3,256,256]{3,2,1,0:T(8,128)(2,1)}, u32[]{:S(2)}, u32[]{:S(2)}) collective-permute-start(s16[4,3,256,256]{3,2,1,0:T(8,128)(2,1)S(1)} %all_to_all.10.even), channel_id=1, source_target_pairs={{4,0},{12,8},{20,16},{28,24},{36,32},{44,40},{52,48},{60,56},{68,6... | collective-permute-start | bytes 4718600 | tf_op jit(solution)/shard_map/ppermute | solution.py:654
  46.7 6.4 %copy-start.1 = (bf16[4,256,256]{2,1,0:T(8,128)(2,1)S(1)}, bf16[4,256,256]{2,1,0:T(8,128)(2,1)}, u32[]{:S(2)}) copy-start(bf16[4,256,256]{2,1,0:T(8,128)(2,1)} %constant.70.clone.refs_3_.chirp) | copy-start | bytes 1572868
  46.7 6.4 %copy-start.3 = (bf16[2,256,256]{2,1,0:T(8,128)(2,1)S(1)}, bf16[2,256,256]{2,1,0:T(8,128)(2,1)}, u32[]{:S(2)}) copy-start(bf16[2,256,256]{2,1,0:T(8,128)(2,1)} %refs_1_.1) | copy-start | bytes 786436
  61.0 5.3 %collective-permute-start.2 = (s16[2,272,256]{2,1,0:T(8,128)(2,1)S(1)}, s16[2,272,256]{2,1,0:T(8,128)(2,1)S(1)}, u32[]{:S(2)}, u32[]{:S(2)}) collective-permute-start(s16[2,272,256]{2,1,0:T(8,128)(2,1)S(1)} %get-tuple-element.24), channel_id=1, source_target_pairs={{0,32},{8,40},{16,48},{24,56},{1,33},{9,41},{17,49},{25,57},{2,34}... | collective-permute-start | bytes 835592 | tf_op jit(solution)/shard_map/ppermute | solution.py:665
  66.4 0.7 collective-permute-start.3
  67.2 0.7 collective-permute-start.4
  68.1 0.7 collective-permute-start.5
  68.9 0.7 collective-permute-start.6
  69.7 84.6 %collective-permute-start.7 = (s16[2,272,256]{2,1,0:T(8,128)(2,1)S(1)}, s16[2,272,256]{2,1,0:T(8,128)(2,1)S(1)}, u32[]{:S(2)}, u32[]{:S(2)}) collective-permute-start(s16[2,272,256]{2,1,0:T(8,128)(2,1)S(1)} %get-tuple-element.36), channel_id=1, source_target_pairs={{32,0},{40,8},{48,16},{56,24},{33,1},{41,9},{49,17},{57,25},{34,2}... | collective-permute-start | bytes 835592 | tf_op jit(solution)/shard_map/ppermute | solution.py:665
  164.3 3.9 %collective-permute-start.8 = (s16[4,2,272,256]{3,2,1,0:T(8,128)(2,1)}, s16[4,2,272,256]{3,2,1,0:T(8,128)(2,1)S(1)}, u32[]{:S(2)}, u32[]{:S(2)}) collective-permute-start(s16[4,2,272,256]{3,2,1,0:T(8,128)(2,1)} %get-tuple-element.39), channel_id=1, source_target_pairs={{0,4},{8,12},{16,20},{24,28},{32,36},{40,44},{48,52},{56,60},{64,6... | collective-permute-start | bytes 3342344 | tf_op jit(solution)/shard_map/ppermute | solution.py:654
  191.5 11.9 %collective-permute-start.9 = (s16[2,272,384]{2,1,0:T(8,128)(2,1)S(1)}, s16[2,272,384]{2,1,0:T(8,128)(2,1)S(1)}, u32[]{:S(2)}, u32[]{:S(2)}) collective-permute-start(s16[2,272,384]{2,1,0:T(8,128)(2,1)S(1)} %get-tuple-element.42), channel_id=1, source_target_pairs={{0,1},{1,2},{2,3},{3,0},{4,5},{5,6},{6,7},{7,4},{8,9},{9,10},{10,1... | collective-permute-start | bytes 1253384 | tf_op jit(solution)/shard_map/ppermute | solution.py:700

commit v4 on v3

--- a/solution.py
+++ b/solution.py
@@ -228,7 +228,10 @@
     wr, wi = wave[0, part, :], wave[1, part, :]
     half = part.start // HALF
     for comp, value in enumerate((wr * re - wi * im, -(wr * im + wi * re))):
-        tails[comp, 8 * half:8 * half + 8, :] = encode(grad.at[comp], part, value)
+        if tails is None:
+            grad[comp, part, :] = value
+        else:
+            tails[comp, 8 * half:8 * half + 8, :] = encode(grad.at[comp], part, value)
     adj[0, part, :], adj[1, part, :] = times(re, im, windows.at(i), part)
 
 
@@ -245,7 +248,8 @@
         retreat(i, part, re, im, adj, wave, windows, grad, tails)
 
     propagate(source, sink, chirp)
-    finish_grad(grad, tails)
+    if tails is not None:
+        finish_grad(grad, tails)
 
 
 def copy_wave(dst, src):
@@ -253,8 +257,8 @@
         dst[comp] = src[comp].astype(f32)
 
 
-def forward_kernel(first, flag, coded, wins, chirp, *rest):
-    wave_out, waves, win_buf, win_sem, buf, sem = rest[-6:]
+def forward_kernel(first, flag, coded, wins, chirp, first_win, *rest):
+    wave_out, waves, edge, win_buf, win_sem, buf, sem = rest[-7:]
     windows = Ahead(wins, win_buf, win_sem, win_buf.shape[0])
 
     def store(i):
@@ -263,8 +267,9 @@
 
     @pl.when(flag[0] >= 4)
     def _():
-        for i in range(DEPTH - 1):
+        for i in range(1, DEPTH - 1):
             windows.start(jnp.int32(i))
+        copy_wave(win_buf.at[0], first_win)
         if first:
             copy_wave(buf.at[0], coded)
         else:
@@ -282,10 +287,14 @@
             def _():
                 store(i - 2).wait()
 
-            windows.wait(i)
+            @pl.when(i > 0)
+            def _():
+                windows.wait(i)
+
             forward_slice(buf.at[lax.rem(i, 3)], buf.at[lax.rem(i + 1, 3)], windows, i, chirp)
 
         encode_wave(wave_out, buf.at[GROUP % 3])
+        copy_wave(edge, buf.at[(GROUP - 1) % 3])
         store(jnp.int32(GROUP - 2)).wait()
         store(jnp.int32(GROUP - 1)).wait()
 
@@ -310,24 +319,28 @@
                 self.copy(i, odd).wait()
 
 
-def turn_kernel(flag, coded, wins, chirp, dft_in, patterns, pick_in, adj_out, *rest):
-    *grads, win_buf, win_sem, grad_buf, grad_sem, adj, tails = rest[:8]
-    waves, mid, far_amp, dft, pattern, pick, late_sem = rest[8:]
+def turn_kernel(flag, coded, wins, chirp, first_win, dft_in, patterns, pick_in, adj_out, *rest):
+    *grads, win_buf, win_sem, grad_buf, grad_sem, adj = rest[:7]
+    waves, mid, far_amp, dft, pattern, pick, late_sem = rest[7:]
     windows = Ahead(wins, win_buf, win_sem, win_buf.shape[0])
     out = Gradients(grads, grad_buf, grad_sem)
     end = GROUP - 1
 
     @pl.when(flag[0] >= 4)
     def _():
-        for i in range(GROUP):
+        for i in range(1, GROUP):
             windows.start(jnp.int32(i))
+        copy_wave(win_buf.at[0], first_win)
         late = Fetch([(dft_in, dft), (patterns.at[flag[0] & 3], pattern), (pick_in, pick)], late_sem)
         late.start()
         decode_wave(waves.at[0], coded)
 
         @pl.loop(0, end)
         def _(i):
-            windows.wait(i)
+            @pl.when(i > 0)
+            def _():
+                windows.wait(i)
+
             forward_slice(waves.at[i], waves.at[i + 1], windows, i, chirp)
 
         windows.wait(jnp.int32(end))
@@ -344,10 +357,9 @@
             return factor * re, factor * im
 
         def sink(part, re, im):
-            retreat(end, part, re, -im, adj, waves.at[end], windows, grad_buf.at[end & 1], tails)
+            retreat(end, part, re, -im, adj, waves.at[end], windows, grad_buf.at[end & 1], None)
 
         exit_wave(source, sink, dft, mid, exit_point)
-        finish_grad(grad_buf.at[end & 1], tails)
         out.start(jnp.int32(end))
 
         @pl.loop(0, end)
@@ -358,7 +370,7 @@
             def _():
                 out.wait(i + 2)
 
-            backward_slice(i, adj, waves.at[i], windows, chirp, grad_buf.at[i & 1], tails)
+            backward_slice(i, adj, waves.at[i], windows, chirp, grad_buf.at[i & 1], None)
             out.start(i)
 
         encode_wave(adj_out, adj)
@@ -366,12 +378,12 @@
         out.wait(jnp.int32(0))
 
 
-def backward_kernel(final, flag, coded, wins, chirp, waves, *rest):
+def backward_kernel(final, flag, coded, wins, chirp, waves, last_win, last_wave, *rest):
     rest = rest[2:]
     if not final:
         adj_out, rest = rest[0], rest[1:]
-    *grads, win_buf, win_sem, grad_buf, grad_sem, adj, tails = rest[:8]
-    wave_buf, wave_sem = rest[8:]
+    *grads, win_buf, win_sem, grad_buf, grad_sem, adj, wave_buf, wave_sem = rest[:9]
+    tails = rest[9] if final else None
     windows = Ahead(wins, win_buf, win_sem, win_buf.shape[0])
     out = Gradients(grads, grad_buf, grad_sem)
 
@@ -379,16 +391,20 @@
 
     @pl.when(flag[0] >= 4)
     def _():
-        for i in range(DEPTH - 1):
+        for i in range(1, DEPTH - 1):
             windows.start(jnp.int32(GROUP - 1 - i))
             kept.start(jnp.int32(GROUP - 1 - i))
+        copy_wave(win_buf.at[(GROUP - 1) % DEPTH], last_win)
+        copy_wave(wave_buf.at[(GROUP - 1) % DEPTH], last_wave)
         decode_wave(adj, coded)
 
         @pl.loop(0, GROUP)
         def _(step):
             i = GROUP - 1 - step
-            windows.wait(i)
-            kept.wait(i)
+            @pl.when(step > 0)
+            def _():
+                windows.wait(i)
+                kept.wait(i)
 
             @pl.when(i >= DEPTH - 1)
             def _():
@@ -418,28 +434,29 @@
 dma = pltpu.SemaphoreType.DMA
 DEPTH = 4
 win_scratch = lambda depth: [pltpu.VMEM((depth, 2, WIN, WIN), f32), dma((depth,))]
-grad_scratch = lambda: [
-    pltpu.VMEM((2, 2, CODED, WIN), i16),
+raw_shape = [pltpu.HBM((GROUP // 2, 2, WIN, WIN), f32)] * 2
+grad_scratch = lambda coded: [
+    pltpu.VMEM((2, 2, CODED, WIN), i16) if coded else pltpu.VMEM((2, 2, WIN, WIN), f32),
     dma((2,)),
     pltpu.VMEM((2, WIN, WIN), f32),
-    pltpu.VMEM((2, 16, WIN), jnp.int32),
 ]
+tail_scratch = lambda: [pltpu.VMEM((2, 16, WIN), jnp.int32)]
 
 
 def in_hbm(value):
     return pltpu.with_memory_space_constraint(value, pltpu.HBM)
 
 
-def forward_stage(flag, wave, wins, chirp, waves):
+def forward_stage(flag, wave, wins, chirp, first_win, waves):
     first = waves is None
-    args = [flag, wave, in_hbm(wins), chirp]
+    args = [flag, wave, in_hbm(wins), chirp, first_win]
     args += [] if first else [in_hbm(waves)]
     return pl.pallas_call(
         lambda *refs: forward_kernel(first, *refs),
-        in_specs=[smem, vmem, hbm, vmem] + [hbm] * (len(args) - 4),
-        out_specs=[vmem, hbm],
-        out_shape=[wave_shape, waves_shape],
-        input_output_aliases={} if first else {4: 1},
+        in_specs=[smem, vmem, hbm, vmem, vmem] + [hbm] * (len(args) - 5),
+        out_specs=[vmem, hbm, vmem],
+        out_shape=[wave_shape, waves_shape, jax.ShapeDtypeStruct((2, WIN, WIN), f32)],
+        input_output_aliases={} if first else {5: 1},
         scratch_shapes=win_scratch(DEPTH) + [
             pltpu.VMEM((3, 2, WIN, WIN), f32),
             dma((3,)),
@@ -449,13 +466,13 @@
     )(*args)
 
 
-def turn_stage(flag, wave, wins, chirp, dft, patterns, pick):
+def turn_stage(flag, wave, wins, chirp, first_win, dft, patterns, pick):
     return pl.pallas_call(
         turn_kernel,
-        in_specs=[smem, vmem, hbm, vmem] + [hbm] * 3,
+        in_specs=[smem, vmem, hbm, vmem, vmem] + [hbm] * 3,
         out_specs=[vmem] + [hbm] * 2,
-        out_shape=[wave_shape, *grads_shape],
-        scratch_shapes=win_scratch(GROUP) + grad_scratch() + [
+        out_shape=[wave_shape, *raw_shape],
+        scratch_shapes=win_scratch(GROUP) + grad_scratch(False) + [
             pltpu.VMEM((GROUP, 2, WIN, WIN), f32),
             pltpu.VMEM((2, WIN, WIN), f32),
             pltpu.VMEM((WIN, WIN), f32),
@@ -466,24 +483,71 @@
         ],
         compiler_params=params,
         name="turn_stage",
-    )(flag, wave, in_hbm(wins), chirp, in_hbm(dft), in_hbm(patterns), in_hbm(pick))
-
-
-def backward_stage(final, flag, adj, wins, chirp, waves, grads):
+    )(flag, wave, in_hbm(wins), chirp, first_win, in_hbm(dft), in_hbm(patterns), in_hbm(pick))
+
+
+def backward_stage(final, flag, adj, wins, chirp, waves, last_win, last_wave, grads):
     lead = 0 if final else 1
     return pl.pallas_call(
         lambda *refs: backward_kernel(final, *refs),
-        in_specs=[smem, vmem, hbm, vmem] + [hbm] * 3,
+        in_specs=[smem, vmem, hbm, vmem, hbm, vmem, vmem] + [hbm] * 2,
         out_specs=[vmem] * lead + [hbm] * 2,
-        out_shape=[wave_shape] * lead + grads_shape,
-        input_output_aliases={5 + k: lead + k for k in range(2)},
-        scratch_shapes=win_scratch(DEPTH) + grad_scratch() + [
+        out_shape=[wave_shape] * lead + (grads_shape if final else raw_shape),
+        input_output_aliases={7 + k: lead + k for k in range(2)},
+        scratch_shapes=win_scratch(DEPTH) + grad_scratch(final) + [
             pltpu.VMEM((DEPTH, 2, WIN, WIN), f32),
             dma((DEPTH,)),
-        ],
+        ] + (tail_scratch() if final else []),
         compiler_params=params,
         name="backward_stage",
-    )(flag, adj, in_hbm(wins), chirp, in_hbm(waves), *[in_hbm(grad) for grad in grads])
+    )(flag, adj, in_hbm(wins), chirp, in_hbm(waves), last_win, last_wave, *[in_hbm(grad) for grad in grads])
+
+
+def code_kernel(flag, even, odd, coded_even, coded_odd, buf, sem, out_buf, out_sem, tails):
+    def load(i):
+        return pltpu.make_async_copy((even, odd)[i % 2].at[i // 2], buf.at[i % DEPTH], sem.at[i % DEPTH])
+
+    def store(i):
+        return pltpu.make_async_copy(
+            out_buf.at[i % 2], (coded_even, coded_odd)[i % 2].at[i // 2], out_sem.at[i % 2]
+        )
+
+    @pl.when(flag[0] >= 4)
+    def _():
+        for i in range(DEPTH):
+            load(i).start()
+        for i in range(GROUP):
+            load(i).wait()
+            if i >= 2:
+                store(i - 2).wait()
+            for comp in range(2):
+                for half, part in enumerate((TOP, LOW)):
+                    tails[comp, 8 * half:8 * half + 8, :] = encode(
+                        out_buf.at[i % 2, comp], part, buf[i % DEPTH, comp, part, :]
+                    )
+            finish_grad(out_buf.at[i % 2], tails)
+            store(i).start()
+            if i + DEPTH < GROUP:
+                load(i + DEPTH).start()
+        store(GROUP - 2).wait()
+        store(GROUP - 1).wait()
+
+
+def code_grads(flag, grads):
+    return pl.pallas_call(
+        code_kernel,
+        in_specs=[smem] + [hbm] * 2,
+        out_specs=[hbm] * 2,
+        out_shape=grads_shape,
+        scratch_shapes=[
+            pltpu.VMEM((DEPTH, 2, WIN, WIN), f32),
+            dma((DEPTH,)),
+            pltpu.VMEM((2, 2, CODED, WIN), i16),
+            dma((2,)),
+        ] + tail_scratch(),
+        compiler_params=params,
+        name="code_grads",
+    )(flag, *[in_hbm(grad) for grad in grads])
 
 
 FINE = 2.0**23
@@ -511,7 +575,7 @@
     )(own)
 
 
-def unpack_kernel(even, odd, out, buf, sem):
+def unpack_kernel(even, odd, out, first, last, buf, sem):
     copies = []
     for i in range(GROUP):
         array = (even, odd)[i % 2]
@@ -521,6 +585,8 @@
             for comp, byte in enumerate((both >> 8, both & 255)):
                 word = (array[i // 2, 1 + comp, part, :].astype(jnp.int32) << 8) + byte
                 buf[i, comp, part, :] = word.astype(f32) * (1.0 / FINE)
+                if i in (0, GROUP - 1):
+                    (last if i else first)[comp, part, :] = buf[i, comp, part, :]
         copies.append(pltpu.make_async_copy(buf.at[i], out.at[i], sem.at[i]))
         copies[-1].start()
     for copy in copies:
@@ -531,8 +597,8 @@
     return pl.pallas_call(
         unpack_kernel,
         in_specs=[vmem] * 2,
-        out_specs=hbm,
-        out_shape=pltpu.HBM((GROUP, 2, WIN, WIN), f32),
+        out_specs=[hbm, vmem, vmem],
+        out_shape=[pltpu.HBM((GROUP, 2, WIN, WIN), f32)] + [jax.ShapeDtypeStruct((2, WIN, WIN), f32)] * 2,
         scratch_shapes=[pltpu.VMEM((GROUP, 2, WIN, WIN), f32), dma((GROUP,))],
         compiler_params=params,
         name="unpack",
@@ -682,16 +748,19 @@
     own = pack(object_slices)
     after = lax.ppermute(own, "stripe", [(i, (i - 1) % 4) for i in ring])
     even = exchange(cut_windows(place, own, after))
-    wins = unpack(even, ring_step(even, 0, 1, 0))
-
-    wave, waves = probe_wave, None
+    wins, first, final_win = unpack(even, ring_step(even, 0, 1, 0))
+
+    wave, waves, edges = probe_wave, None, []
     for t in range(STAGES - 1):
-        wave, waves = forward_stage(flag_of(t), wave, wins, chirp, waves)
+        wave, waves, edge = forward_stage(flag_of(t), wave, wins, chirp, first, waves)
+        edges.append(edge)
         wave = hop(wave, t, t + 1)
-    wave, *grads = turn_stage(flag_of(STAGES - 1), wave, wins, chirp, dft, amplitudes, pick)
+    wave, *grads = turn_stage(flag_of(STAGES - 1), wave, wins, chirp, first, dft, amplitudes, pick)
     for t in reversed(range(STAGES - 1)):
         wave = hop(wave, t + 1, t)
-        results = backward_stage(t == 0, flag_of(t), wave, wins, chirp, waves, grads)
+        if t == 0:
+            grads = code_grads((4 * (works & (stage > 0))).astype(jnp.int32)[None], grads)
+        results = backward_stage(t == 0, flag_of(t), wave, wins, chirp, waves, final_win, edges[t], grads)
         grads = results[-2:]
         wave = results[0]
 

time: 207 us -> 200 us (0.966)
  waiting for transfers between devices: 118 us -> 111 us
    ppermute x6, waiting for transfers between devices: 87.4 us -> 80.5 us  [hop(): lax.ppermute(value, 'depth', [(device(source, z, 0), device(target, z, 0)...]
where the time goes in v4:
time: 200 us; the launch traced here: 197 us
  waiting for transfers between devices  111 us (56%)
  blocking collectives  45.3 us (23%)
  Pallas kernels  28.4 us (14%)
  starting transfers between devices  10.1 us (5%)
    ppermute x6, waiting for transfers between devices, hop(): lax.ppermute(value, 'depth', [(device(source, z, 0), device(target, z, 0)...  80.5 us
    all_to_all x2, blocking collectives, exchange(): lax.all_to_all(value, 'depth', 0, 0, axis_index_groups=rings, tiled=True)  45.3 us
    ppermute x1, waiting for transfers between devices, body(): after = lax.ppermute(own, 'stripe', [(i, (i - 1) % 4) for i in ring])  14.4 us
    ppermute x1, waiting for transfers between devices, body(): lax.ppermute(low, 'stripe', [(i, (i + 1) % 4) for i in ring])  10.4 us
    pallas_call x3, Pallas kernels, backward_stage(): pl.pallas_call(lambda *refs: backward_kernel(final, *refs), in_specs=[sme...  8.92 us
    pallas_call x3, Pallas kernels, forward_stage(): pl.pallas_call(lambda *refs: forward_kernel(first, *refs), in_specs=[smem...  8.68 us
    ppermute x6, starting transfers between devices, hop(): lax.ppermute(value, 'depth', [(device(source, z, 0), device(target, z, 0)...  5.31 us
    ppermute x2, waiting for transfers between devices, ring_step(): return lax.ppermute(value, 'depth', pairs)  5.22 us
  transfers between devices with their start and end apart: 10, of which 6 were waited for; matrix products, arithmetic and copies ran while one was open for 0% of the time, Pallas kernels for 0%

profile of v4, /device:TPU:16, one launch (start us, length us, event | category | flops | bytes accessed | tf_op | source)
XLA Modules:
  0.0 197.3 jit_solution(17620997071217186119)
XLA Ops:
  0.0 0.0 copy-start
  0.0 0.0 copy-start.2
  0.0 1.1 copy-done.2
  1.2 0.2 pack.1.own
  1.4 0.5 collective-permute-start
  1.9 0.0 copy-done
  1.9 0.1 constant_dynamic-slice_fusion
  2.0 0.1 copy.19.place
  2.1 14.4 %collective-permute-done.after = s16[3,256,384]{2,1,0:T(8,128)(2,1)S(1)} collective-permute-done((s16[3,256,384]{2,1,0:T(8,128)(2,1)S(1)}, s16[3,256,384]{2,1,0:T(8,128)(2,1)S(1)}, u32[]{:S(2)}, u32[]{:S(2)}) %collective-permute-start) | collective-permute-done | bytes 589856 | tf_op jit(solution)/shard_map/ppermute | solution.py:749
  16.5 2.6 %cut_windows.1 = s16[4,3,256,256]{3,2,1,0:T(8,128)(2,1)S(1)} custom-call(s32[4,2]{1,0:T(4,128)S(1)} %copy.19.place, s16[3,256,384]{2,1,0:T(8,128)(2,1)S(1)} %pack.1.own, s16[3,256,384]{2,1,0:T(8,128)(2,1)S(1)} %collective-permute-done.after), custom_call_target="tpu_custom_call" | custom-call | tf_op jit(solution)/shard_map/cut_windows/pallas_call | solution.py:627
  19.1 0.0 copy-start.4
  19.1 24.9 %all_to_all.10.even = s16[4,3,256,256]{3,2,1,0:T(8,128)(2,1)S(1)} all-to-all(s16[4,3,256,256]{3,2,1,0:T(8,128)(2,1)S(1)} %cut_windows.1), channel_id=1, replica_groups={{0,8,16,24},{4,12,20,28},{32,40,48,56},{36,44,52,60},{64,72,80,88},{68,..., dimensions={0} | all-to-all | bytes 3145728 | tf_op jit(solution)/shard_map/all_to_all | solution.py:727
  44.1 0.0 copy-start.1
  44.1 0.0 copy-start.3
  44.1 1.4 collective-permute-start.1
  45.5 0.0 copy-done.4
  45.5 0.7 dynamic_slice.7.live
  46.9 2.7 %collective-permute-done.1.odd = s16[4,3,256,256]{3,2,1,0:T(8,128)(2,1)} collective-permute-done((s16[4,3,256,256]{3,2,1,0:T(8,128)(2,1)S(1)}, s16[4,3,256,256]{3,2,1,0:T(8,128)(2,1)}, u32[]{:S(2)}, u32[]{:S(2)}) %collective-permute-start.1) | collective-permute-done | bytes 1572896 | tf_op jit(solution)/shard_map/ppermute | solution.py:720
  49.6 3.5 %unpack.1 = (f32[8,2,256,256]{3,2,1,0:T(8,128)}, f32[2,256,256]{2,1,0:T(8,128)S(1)}, f32[2,256,256]{2,1,0:T(8,128)S(1)}) custom-call(s16[4,3,256,256]{3,2,1,0:T(8,128)(2,1)S(1)} %all_to_all.10.even, s16[4,3,256,256]{3,2,1,0:T(8,128)(2,1)} %collective-permute-done.1.odd), custom_call_target="tpu_custom_call" | custom-call | tf_op jit(solution)/shard_map/unpack/pallas_call | solution.py:597
  53.2 0.0 copy-done.1
  53.2 0.0 copy-done.3
  53.2 7.1 %forward_stage.3 = (s16[2,272,256]{2,1,0:T(8,128)(2,1)S(1)}, f32[8,2,256,256]{3,2,1,0:T(8,128)}, f32[2,256,256]{2,1,0:T(8,128)S(1)}) custom-call(s32[1]{0:T(128)} %bitcast.2.refs_0_, bf16[2,256,256]{2,1,0:T(8,128)(2,1)S(1)} %copy-done.3, f32[8,2,256,256]{3,2,1,0:T(8,128)} %get-tuple-element.32.refs_2_.wins, bf16[4,256,256]{2,1,0:T(8,128)(2,1)S(1)} %copy-done.1, ...), custom_call_target="tpu_custom_call" | custom-call | tf_op jit(solution)/shard_map/forward_stage/pallas_call | solution.py:454
  60.3 1.3 collective-permute-start.2
  61.7 4.0 %collective-permute-done.2.refs_1_ = s16[2,272,256]{2,1,0:T(8,128)(2,1)S(1)} collective-permute-done((s16[2,272,256]{2,1,0:T(8,128)(2,1)S(1)}, s16[2,272,256]{2,1,0:T(8,128)(2,1)S(1)}, u32[]{:S(2)}, u32[]{:S(2)}) %collective-permute-start.2) | collective-permute-done | bytes 278560 | tf_op jit(solution)/shard_map/ppermute | solution.py:731
  65.7 0.8 forward_stage.4
  66.5 0.7 collective-permute-start.3
  67.2 0.0 collective-permute-done.3.refs_1_
  67.2 0.8 forward_stage.5
  68.0 0.7 collective-permute-start.4
  68.7 0.0 collective-permute-done.4.coded
  68.7 0.1 turn_stage.1
  68.8 0.7 collective-permute-start.5
  69.5 0.0 collective-permute-done.5.refs_1_
  69.5 0.1 backward_stage.3
  69.6 0.7 collective-permute-start.6
  70.3 0.0 collective-permute-done.6.refs_1_
  70.3 0.1 backward_stage.4
  70.4 1.3 collective-permute-start.7
  71.7 0.2 code_grads.1
  72.0 76.5 %collective-permute-done.7.refs_1_ = s16[2,272,256]{2,1,0:T(8,128)(2,1)S(1)} collective-permute-done((s16[2,272,256]{2,1,0:T(8,128)(2,1)S(1)}, s16[2,272,256]{2,1,0:T(8,128)(2,1)S(1)}, u32[]{:S(2)}, u32[]{:S(2)}) %collective-permute-start.7) | collective-permute-done | bytes 278560 | tf_op jit(solution)/shard_map/ppermute | solution.py:731
  148.4 8.7 %backward_stage.5 = (s16[4,2,272,256]{3,2,1,0:T(8,128)(2,1)}, s16[4,2,272,256]{3,2,1,0:T(8,128)(2,1)}) custom-call(s32[1]{0:T(128)} %bitcast.2.refs_0_, s16[2,272,256]{2,1,0:T(8,128)(2,1)S(1)} %collective-permute-done.7.refs_1_, f32[8,2,256,256]{3,2,1,0:T(8,128)} %get-tuple-element.32.refs_2_.wins, ...), custom_call_target="tpu_custom_call", output_to_operand_aliasing={{0}: (7, {}), {1}: (8, {})} | custom-call | tf_op jit(solution)/shard_map/backward_stage/pallas_call | solution.py:491
  157.2 1.4 collective-permute-start.8
  158.5 2.5 %collective-permute-done.8.odd = s16[4,2,272,256]{3,2,1,0:T(8,128)(2,1)S(1)} collective-permute-done((s16[4,2,272,256]{3,2,1,0:T(8,128)(2,1)}, s16[4,2,272,256]{3,2,1,0:T(8,128)(2,1)S(1)}, u32[]{:S(2)}, u32[]{:S(2)}) %collective-permute-start.8) | collective-permute-done | bytes 1114144 | tf_op jit(solution)/shard_map/ppermute | solution.py:720
  161.0 0.1 pick_pile.1
  161.1 20.4 %all_to_all.11.grads = s16[4,2,272,256]{3,2,1,0:T(8,128)(2,1)S(1)} all-to-all(s16[4,2,272,256]{3,2,1,0:T(8,128)(2,1)} %pick_pile.1), channel_id=1, replica_groups={{0,8,16,24},{4,12,20,28},{32,40,48,56},{36,44,52,60},{64,72,80,88},{68,..., dimensions={0} | all-to-all | bytes 2228224 | tf_op jit(solution)/shard_map/all_to_all | solution.py:727
  181.5 3.0 %add_windows.1 = (f32[2,256,384]{2,1,0:T(8,128)S(1)}, s16[2,272,384]{2,1,0:T(8,128)(2,1)S(1)}) custom-call(s32[4,2]{1,0:T(4,128)S(1)} %copy.19.place, s32[1]{0:T(128)} %dynamic_slice.7.live, s16[4,2,272,256]{3,2,1,0:T(8,128)(2,1)S(1)} %all_to_all.11.grads), custom_call_target="tpu_custom_call" | custom-call | tf_op jit(solution)/shard_map/add_windows/pallas_call | solution.py:657
  184.5 1.4 collective-permute-start.9
  185.9 10.4 %collective-permute-done.9.low = s16[2,272,384]{2,1,0:T(8,128)(2,1)S(1)} collective-permute-done((s16[2,272,384]{2,1,0:T(8,128)(2,1)S(1)}, s16[2,272,384]{2,1,0:T(8,128)(2,1)S(1)}, u32[]{:S(2)}, u32[]{:S(2)}) %collective-permute-start.9) | collective-permute-done | bytes 417824 | tf_op jit(solution)/shard_map/ppermute | solution.py:769
  196.3 1.0 join.1
Async XLA Ops:
  0.0 1.9 copy-start
  0.0 1.1 copy-start.2
  1.4 15.1 %collective-permute-start = (s16[3,256,384]{2,1,0:T(8,128)(2,1)S(1)}, s16[3,256,384]{2,1,0:T(8,128)(2,1)S(1)}, u32[]{:S(2)}, u32[]{:S(2)}) collective-permute-start(s16[3,256,384]{2,1,0:T(8,128)(2,1)S(1)} %pack.1.own), channel_id=1, source_target_pairs={{0,3},{1,0},{2,1},{3,2},{4,7},{5,4},{6,5},{7,6},{8,11},{9,8},{10,9... | collective-permute-start | bytes 1769480 | tf_op jit(solution)/shard_map/ppermute | solution.py:749
  19.1 26.4 %copy-start.4 = (s32[4]{0:T(128)S(1)}, s32[4]{0:T(128)}, u32[]{:S(2)}) copy-start(s32[4]{0:T(128)} %param.12) | copy-start | bytes 52
  44.1 9.1 %copy-start.1 = (bf16[4,256,256]{2,1,0:T(8,128)(2,1)S(1)}, bf16[4,256,256]{2,1,0:T(8,128)(2,1)}, u32[]{:S(2)}) copy-start(bf16[4,256,256]{2,1,0:T(8,128)(2,1)} %constant.71.clone.refs_3_.chirp) | copy-start | bytes 1572868
  44.1 9.1 %copy-start.3 = (bf16[2,256,256]{2,1,0:T(8,128)(2,1)S(1)}, bf16[2,256,256]{2,1,0:T(8,128)(2,1)}, u32[]{:S(2)}) copy-start(bf16[2,256,256]{2,1,0:T(8,128)(2,1)} %refs_1_.1) | copy-start | bytes 786436
  44.1 5.6 %collective-permute-start.1 = (s16[4,3,256,256]{3,2,1,0:T(8,128)(2,1)S(1)}, s16[4,3,256,256]{3,2,1,0:T(8,128)(2,1)}, u32[]{:S(2)}, u32[]{:S(2)}) collective-permute-start(s16[4,3,256,256]{3,2,1,0:T(8,128)(2,1)S(1)} %all_to_all.10.even), channel_id=1, source_target_pairs={{4,0},{12,8},{20,16},{28,24},{36,32},{44,40},{52,48},{60,56},{68,6... | collective-permute-start | bytes 4718600 | tf_op jit(solution)/shard_map/ppermute | solution.py:720
  60.3 5.3 %collective-permute-start.2 = (s16[2,272,256]{2,1,0:T(8,128)(2,1)S(1)}, s16[2,272,256]{2,1,0:T(8,128)(2,1)S(1)}, u32[]{:S(2)}, u32[]{:S(2)}) collective-permute-start(s16[2,272,256]{2,1,0:T(8,128)(2,1)S(1)} %get-tuple-element.34), channel_id=1, source_target_pairs={{0,32},{8,40},{16,48},{24,56},{1,33},{9,41},{17,49},{25,57},{2,34}... | collective-permute-start | bytes 835592 | tf_op jit(solution)/shard_map/ppermute | solution.py:731
  66.5 0.7 collective-permute-start.3
  68.0 0.7 collective-permute-start.4
  68.8 0.7 collective-permute-start.5
  69.6 0.7 collective-permute-start.6
  70.4 78.0 %collective-permute-start.7 = (s16[2,272,256]{2,1,0:T(8,128)(2,1)S(1)}, s16[2,272,256]{2,1,0:T(8,128)(2,1)S(1)}, u32[]{:S(2)}, u32[]{:S(2)}) collective-permute-start(s16[2,272,256]{2,1,0:T(8,128)(2,1)S(1)} %get-tuple-element.49), channel_id=1, source_target_pairs={{32,0},{40,8},{48,16},{56,24},{33,1},{41,9},{49,17},{57,25},{34,2}... | collective-permute-start | bytes 835592 | tf_op jit(solution)/shard_map/ppermute | solution.py:731
  157.2 3.9 %collective-permute-start.8 = (s16[4,2,272,256]{3,2,1,0:T(8,128)(2,1)}, s16[4,2,272,256]{3,2,1,0:T(8,128)(2,1)S(1)}, u32[]{:S(2)}, u32[]{:S(2)}) collective-permute-start(s16[4,2,272,256]{3,2,1,0:T(8,128)(2,1)} %get-tuple-element.55), channel_id=1, source_target_pairs={{0,4},{8,12},{16,20},{24,28},{32,36},{40,44},{48,52},{56,60},{64,6... | collective-permute-start | bytes 3342344 | tf_op jit(solution)/shard_map/ppermute | solution.py:720
  184.5 11.8 %collective-permute-start.9 = (s16[2,272,384]{2,1,0:T(8,128)(2,1)S(1)}, s16[2,272,384]{2,1,0:T(8,128)(2,1)S(1)}, u32[]{:S(2)}, u32[]{:S(2)}) collective-permute-start(s16[2,272,384]{2,1,0:T(8,128)(2,1)S(1)} %get-tuple-element.58), channel_id=1, source_target_pairs={{0,1},{1,2},{2,3},{3,0},{4,5},{5,6},{6,7},{7,4},{8,9},{9,10},{10,1... | collective-permute-start | bytes 1253384 | tf_op jit(solution)/shard_map/ppermute | solution.py:769

commit v5 on v4

--- a/solution.py
+++ b/solution.py
@@ -258,7 +258,7 @@
 
 
 def forward_kernel(first, flag, coded, wins, chirp, first_win, *rest):
-    wave_out, waves, edge, win_buf, win_sem, buf, sem = rest[-7:]
+    wave_out, waves, win_buf, win_sem, buf, sem = rest[-6:]
     windows = Ahead(wins, win_buf, win_sem, win_buf.shape[0])
 
     def store(i):
@@ -294,7 +294,6 @@
             forward_slice(buf.at[lax.rem(i, 3)], buf.at[lax.rem(i + 1, 3)], windows, i, chirp)
 
         encode_wave(wave_out, buf.at[GROUP % 3])
-        copy_wave(edge, buf.at[(GROUP - 1) % 3])
         store(jnp.int32(GROUP - 2)).wait()
         store(jnp.int32(GROUP - 1)).wait()
 
@@ -454,8 +453,8 @@
     return pl.pallas_call(
         lambda *refs: forward_kernel(first, *refs),
         in_specs=[smem, vmem, hbm, vmem, vmem] + [hbm] * (len(args) - 5),
-        out_specs=[vmem, hbm, vmem],
-        out_shape=[wave_shape, waves_shape, jax.ShapeDtypeStruct((2, WIN, WIN), f32)],
+        out_specs=[vmem, hbm],
+        out_shape=[wave_shape, waves_shape],
         input_output_aliases={} if first else {5: 1},
         scratch_shapes=win_scratch(DEPTH) + [
             pltpu.VMEM((3, 2, WIN, WIN), f32),
@@ -750,17 +749,17 @@
     even = exchange(cut_windows(place, own, after))
     wins, first, final_win = unpack(even, ring_step(even, 0, 1, 0))
 
-    wave, waves, edges = probe_wave, None, []
+    wave, waves = probe_wave, None
     for t in range(STAGES - 1):
-        wave, waves, edge = forward_stage(flag_of(t), wave, wins, chirp, first, waves)
-        edges.append(edge)
+        wave, waves = forward_stage(flag_of(t), wave, wins, chirp, first, waves)
         wave = hop(wave, t, t + 1)
+    last_wave = waves[GROUP - 1]
     wave, *grads = turn_stage(flag_of(STAGES - 1), wave, wins, chirp, first, dft, amplitudes, pick)
     for t in reversed(range(STAGES - 1)):
         wave = hop(wave, t + 1, t)
         if t == 0:
             grads = code_grads((4 * (works & (stage > 0))).astype(jnp.int32)[None], grads)
-        results = backward_stage(t == 0, flag_of(t), wave, wins, chirp, waves, final_win, edges[t], grads)
+        results = backward_stage(t == 0, flag_of(t), wave, wins, chirp, waves, final_win, last_wave, grads)
         grads = results[-2:]
         wave = results[0]
 

time: 200 us -> 199 us (level)
  Pallas kernels: 28.4 us -> 26.4 us
  waiting for transfers between devices: 111 us -> 109 us
  transfers between devices with their start and end apart: 10 -> 10, of which waited for: 6 -> 6; matrix products, arithmetic and copies ran while one was open for 0% -> 1% of each run, Pallas kernels for 0% -> 0%
where the time goes in v5:
time: 199 us; the launch traced here: 196 us
  waiting for transfers between devices  109 us (55%)
  blocking collectives  45.3 us (23%)
  Pallas kernels  26.4 us (13%)
  starting transfers between devices  10.8 us (5%)
  local copies, waits for them, and re-layouts  3 us (2%)
    ppermute x6, waiting for transfers between devices, hop(): lax.ppermute(value, 'depth', [(device(source, z, 0), device(target, z, 0)...  79.7 us
    all_to_all x2, blocking collectives, exchange(): lax.all_to_all(value, 'depth', 0, 0, axis_index_groups=rings, tiled=True)  45.3 us
    ppermute x1, waiting for transfers between devices, body(): after = lax.ppermute(own, 'stripe', [(i, (i - 1) % 4) for i in ring])  14.4 us
    ppermute x1, waiting for transfers between devices, body(): lax.ppermute(low, 'stripe', [(i, (i + 1) % 4) for i in ring])  9.61 us
    pallas_call x3, Pallas kernels, backward_stage(): pl.pallas_call(lambda *refs: backward_kernel(final, *refs), in_specs=[sme...  9.16 us
    pallas_call x3, Pallas kernels, forward_stage(): pl.pallas_call(lambda *refs: forward_kernel(first, *refs), in_specs=[smem...  7.24 us
    ppermute x2, waiting for transfers between devices, ring_step(): return lax.ppermute(value, 'depth', pairs)  5.32 us
    ppermute x6, starting transfers between devices, hop(): lax.ppermute(value, 'depth', [(device(source, z, 0), device(target, z, 0)...  5.31 us
  transfers between devices with their start and end apart: 10, of which 6 were waited for; matrix products, arithmetic and copies ran while one was open for 1% of the time, Pallas kernels for 0%

profile of v5, /device:TPU:16, one launch (start us, length us, event | category | flops | bytes accessed | tf_op | source)
XLA Modules:
  0.0 195.6 jit_solution(4397046299955980495)
XLA Ops:
  0.0 0.0 copy-start
  0.0 0.0 copy-start.2
  0.0 1.1 copy-done.2
  1.2 0.2 pack.1.own
  1.4 0.5 collective-permute-start
  1.9 0.0 copy-done
  1.9 0.1 constant_dynamic-slice_fusion
  2.0 0.1 copy.19.place
  2.1 14.4 %collective-permute-done.after = s16[3,256,384]{2,1,0:T(8,128)(2,1)S(1)} collective-permute-done((s16[3,256,384]{2,1,0:T(8,128)(2,1)S(1)}, s16[3,256,384]{2,1,0:T(8,128)(2,1)S(1)}, u32[]{:S(2)}, u32[]{:S(2)}) %collective-permute-start) | collective-permute-done | bytes 589856 | tf_op jit(solution)/shard_map/ppermute | solution.py:748
  16.5 2.6 %cut_windows.1 = s16[4,3,256,256]{3,2,1,0:T(8,128)(2,1)S(1)} custom-call(s32[4,2]{1,0:T(4,128)S(1)} %copy.19.place, s16[3,256,384]{2,1,0:T(8,128)(2,1)S(1)} %pack.1.own, s16[3,256,384]{2,1,0:T(8,128)(2,1)S(1)} %collective-permute-done.after), custom_call_target="tpu_custom_call" | custom-call | tf_op jit(solution)/shard_map/cut_windows/pallas_call | solution.py:626
  19.1 0.0 copy-start.4
  19.1 24.9 %all_to_all.10.even = s16[4,3,256,256]{3,2,1,0:T(8,128)(2,1)S(1)} all-to-all(s16[4,3,256,256]{3,2,1,0:T(8,128)(2,1)S(1)} %cut_windows.1), channel_id=1, replica_groups={{0,8,16,24},{4,12,20,28},{32,40,48,56},{36,44,52,60},{64,72,80,88},{68,..., dimensions={0} | all-to-all | bytes 3145728 | tf_op jit(solution)/shard_map/all_to_all | solution.py:726
  44.1 0.0 copy-start.1
  44.1 0.0 copy-start.3
  44.1 1.4 collective-permute-start.1
  45.5 0.0 copy-done.4
  45.5 0.6 dynamic_slice.7.live
  46.8 2.8 %collective-permute-done.1.odd = s16[4,3,256,256]{3,2,1,0:T(8,128)(2,1)} collective-permute-done((s16[4,3,256,256]{3,2,1,0:T(8,128)(2,1)S(1)}, s16[4,3,256,256]{3,2,1,0:T(8,128)(2,1)}, u32[]{:S(2)}, u32[]{:S(2)}) %collective-permute-start.1) | collective-permute-done | bytes 1572896 | tf_op jit(solution)/shard_map/ppermute | solution.py:719
  49.6 3.5 %unpack.1 = (f32[8,2,256,256]{3,2,1,0:T(8,128)}, f32[2,256,256]{2,1,0:T(8,128)S(1)}, f32[2,256,256]{2,1,0:T(8,128)S(1)}) custom-call(s16[4,3,256,256]{3,2,1,0:T(8,128)(2,1)S(1)} %all_to_all.10.even, s16[4,3,256,256]{3,2,1,0:T(8,128)(2,1)} %collective-permute-done.1.odd), custom_call_target="tpu_custom_call" | custom-call | tf_op jit(solution)/shard_map/unpack/pallas_call | solution.py:596
  53.2 0.0 copy-done.1
  53.2 0.0 copy-done.3
  53.2 7.1 %forward_stage.3 = (s16[2,272,256]{2,1,0:T(8,128)(2,1)S(1)}, f32[8,2,256,256]{3,2,1,0:T(8,128)}) custom-call(s32[1]{0:T(128)} %bitcast.2.refs_0_, bf16[2,256,256]{2,1,0:T(8,128)(2,1)S(1)} %copy-done.3, f32[8,2,256,256]{3,2,1,0:T(8,128)} %get-tuple-element.29.refs_2_.wins, bf16[4,256,256]{2,1,0:T(8,128)(2,1)S(1)} %copy-done.1, ...), custom_call_target="tpu_custom_call" | custom-call | tf_op jit(solution)/shard_map/forward_stage/pallas_call | solution.py:453
  60.3 1.3 collective-permute-start.2
  61.6 4.0 %collective-permute-done.2.refs_1_ = s16[2,272,256]{2,1,0:T(8,128)(2,1)S(1)} collective-permute-done((s16[2,272,256]{2,1,0:T(8,128)(2,1)S(1)}, s16[2,272,256]{2,1,0:T(8,128)(2,1)S(1)}, u32[]{:S(2)}, u32[]{:S(2)}) %collective-permute-start.2) | collective-permute-done | bytes 278560 | tf_op jit(solution)/shard_map/ppermute | solution.py:730
  65.7 0.1 forward_stage.4
  65.7 0.7 collective-permute-start.3
  66.4 0.0 collective-permute-done.3.refs_1_
  66.4 0.1 forward_stage.5
  66.5 0.7 collective-permute-start.4
  67.2 0.0 collective-permute-done.4.coded
  67.2 0.1 turn_stage.1
  67.4 0.7 collective-permute-start.5
  68.1 1.1 slice_bitcast_fusion.refs_6_
  69.1 0.0 collective-permute-done.5.refs_1_
  69.1 0.1 backward_stage.3
  69.3 0.7 collective-permute-start.6
  69.9 0.0 collective-permute-done.6.refs_1_
  70.0 0.1 backward_stage.4
  70.1 1.3 collective-permute-start.7
  71.4 0.2 code_grads.1
  71.6 75.6 %collective-permute-done.7.refs_1_ = s16[2,272,256]{2,1,0:T(8,128)(2,1)S(1)} collective-permute-done((s16[2,272,256]{2,1,0:T(8,128)(2,1)S(1)}, s16[2,272,256]{2,1,0:T(8,128)(2,1)S(1)}, u32[]{:S(2)}, u32[]{:S(2)}) %collective-permute-start.7) | collective-permute-done | bytes 278560 | tf_op jit(solution)/shard_map/ppermute | solution.py:730
  147.3 9.0 %backward_stage.5 = (s16[4,2,272,256]{3,2,1,0:T(8,128)(2,1)}, s16[4,2,272,256]{3,2,1,0:T(8,128)(2,1)}) custom-call(s32[1]{0:T(128)} %bitcast.2.refs_0_, s16[2,272,256]{2,1,0:T(8,128)(2,1)S(1)} %collective-permute-done.7.refs_1_, f32[8,2,256,256]{3,2,1,0:T(8,128)} %get-tuple-element.29.refs_2_.wins, ...), custom_call_target="tpu_custom_call", output_to_operand_aliasing={{0}: (7, {}), {1}: (8, {})} | custom-call | tf_op jit(solution)/shard_map/backward_stage/pallas_call | solution.py:490
  156.2 1.4 collective-permute-start.8
  157.6 2.5 %collective-permute-done.8.odd = s16[4,2,272,256]{3,2,1,0:T(8,128)(2,1)S(1)} collective-permute-done((s16[4,2,272,256]{3,2,1,0:T(8,128)(2,1)}, s16[4,2,272,256]{3,2,1,0:T(8,128)(2,1)S(1)}, u32[]{:S(2)}, u32[]{:S(2)}) %collective-permute-start.8) | collective-permute-done | bytes 1114144 | tf_op jit(solution)/shard_map/ppermute | solution.py:719
  160.1 0.1 pick_pile.1
  160.2 20.4 %all_to_all.11.grads = s16[4,2,272,256]{3,2,1,0:T(8,128)(2,1)S(1)} all-to-all(s16[4,2,272,256]{3,2,1,0:T(8,128)(2,1)} %pick_pile.1), channel_id=1, replica_groups={{0,8,16,24},{4,12,20,28},{32,40,48,56},{36,44,52,60},{64,72,80,88},{68,..., dimensions={0} | all-to-all | bytes 2228224 | tf_op jit(solution)/shard_map/all_to_all | solution.py:726
  180.5 2.2 %add_windows.1 = (f32[2,256,384]{2,1,0:T(8,128)S(1)}, s16[2,272,384]{2,1,0:T(8,128)(2,1)S(1)}) custom-call(s32[4,2]{1,0:T(4,128)S(1)} %copy.19.place, s32[1]{0:T(128)} %dynamic_slice.7.live, s16[4,2,272,256]{3,2,1,0:T(8,128)(2,1)S(1)} %all_to_all.11.grads), custom_call_target="tpu_custom_call" | custom-call | tf_op jit(solution)/shard_map/add_windows/pallas_call | solution.py:656
  182.8 2.2 %collective-permute-start.9 = (s16[2,272,384]{2,1,0:T(8,128)(2,1)S(1)}, s16[2,272,384]{2,1,0:T(8,128)(2,1)S(1)}, u32[]{:S(2)}, u32[]{:S(2)}) collective-permute-start(s16[2,272,384]{2,1,0:T(8,128)(2,1)S(1)} %get-tuple-element.52), channel_id=1, source_target_pairs={{0,1},{1,2},{2,3},{3,0},{4,5},{5,6},{6,7},{7,4},{8,9},{9,10},{10,1... | collective-permute-start | bytes 1253384 | tf_op jit(solution)/shard_map/ppermute | solution.py:768
  185.0 9.6 %collective-permute-done.9.low = s16[2,272,384]{2,1,0:T(8,128)(2,1)S(1)} collective-permute-done((s16[2,272,384]{2,1,0:T(8,128)(2,1)S(1)}, s16[2,272,384]{2,1,0:T(8,128)(2,1)S(1)}, u32[]{:S(2)}, u32[]{:S(2)}) %collective-permute-start.9) | collective-permute-done | bytes 417824 | tf_op jit(solution)/shard_map/ppermute | solution.py:768
  194.6 1.0 join.1
Async XLA Ops:
  0.0 1.9 copy-start
  0.0 1.1 copy-start.2
  1.4 15.1 %collective-permute-start = (s16[3,256,384]{2,1,0:T(8,128)(2,1)S(1)}, s16[3,256,384]{2,1,0:T(8,128)(2,1)S(1)}, u32[]{:S(2)}, u32[]{:S(2)}) collective-permute-start(s16[3,256,384]{2,1,0:T(8,128)(2,1)S(1)} %pack.1.own), channel_id=1, source_target_pairs={{0,3},{1,0},{2,1},{3,2},{4,7},{5,4},{6,5},{7,6},{8,11},{9,8},{10,9... | collective-permute-start | bytes 1769480 | tf_op jit(solution)/shard_map/ppermute | solution.py:748
  19.1 26.4 %copy-start.4 = (s32[4]{0:T(128)S(1)}, s32[4]{0:T(128)}, u32[]{:S(2)}) copy-start(s32[4]{0:T(128)} %param.12) | copy-start | bytes 52
  44.1 9.1 %copy-start.1 = (bf16[4,256,256]{2,1,0:T(8,128)(2,1)S(1)}, bf16[4,256,256]{2,1,0:T(8,128)(2,1)}, u32[]{:S(2)}) copy-start(bf16[4,256,256]{2,1,0:T(8,128)(2,1)} %constant.71.clone.refs_3_.chirp) | copy-start | bytes 1572868
  44.1 9.1 %copy-start.3 = (bf16[2,256,256]{2,1,0:T(8,128)(2,1)S(1)}, bf16[2,256,256]{2,1,0:T(8,128)(2,1)}, u32[]{:S(2)}) copy-start(bf16[2,256,256]{2,1,0:T(8,128)(2,1)} %refs_1_.1) | copy-start | bytes 786436
  44.1 5.6 %collective-permute-start.1 = (s16[4,3,256,256]{3,2,1,0:T(8,128)(2,1)S(1)}, s16[4,3,256,256]{3,2,1,0:T(8,128)(2,1)}, u32[]{:S(2)}, u32[]{:S(2)}) collective-permute-start(s16[4,3,256,256]{3,2,1,0:T(8,128)(2,1)S(1)} %all_to_all.10.even), channel_id=1, source_target_pairs={{4,0},{12,8},{20,16},{28,24},{36,32},{44,40},{52,48},{60,56},{68,6... | collective-permute-start | bytes 4718600 | tf_op jit(solution)/shard_map/ppermute | solution.py:719
  60.3 5.3 %collective-permute-start.2 = (s16[2,272,256]{2,1,0:T(8,128)(2,1)S(1)}, s16[2,272,256]{2,1,0:T(8,128)(2,1)S(1)}, u32[]{:S(2)}, u32[]{:S(2)}) collective-permute-start(s16[2,272,256]{2,1,0:T(8,128)(2,1)S(1)} %get-tuple-element.31), channel_id=1, source_target_pairs={{0,32},{8,40},{16,48},{24,56},{1,33},{9,41},{17,49},{25,57},{2,34}... | collective-permute-start | bytes 835592 | tf_op jit(solution)/shard_map/ppermute | solution.py:730
  65.7 0.7 collective-permute-start.3
  66.5 0.7 collective-permute-start.4
  67.4 1.8 collective-permute-start.5
  69.3 0.7 collective-permute-start.6
  70.1 77.2 %collective-permute-start.7 = (s16[2,272,256]{2,1,0:T(8,128)(2,1)S(1)}, s16[2,272,256]{2,1,0:T(8,128)(2,1)S(1)}, u32[]{:S(2)}, u32[]{:S(2)}) collective-permute-start(s16[2,272,256]{2,1,0:T(8,128)(2,1)S(1)} %get-tuple-element.44), channel_id=1, source_target_pairs={{32,0},{40,8},{48,16},{56,24},{33,1},{41,9},{49,17},{57,25},{34,2}... | collective-permute-start | bytes 835592 | tf_op jit(solution)/shard_map/ppermute | solution.py:730
  156.2 3.9 %collective-permute-start.8 = (s16[4,2,272,256]{3,2,1,0:T(8,128)(2,1)}, s16[4,2,272,256]{3,2,1,0:T(8,128)(2,1)S(1)}, u32[]{:S(2)}, u32[]{:S(2)}) collective-permute-start(s16[4,2,272,256]{3,2,1,0:T(8,128)(2,1)} %get-tuple-element.49), channel_id=1, source_target_pairs={{0,4},{8,12},{16,20},{24,28},{32,36},{40,44},{48,52},{56,60},{64,6... | collective-permute-start | bytes 3342344 | tf_op jit(solution)/shard_map/ppermute | solution.py:719
  182.8 11.8 %collective-permute-start.9 = (s16[2,272,384]{2,1,0:T(8,128)(2,1)S(1)}, s16[2,272,384]{2,1,0:T(8,128)(2,1)S(1)}, u32[]{:S(2)}, u32[]{:S(2)}) collective-permute-start(s16[2,272,384]{2,1,0:T(8,128)(2,1)S(1)} %get-tuple-element.52), channel_id=1, source_target_pairs={{0,1},{1,2},{2,3},{3,0},{4,5},{5,6},{6,7},{7,4},{8,9},{9,10},{10,1... | collective-permute-start | bytes 1253384 | tf_op jit(solution)/shard_map/ppermute | solution.py:768

commit v6 on v5

--- a/solution.py
+++ b/solution.py
@@ -574,10 +574,14 @@
     )(own)
 
 
-def unpack_kernel(even, odd, out, first, last, buf, sem):
+def unpack_kernel(even, odd_in, out, first, last, buf, sem, odd, odd_sem):
     copies = []
-    for i in range(GROUP):
+    fetch = Fetch([(odd_in.at[i], odd.at[i]) for i in range(GROUP // 2)], odd_sem)
+    fetch.start()
+    for i in (*range(0, GROUP, 2), *range(1, GROUP, 2)):
         array = (even, odd)[i % 2]
+        if i % 2:
+            fetch.copies[i // 2].wait()
         for start in range(0, WIN, 64):
             part = slice(start, start + 64)
             both = array[i // 2, 0, part, :].astype(jnp.int32) + 2**15
@@ -595,10 +599,15 @@
 def unpack(even, odd):
     return pl.pallas_call(
         unpack_kernel,
-        in_specs=[vmem] * 2,
+        in_specs=[vmem, hbm],
         out_specs=[hbm, vmem, vmem],
         out_shape=[pltpu.HBM((GROUP, 2, WIN, WIN), f32)] + [jax.ShapeDtypeStruct((2, WIN, WIN), f32)] * 2,
-        scratch_shapes=[pltpu.VMEM((GROUP, 2, WIN, WIN), f32), dma((GROUP,))],
+        scratch_shapes=[
+            pltpu.VMEM((GROUP, 2, WIN, WIN), f32),
+            dma((GROUP,)),
+            pltpu.VMEM((GROUP // 2, 3, WIN, WIN), i16),
+            dma((GROUP // 2,)),
+        ],
         compiler_params=params,
         name="unpack",
     )(even, odd)

time: 199 us -> 199 us (level)
  no operation moved by 1% of the time
where the time goes in v6:
time: 199 us; the launch traced here: 196 us
  waiting for transfers between devices  109 us (55%)
  blocking collectives  45.3 us (23%)
  Pallas kernels  26 us (13%)
  starting transfers between devices  11.9 us (6%)
  local copies, waits for them, and re-layouts  3 us (2%)
    ppermute x6, waiting for transfers between devices, hop(): lax.ppermute(value, 'depth', [(device(source, z, 0), device(target, z, 0)...  79.7 us
    all_to_all x2, blocking collectives, exchange(): lax.all_to_all(value, 'depth', 0, 0, axis_index_groups=rings, tiled=True)  45.3 us
    ppermute x1, waiting for transfers between devices, body(): after = lax.ppermute(own, 'stripe', [(i, (i - 1) % 4) for i in ring])  14.4 us
    ppermute x1, waiting for transfers between devices, body(): lax.ppermute(low, 'stripe', [(i, (i + 1) % 4) for i in ring])  9.25 us
    pallas_call x3, Pallas kernels, backward_stage(): pl.pallas_call(lambda *refs: backward_kernel(final, *refs), in_specs=[sme...  9.16 us
    pallas_call x3, Pallas kernels, forward_stage(): pl.pallas_call(lambda *refs: forward_kernel(first, *refs), in_specs=[smem...  7.24 us
    ppermute x2, waiting for transfers between devices, ring_step(): return lax.ppermute(value, 'depth', pairs)  5.32 us
    ppermute x6, starting transfers between devices, hop(): lax.ppermute(value, 'depth', [(device(source, z, 0), device(target, z, 0)...  5.31 us
  transfers between devices with their start and end apart: 10, of which 6 were waited for; matrix products, arithmetic and copies ran while one was open for 1% of the time, Pallas kernels for 0%

profile of v6, /device:TPU:16, one launch (start us, length us, event | category | flops | bytes accessed | tf_op | source)
XLA Modules:
  0.0 195.9 jit_solution(17882007355913580684)
XLA Ops:
  0.0 0.0 copy-start
  0.0 0.0 copy-start.2
  0.0 1.1 copy-done.2
  1.2 0.2 pack.1.own
  1.4 0.5 collective-permute-start
  1.9 0.0 copy-done
  1.9 0.1 constant_dynamic-slice_fusion
  2.0 0.1 copy.19.place
  2.1 14.4 %collective-permute-done.after = s16[3,256,384]{2,1,0:T(8,128)(2,1)S(1)} collective-permute-done((s16[3,256,384]{2,1,0:T(8,128)(2,1)S(1)}, s16[3,256,384]{2,1,0:T(8,128)(2,1)S(1)}, u32[]{:S(2)}, u32[]{:S(2)}) %collective-permute-start) | collective-permute-done | bytes 589856 | tf_op jit(solution)/shard_map/ppermute | solution.py:757
  16.5 2.6 %cut_windows.1 = s16[4,3,256,256]{3,2,1,0:T(8,128)(2,1)S(1)} custom-call(s32[4,2]{1,0:T(4,128)S(1)} %copy.19.place, s16[3,256,384]{2,1,0:T(8,128)(2,1)S(1)} %pack.1.own, s16[3,256,384]{2,1,0:T(8,128)(2,1)S(1)} %collective-permute-done.after), custom_call_target="tpu_custom_call" | custom-call | tf_op jit(solution)/shard_map/cut_windows/pallas_call | solution.py:635
  19.1 0.0 copy-start.4
  19.1 24.9 %all_to_all.10.even = s16[4,3,256,256]{3,2,1,0:T(8,128)(2,1)S(1)} all-to-all(s16[4,3,256,256]{3,2,1,0:T(8,128)(2,1)S(1)} %cut_windows.1), channel_id=1, replica_groups={{0,8,16,24},{4,12,20,28},{32,40,48,56},{36,44,52,60},{64,72,80,88},{68,..., dimensions={0} | all-to-all | bytes 3145728 | tf_op jit(solution)/shard_map/all_to_all | solution.py:735
  44.1 0.0 copy-start.1
  44.1 0.0 copy-start.3
  44.1 1.4 collective-permute-start.1
  45.5 0.0 copy-done.4
  45.5 0.6 dynamic_slice.7.live
  46.8 2.8 %collective-permute-done.1.odd_in = s16[4,3,256,256]{3,2,1,0:T(8,128)(2,1)} collective-permute-done((s16[4,3,256,256]{3,2,1,0:T(8,128)(2,1)S(1)}, s16[4,3,256,256]{3,2,1,0:T(8,128)(2,1)}, u32[]{:S(2)}, u32[]{:S(2)}) %collective-permute-start.1) | collective-permute-done | bytes 1572896 | tf_op jit(solution)/shard_map/ppermute | solution.py:728
  49.6 3.2 %unpack.1 = (f32[8,2,256,256]{3,2,1,0:T(8,128)}, f32[2,256,256]{2,1,0:T(8,128)S(1)}, f32[2,256,256]{2,1,0:T(8,128)S(1)}) custom-call(s16[4,3,256,256]{3,2,1,0:T(8,128)(2,1)S(1)} %all_to_all.10.even, s16[4,3,256,256]{3,2,1,0:T(8,128)(2,1)} %collective-permute-done.1.odd_in), custom_call_target="tpu_custom_call" | custom-call | tf_op jit(solution)/shard_map/unpack/pallas_call | solution.py:600
  52.8 0.0 copy-done.1
  52.8 0.0 copy-done.3
  52.8 7.1 %forward_stage.3 = (s16[2,272,256]{2,1,0:T(8,128)(2,1)S(1)}, f32[8,2,256,256]{3,2,1,0:T(8,128)}) custom-call(s32[1]{0:T(128)} %bitcast.2.refs_0_, bf16[2,256,256]{2,1,0:T(8,128)(2,1)S(1)} %copy-done.3, f32[8,2,256,256]{3,2,1,0:T(8,128)} %get-tuple-element.29.refs_2_.wins, bf16[4,256,256]{2,1,0:T(8,128)(2,1)S(1)} %copy-done.1, ...), custom_call_target="tpu_custom_call" | custom-call | tf_op jit(solution)/shard_map/forward_stage/pallas_call | solution.py:453
  59.9 1.3 collective-permute-start.2
  61.3 4.0 %collective-permute-done.2.refs_1_ = s16[2,272,256]{2,1,0:T(8,128)(2,1)S(1)} collective-permute-done((s16[2,272,256]{2,1,0:T(8,128)(2,1)S(1)}, s16[2,272,256]{2,1,0:T(8,128)(2,1)S(1)}, u32[]{:S(2)}, u32[]{:S(2)}) %collective-permute-start.2) | collective-permute-done | bytes 278560 | tf_op jit(solution)/shard_map/ppermute | solution.py:739
  65.3 0.1 forward_stage.4
  65.4 0.7 collective-permute-start.3
  66.1 0.0 collective-permute-done.3.refs_1_
  66.1 0.1 forward_stage.5
  66.1 0.7 collective-permute-start.4
  66.8 0.0 collective-permute-done.4.coded
  66.9 0.1 turn_stage.1
  67.0 0.7 collective-permute-start.5
  67.7 1.1 slice_bitcast_fusion.refs_6_
  68.8 0.0 collective-permute-done.5.refs_1_
  68.8 0.1 backward_stage.3
  68.9 0.7 collective-permute-start.6
  69.6 0.0 collective-permute-done.6.refs_1_
  69.6 0.1 backward_stage.4
  69.7 1.3 collective-permute-start.7
  71.0 0.2 code_grads.1
  71.2 75.6 %collective-permute-done.7.refs_1_ = s16[2,272,256]{2,1,0:T(8,128)(2,1)S(1)} collective-permute-done((s16[2,272,256]{2,1,0:T(8,128)(2,1)S(1)}, s16[2,272,256]{2,1,0:T(8,128)(2,1)S(1)}, u32[]{:S(2)}, u32[]{:S(2)}) %collective-permute-start.7) | collective-permute-done | bytes 278560 | tf_op jit(solution)/shard_map/ppermute | solution.py:739
  146.9 9.0 %backward_stage.5 = (s16[4,2,272,256]{3,2,1,0:T(8,128)(2,1)}, s16[4,2,272,256]{3,2,1,0:T(8,128)(2,1)}) custom-call(s32[1]{0:T(128)} %bitcast.2.refs_0_, s16[2,272,256]{2,1,0:T(8,128)(2,1)S(1)} %collective-permute-done.7.refs_1_, f32[8,2,256,256]{3,2,1,0:T(8,128)} %get-tuple-element.29.refs_2_.wins, ...), custom_call_target="tpu_custom_call", output_to_operand_aliasing={{0}: (7, {}), {1}: (8, {})} | custom-call | tf_op jit(solution)/shard_map/backward_stage/pallas_call | solution.py:490
  155.8 1.4 collective-permute-start.8
  157.2 2.5 %collective-permute-done.8.odd = s16[4,2,272,256]{3,2,1,0:T(8,128)(2,1)S(1)} collective-permute-done((s16[4,2,272,256]{3,2,1,0:T(8,128)(2,1)}, s16[4,2,272,256]{3,2,1,0:T(8,128)(2,1)S(1)}, u32[]{:S(2)}, u32[]{:S(2)}) %collective-permute-start.8) | collective-permute-done | bytes 1114144 | tf_op jit(solution)/shard_map/ppermute | solution.py:728
  159.7 0.1 pick_pile.1
  159.8 20.4 %all_to_all.11.grads = s16[4,2,272,256]{3,2,1,0:T(8,128)(2,1)S(1)} all-to-all(s16[4,2,272,256]{3,2,1,0:T(8,128)(2,1)} %pick_pile.1), channel_id=1, replica_groups={{0,8,16,24},{4,12,20,28},{32,40,48,56},{36,44,52,60},{64,72,80,88},{68,..., dimensions={0} | all-to-all | bytes 2228224 | tf_op jit(solution)/shard_map/all_to_all | solution.py:735
  180.2 2.2 %add_windows.1 = (f32[2,256,384]{2,1,0:T(8,128)S(1)}, s16[2,272,384]{2,1,0:T(8,128)(2,1)S(1)}) custom-call(s32[4,2]{1,0:T(4,128)S(1)} %copy.19.place, s32[1]{0:T(128)} %dynamic_slice.7.live, s16[4,2,272,256]{3,2,1,0:T(8,128)(2,1)S(1)} %all_to_all.11.grads), custom_call_target="tpu_custom_call" | custom-call | tf_op jit(solution)/shard_map/add_windows/pallas_call | solution.py:665
  182.4 3.3 %collective-permute-start.9 = (s16[2,272,384]{2,1,0:T(8,128)(2,1)S(1)}, s16[2,272,384]{2,1,0:T(8,128)(2,1)S(1)}, u32[]{:S(2)}, u32[]{:S(2)}) collective-permute-start(s16[2,272,384]{2,1,0:T(8,128)(2,1)S(1)} %get-tuple-element.52), channel_id=1, source_target_pairs={{0,1},{1,2},{2,3},{3,0},{4,5},{5,6},{6,7},{7,4},{8,9},{9,10},{10,1... | collective-permute-start | bytes 1253384 | tf_op jit(solution)/shard_map/ppermute | solution.py:777
  185.7 9.2 %collective-permute-done.9.low = s16[2,272,384]{2,1,0:T(8,128)(2,1)S(1)} collective-permute-done((s16[2,272,384]{2,1,0:T(8,128)(2,1)S(1)}, s16[2,272,384]{2,1,0:T(8,128)(2,1)S(1)}, u32[]{:S(2)}, u32[]{:S(2)}) %collective-permute-start.9) | collective-permute-done | bytes 417824 | tf_op jit(solution)/shard_map/ppermute | solution.py:777
  194.9 1.0 join.1
Async XLA Ops:
  0.0 1.9 copy-start
  0.0 1.1 copy-start.2
  1.4 15.1 %collective-permute-start = (s16[3,256,384]{2,1,0:T(8,128)(2,1)S(1)}, s16[3,256,384]{2,1,0:T(8,128)(2,1)S(1)}, u32[]{:S(2)}, u32[]{:S(2)}) collective-permute-start(s16[3,256,384]{2,1,0:T(8,128)(2,1)S(1)} %pack.1.own), channel_id=1, source_target_pairs={{0,3},{1,0},{2,1},{3,2},{4,7},{5,4},{6,5},{7,6},{8,11},{9,8},{10,9... | collective-permute-start | bytes 1769480 | tf_op jit(solution)/shard_map/ppermute | solution.py:757
  19.1 26.4 %copy-start.4 = (s32[4]{0:T(128)S(1)}, s32[4]{0:T(128)}, u32[]{:S(2)}) copy-start(s32[4]{0:T(128)} %param.12) | copy-start | bytes 52
  44.1 8.7 %copy-start.1 = (bf16[4,256,256]{2,1,0:T(8,128)(2,1)S(1)}, bf16[4,256,256]{2,1,0:T(8,128)(2,1)}, u32[]{:S(2)}) copy-start(bf16[4,256,256]{2,1,0:T(8,128)(2,1)} %constant.71.clone.refs_3_.chirp) | copy-start | bytes 1572868
  44.1 8.8 %copy-start.3 = (bf16[2,256,256]{2,1,0:T(8,128)(2,1)S(1)}, bf16[2,256,256]{2,1,0:T(8,128)(2,1)}, u32[]{:S(2)}) copy-start(bf16[2,256,256]{2,1,0:T(8,128)(2,1)} %refs_1_.1) | copy-start | bytes 786436
  44.1 5.6 %collective-permute-start.1 = (s16[4,3,256,256]{3,2,1,0:T(8,128)(2,1)S(1)}, s16[4,3,256,256]{3,2,1,0:T(8,128)(2,1)}, u32[]{:S(2)}, u32[]{:S(2)}) collective-permute-start(s16[4,3,256,256]{3,2,1,0:T(8,128)(2,1)S(1)} %all_to_all.10.even), channel_id=1, source_target_pairs={{4,0},{12,8},{20,16},{28,24},{36,32},{44,40},{52,48},{60,56},{68,6... | collective-permute-start | bytes 4718600 | tf_op jit(solution)/shard_map/ppermute | solution.py:728
  59.9 5.3 %collective-permute-start.2 = (s16[2,272,256]{2,1,0:T(8,128)(2,1)S(1)}, s16[2,272,256]{2,1,0:T(8,128)(2,1)S(1)}, u32[]{:S(2)}, u32[]{:S(2)}) collective-permute-start(s16[2,272,256]{2,1,0:T(8,128)(2,1)S(1)} %get-tuple-element.31), channel_id=1, source_target_pairs={{0,32},{8,40},{16,48},{24,56},{1,33},{9,41},{17,49},{25,57},{2,34}... | collective-permute-start | bytes 835592 | tf_op jit(solution)/shard_map/ppermute | solution.py:739
  65.4 0.7 collective-permute-start.3
  66.1 0.7 collective-permute-start.4
  67.0 1.8 collective-permute-start.5
  68.9 0.7 collective-permute-start.6
  69.7 77.2 %collective-permute-start.7 = (s16[2,272,256]{2,1,0:T(8,128)(2,1)S(1)}, s16[2,272,256]{2,1,0:T(8,128)(2,1)S(1)}, u32[]{:S(2)}, u32[]{:S(2)}) collective-permute-start(s16[2,272,256]{2,1,0:T(8,128)(2,1)S(1)} %get-tuple-element.44), channel_id=1, source_target_pairs={{32,0},{40,8},{48,16},{56,24},{33,1},{41,9},{49,17},{57,25},{34,2}... | collective-permute-start | bytes 835592 | tf_op jit(solution)/shard_map/ppermute | solution.py:739
  155.8 3.9 %collective-permute-start.8 = (s16[4,2,272,256]{3,2,1,0:T(8,128)(2,1)}, s16[4,2,272,256]{3,2,1,0:T(8,128)(2,1)S(1)}, u32[]{:S(2)}, u32[]{:S(2)}) collective-permute-start(s16[4,2,272,256]{3,2,1,0:T(8,128)(2,1)} %get-tuple-element.49), channel_id=1, source_target_pairs={{0,4},{8,12},{16,20},{24,28},{32,36},{40,44},{48,52},{56,60},{64,6... | collective-permute-start | bytes 3342344 | tf_op jit(solution)/shard_map/ppermute | solution.py:728
  182.4 12.5 %collective-permute-start.9 = (s16[2,272,384]{2,1,0:T(8,128)(2,1)S(1)}, s16[2,272,384]{2,1,0:T(8,128)(2,1)S(1)}, u32[]{:S(2)}, u32[]{:S(2)}) collective-permute-start(s16[2,272,384]{2,1,0:T(8,128)(2,1)S(1)} %get-tuple-element.52), channel_id=1, source_target_pairs={{0,1},{1,2},{2,3},{3,0},{4,5},{5,6},{6,7},{7,4},{8,9},{9,10},{10,1... | collective-permute-start | bytes 1253384 | tf_op jit(solution)/shard_map/ppermute | solution.py:777
